TPU v7x, 32 devices: a whole 2x2x4 slice. The times are simulated.
32 devices in a mesh: fsdp: 2 (over y), ctx: 16 (over z, x, core).
Axes of the slice: x: 2, y: 2, z: 4, core: 2. Of those that a mesh axis runs over, the one named last changes fastest.
Arguments:
- tokens: bfloat16 [4, 1024, 2048], P('fsdp', 'ctx'), may hold values from -6 to 6
- out_grad: bfloat16 [4, 1024, 2048], P('fsdp', 'ctx'), may hold values from -6 to 6
- segments: int32 [4, 1024], P('fsdp'), may hold values from 0 to 12, as said below
- path_mask: int32 [4, 13, 13], P('fsdp'), may hold values from 0 to 1, as said below
- expert_ids: int32 [4, 1024, 6], P('fsdp', 'ctx'), may hold values from 0 to 15, all different within a row; in each aligned block of 64 rows (0 to 63, 64 to 127, ..., all dimensions but the last counted through in order) at most 32 rows name the same one
- norm_attn: bfloat16 [2048], P(('fsdp', 'ctx')), may hold values from 0.5 to 1.5
- attn_q: bfloat16 [2048, 3072], P(('fsdp', 'ctx')), may hold values from -0.25 to 0.25
- attn_kva: bfloat16 [2048, 576], P(('fsdp', 'ctx')), may hold values from -0.125 to 0.125
- norm_latent: bfloat16 [512], P(('fsdp', 'ctx')), may hold values from 0.5 to 1.5
- attn_kvb: bfloat16 [512, 4096], P(('fsdp', 'ctx')), may hold values from -0.25 to 0.25
- attn_out: bfloat16 [2048, 2048], P(('fsdp', 'ctx')), may hold values from -1 to 1
- norm_ffn: bfloat16 [2048], P(('fsdp', 'ctx')), may hold values from 0.5 to 1.5
- router: bfloat16 [2048, 16], P(('fsdp', 'ctx')), may hold values from -0.0625 to 0.0625
- expert_gate: bfloat16 [2048, 22528], P('fsdp', 'ctx'), may hold values from -0.125 to 0.125
- expert_up: bfloat16 [2048, 22528], P('fsdp', 'ctx'), may hold values from -0.125 to 0.125
- expert_down: bfloat16 [2048, 22528], P('fsdp', 'ctx'), may hold values from -1.75 to 1.75
- shared_gate: bfloat16 [2048, 2816], P('fsdp', 'ctx'), may hold values from -0.125 to 0.125
- shared_up: bfloat16 [2048, 2816], P('fsdp', 'ctx'), may hold values from -0.125 to 0.125
- shared_down: bfloat16 [2048, 2816], P('fsdp', 'ctx'), may hold values from -0.1875 to 0.1875
Outputs:
- output: bfloat16 [4, 1024, 2048], P('fsdp', 'ctx')
- input_grad: float32 [4, 1024, 2048], P('fsdp', 'ctx')
- norm_attn_grad: float32 [2048], P(('fsdp', 'ctx'))
- attn_q_grad: float32 [2048, 3072], P(('fsdp', 'ctx'))
- attn_kva_grad: float32 [2048, 576], P(('fsdp', 'ctx'))
- norm_latent_grad: float32 [512], P(('fsdp', 'ctx'))
- attn_kvb_grad: float32 [512, 4096], P(('fsdp', 'ctx'))
- attn_out_grad: float32 [2048, 2048], P(('fsdp', 'ctx'))
- norm_ffn_grad: float32 [2048], P(('fsdp', 'ctx'))
- router_grad: float32 [2048, 16], P(('fsdp', 'ctx'))
- expert_gate_grad: float32 [2048, 22528], P('fsdp', 'ctx')
- expert_up_grad: float32 [2048, 22528], P('fsdp', 'ctx')
- expert_down_grad: float32 [2048, 22528], P('fsdp', 'ctx')
- shared_gate_grad: float32 [2048, 2816], P('fsdp', 'ctx')
- shared_up_grad: float32 [2048, 2816], P('fsdp', 'ctx')
- shared_down_grad: float32 [2048, 2816], P('fsdp', 'ctx')
Inputs may be any that keep to these rules, and one draw needn't show every extreme that they name: `segments`: within each tree the ids never fall; id 0 is the trunk and holds the first 409 tokens, ids 1 to 4 are branches and 5 to 12 leaves, each holding one token or more. path_mask[s, u] is 1 exactly when segment u is s or an ancestor of s; the trunk is an ancestor of every segment and each branch is the parent of two leaves. `expert_ids`: A token names 6 different experts. Of the 64 tokens of one tree that one device holds, no expert is named by more than 32, a bound that some block reaches.
All inputs are finite; a program needn't handle non-finite values.
Results may differ from a plain program's by a relative error of at most 0.023.
Values may be sent and summed in bfloat16 or wider, within the bound.
A program may use at most 384 MiB of HBM per device.

v0:
```python
import math

import jax
import jax.numpy as jnp
from jax import lax
from jax.sharding import PartitionSpec as P

D = 2048
H = 16
DN = 128
DR = 64
DV = 128
LAT = 512
TOP = 6
SEGS = 13


epsilon = 1e-06
rope_base = 10000.0


def for_sending(value):
    return jax.tree.map(lambda a: a.astype(jnp.bfloat16) if a.dtype == jnp.float32 else a, value)


def multiply(left, right):
    return jnp.dot(left, right, preferred_element_type=jnp.float32)


def multiply_transposed(left, right):
    return lax.dot_general(
        left, right, (((1,), (1,)), ((), ())), preferred_element_type=jnp.float32
    )


def transposed_multiply(left, right):
    return lax.dot_general(
        left, right, (((0,), (0,)), ((), ())), preferred_element_type=jnp.float32
    )


def normalize(tensor_in, gain_vec):
    inverse = lax.rsqrt(jnp.mean(tensor_in * tensor_in, axis=-1, keepdims=True) + epsilon)
    normed = tensor_in * inverse
    return (normed, inverse, normed * gain_vec)


def normalize_back(grad_out, normed, inverse, gain_vec):
    weighted = grad_out * gain_vec
    centre = jnp.mean(weighted * normed, axis=-1, keepdims=True)
    return (inverse * (weighted - normed * centre), jnp.sum(grad_out * normed, axis=0))


def rotate(tensor_in, rotation, direction):
    half_width = tensor_in.shape[-1] // 2
    former = tensor_in[..., :half_width]
    latter = tensor_in[..., half_width:]
    cosine = jnp.cos(rotation)
    sine = direction * jnp.sin(rotation)
    return jnp.concatenate(
        [former * cosine - latter * sine, latter * cosine + former * sine], axis=-1
    )


def tree_mask(segment_ids, path_table, first_row, row_count):
    labels = jnp.arange(SEGS, dtype=jnp.int32)
    own_ids = lax.dynamic_slice_in_dim(segment_ids, first_row, row_count)
    ancestry = jnp.sum(
        jnp.where(own_ids[:, None, None] == labels[None, :, None], path_table[None, :, :], 0),
        axis=1,
    )
    related = jnp.sum(
        jnp.where(segment_ids[None, None, :] == labels[None, :, None], ancestry[:, :, None], 0),
        axis=1,
    )
    places = jnp.arange(segment_ids.shape[0], dtype=jnp.int32)
    queries = first_row + jnp.arange(row_count, dtype=jnp.int32)
    allowed = (related > 0) & (places[None, :] <= queries[:, None])
    positions = jnp.sum(allowed.astype(jnp.int32), axis=1) - 1
    return (allowed, positions)


def swiglu_pair(row_inputs, row_grads, w_gate, w_up, w_down):
    gate_pre = multiply(row_inputs, w_gate)
    up_pre = multiply(row_inputs, w_up)
    sigmoid_gate = jax.nn.sigmoid(gate_pre)
    activated = gate_pre * sigmoid_gate
    hidden_act = (activated * up_pre).astype(jnp.bfloat16)
    result = multiply_transposed(hidden_act, w_down)
    inner_grad = multiply(row_grads, w_down)
    gate_grad = (
        inner_grad * up_pre * sigmoid_gate * (1.0 + gate_pre * (1.0 - sigmoid_gate))
    ).astype(jnp.bfloat16)
    up_grad = (inner_grad * activated).astype(jnp.bfloat16)
    back_rows = multiply_transposed(gate_grad, w_gate) + multiply_transposed(up_grad, w_up)
    weight_grads = (
        transposed_multiply(row_inputs, gate_grad),
        transposed_multiply(row_inputs, up_grad),
        transposed_multiply(row_grads, hidden_act),
    )
    return (result, back_rows, weight_grads)


def attention_scores(query_latent, query_rope, keys_latent, keys_rope, allowed, score_scale):
    raw_scores = jnp.einsum(
        "bthc,bjc->bthj", query_latent, keys_latent, preferred_element_type=jnp.float32
    )
    raw_scores = raw_scores + jnp.einsum(
        "bthr,bjr->bthj", query_rope, keys_rope, preferred_element_type=jnp.float32
    )
    return jnp.where(allowed[:, :, None, :], raw_scores * score_scale, -1e30)


def body(
    tokens,
    out_grad,
    segments,
    path_mask,
    expert_ids,
    norm_attn,
    attn_q,
    attn_kva,
    norm_latent,
    attn_kvb,
    attn_out,
    norm_ffn,
    router,
    expert_gate,
    expert_up,
    expert_down,
    shared_gate,
    shared_up,
    shared_down,
):
    trees = tokens.shape[0]
    tok_loc = tokens.shape[1]
    row_total = trees * tok_loc
    experts = lax.axis_size("ctx")
    first_row = lax.axis_index("ctx") * tok_loc
    capacity = min(tok_loc, tok_loc * TOP * 4 // (3 * experts))
    score_scale = 1.0 / math.sqrt(DN + DR)
    frequency = rope_base ** (-(jnp.arange(DR // 2, dtype=jnp.float32) * 2.0 / DR))
    labels = jnp.arange(experts, dtype=jnp.int32)
    (
        gain_attn_low,
        w_query,
        w_latent,
        gain_latent_low,
        w_expand,
        w_output,
        gain_ffn_low,
        w_router,
    ) = (
        lax.all_gather(norm_attn, ("fsdp", "ctx"), axis=0, tiled=True),
        lax.all_gather(attn_q, ("fsdp", "ctx"), axis=0, tiled=True),
        lax.all_gather(attn_kva, ("fsdp", "ctx"), axis=0, tiled=True),
        lax.all_gather(norm_latent, ("fsdp", "ctx"), axis=0, tiled=True),
        lax.all_gather(attn_kvb, ("fsdp", "ctx"), axis=0, tiled=True),
        lax.all_gather(attn_out, ("fsdp", "ctx"), axis=0, tiled=True),
        lax.all_gather(norm_ffn, ("fsdp", "ctx"), axis=0, tiled=True),
        lax.all_gather(router, ("fsdp", "ctx"), axis=0, tiled=True),
    )
    e_gate, e_up, e_down, s_gate, s_up, s_down = (
        lax.all_gather(expert_gate, "fsdp", axis=0, tiled=True),
        lax.all_gather(expert_up, "fsdp", axis=0, tiled=True),
        lax.all_gather(expert_down, "fsdp", axis=0, tiled=True),
        lax.all_gather(shared_gate, "fsdp", axis=0, tiled=True),
        lax.all_gather(shared_up, "fsdp", axis=0, tiled=True),
        lax.all_gather(shared_down, "fsdp", axis=0, tiled=True),
    )
    gain_attn = gain_attn_low.astype(jnp.float32)
    gain_latent = gain_latent_low.astype(jnp.float32)
    gain_ffn = gain_ffn_low.astype(jnp.float32)

    def one_mask(segment_ids, path_table):
        return tree_mask(segment_ids, path_table, first_row, tok_loc)

    allowed, positions = jax.vmap(one_mask)(segments, path_mask)
    rotation = positions.astype(jnp.float32)[:, :, None] * frequency[None, None, :]
    inputs = tokens.astype(jnp.float32).reshape(row_total, D)
    normed_in, inverse_in, gained_in = normalize(inputs, gain_attn)
    hidden_in = gained_in.astype(jnp.bfloat16)
    query_all = multiply(hidden_in, w_query).reshape(trees, tok_loc, H, DN + DR)
    query_nope = query_all[..., :DN].astype(jnp.bfloat16)
    query_rope = rotate(query_all[..., DN:], rotation[:, :, None, :], 1.0).astype(jnp.bfloat16)
    latent_all = multiply(hidden_in, w_latent)
    latent_normed, latent_inverse, latent_gained = normalize(latent_all[:, :LAT], gain_latent)
    key_latent = latent_gained.astype(jnp.bfloat16).reshape(trees, tok_loc, LAT)
    key_rope = rotate(latent_all[:, LAT:].reshape(trees, tok_loc, DR), rotation, 1.0).astype(
        jnp.bfloat16
    )
    keys_latent, keys_rope = (
        lax.all_gather(key_latent, "ctx", axis=1, tiled=True),
        lax.all_gather(key_rope, "ctx", axis=1, tiled=True),
    )
    expand = w_expand.reshape(LAT, H, DN + DV)
    expand_key = expand[..., :DN]
    expand_value = expand[..., DN:]
    query_latent = jnp.einsum(
        "bthn,chn->bthc", query_nope, expand_key, preferred_element_type=jnp.float32
    ).astype(jnp.bfloat16)
    scores = attention_scores(
        query_latent, query_rope, keys_latent, keys_rope, allowed, score_scale
    )
    highest = jnp.max(scores, axis=-1, keepdims=True)
    exp_total = jnp.sum(jnp.exp(scores - highest), axis=-1, keepdims=True)
    log_total = highest + jnp.log(exp_total)
    weights_low = jnp.exp(scores - log_total).astype(jnp.bfloat16)
    mixed = jnp.einsum(
        "bthj,bjc->bthc", weights_low, keys_latent, preferred_element_type=jnp.float32
    ).astype(jnp.bfloat16)
    heads = (
        jnp.einsum("bthc,chv->bthv", mixed, expand_value, preferred_element_type=jnp.float32)
        .astype(jnp.bfloat16)
        .reshape(row_total, H * DV)
    )
    residual = inputs + multiply(heads, w_output)
    normed_mid, inverse_mid, gained_mid = normalize(residual, gain_ffn)
    hidden_mid = gained_mid.astype(jnp.bfloat16)
    expert_probs = jax.nn.softmax(multiply(hidden_mid, w_router), axis=-1)
    chosen = expert_ids.reshape(row_total, TOP)
    selected = chosen[:, :, None] == labels[None, None, :]
    gate_weights = jnp.sum(jnp.where(selected, expert_probs[:, None, :], 0.0), axis=-1)
    upstream = out_grad.astype(jnp.float32).reshape(row_total, D)
    flat_ids = expert_ids.reshape(trees, tok_loc * TOP)
    member = (flat_ids[:, :, None] == labels[None, None, :]).astype(jnp.int32)
    earlier = jnp.cumsum(member, axis=1) - member
    slot_index = jnp.sum(earlier * member, axis=2)
    tree_of = jnp.arange(trees, dtype=jnp.int32)[:, None]
    target = (flat_ids * (trees * capacity) + tree_of * capacity + slot_index).reshape(-1)
    route_owner = jnp.arange(row_total * TOP, dtype=jnp.int32) // TOP
    slot_total = experts * trees * capacity
    send_rows = jnp.zeros((slot_total, D), jnp.bfloat16).at[target].set(hidden_mid[route_owner])
    route_grad = (gate_weights.reshape(-1)[:, None] * upstream[route_owner]).astype(jnp.bfloat16)
    send_grads = jnp.zeros((slot_total, D), jnp.bfloat16).at[target].set(route_grad)
    recv_rows, recv_grads = (
        lax.all_to_all(
            send_rows.reshape(experts, trees * capacity, D),
            "ctx",
            split_axis=0,
            concat_axis=0,
            tiled=True,
        ),
        lax.all_to_all(
            send_grads.reshape(experts, trees * capacity, D),
            "ctx",
            split_axis=0,
            concat_axis=0,
            tiled=True,
        ),
    )
    expert_result, expert_back, expert_grads = swiglu_pair(
        recv_rows.reshape(-1, D), recv_grads.reshape(-1, D), e_gate, e_up, e_down
    )
    back_out, back_rows = (
        lax.all_to_all(
            expert_result.astype(jnp.bfloat16).reshape(experts, trees * capacity, D),
            "ctx",
            split_axis=0,
            concat_axis=0,
            tiled=True,
        ),
        lax.all_to_all(
            expert_back.astype(jnp.bfloat16).reshape(experts, trees * capacity, D),
            "ctx",
            split_axis=0,
            concat_axis=0,
            tiled=True,
        ),
    )
    route_out = back_out.reshape(-1, D)[target].astype(jnp.float32).reshape(row_total, TOP, D)
    route_back = back_rows.reshape(-1, D)[target].astype(jnp.float32).reshape(row_total, TOP, D)
    routed = jnp.sum(gate_weights[:, :, None] * route_out, axis=1)
    gate_delta = jnp.sum(upstream[:, None, :] * route_out, axis=-1)
    prob_delta = jnp.sum(jnp.where(selected, gate_delta[:, :, None], 0.0), axis=1)
    logit_grad = (
        expert_probs * (prob_delta - jnp.sum(expert_probs * prob_delta, axis=-1, keepdims=True))
    ).astype(jnp.bfloat16)
    grad_router = transposed_multiply(hidden_mid, logit_grad)
    mid_grad = jnp.sum(route_back, axis=1) + multiply_transposed(logit_grad, w_router)
    shared_low = upstream.astype(jnp.bfloat16)
    tree_rows, tree_grads = (
        lax.all_gather(hidden_mid.reshape(trees, tok_loc, D), "ctx", axis=1, tiled=True),
        lax.all_gather(shared_low.reshape(trees, tok_loc, D), "ctx", axis=1, tiled=True),
    )
    part_out, part_back, shared_grads = swiglu_pair(
        tree_rows.reshape(-1, D), tree_grads.reshape(-1, D), s_gate, s_up, s_down
    )
    shared_out, shared_back = (
        lax.psum_scatter(part_out.reshape(trees, -1, D), "ctx", scatter_dimension=1, tiled=True),
        lax.psum_scatter(part_back.reshape(trees, -1, D), "ctx", scatter_dimension=1, tiled=True),
    )
    shared_out = shared_out.reshape(row_total, D)
    shared_back = shared_back.reshape(row_total, D)
    mid_grad = mid_grad + shared_back
    output = (residual + routed + shared_out).astype(jnp.bfloat16).reshape(trees, tok_loc, D)
    mid_input, grad_gain_ffn = normalize_back(mid_grad, normed_mid, inverse_mid, gain_ffn)
    residual_grad = upstream + mid_input
    residual_low = residual_grad.astype(jnp.bfloat16)
    grad_output = transposed_multiply(heads, residual_low)
    heads_grad = (
        multiply_transposed(residual_low, w_output)
        .astype(jnp.bfloat16)
        .reshape(trees, tok_loc, H, DV)
    )
    mixed_grad = jnp.einsum(
        "bthv,chv->bthc", heads_grad, expand_value, preferred_element_type=jnp.float32
    ).astype(jnp.bfloat16)
    grad_value = jnp.einsum("bthc,bthv->chv", mixed, heads_grad, preferred_element_type=jnp.float32)
    scores = attention_scores(
        query_latent, query_rope, keys_latent, keys_rope, allowed, score_scale
    )
    weights_full = jnp.exp(scores - log_total)
    prob_grad = jnp.einsum(
        "bthc,bjc->bthj", mixed_grad, keys_latent, preferred_element_type=jnp.float32
    )
    keys_latent_grad = jnp.einsum(
        "bthj,bthc->bjc",
        weights_full.astype(jnp.bfloat16),
        mixed_grad,
        preferred_element_type=jnp.float32,
    )
    score_grad = (
        weights_full * (prob_grad - jnp.sum(weights_full * prob_grad, axis=-1, keepdims=True))
    ).astype(jnp.bfloat16)
    qlat_grad = (
        jnp.einsum("bthj,bjc->bthc", score_grad, keys_latent, preferred_element_type=jnp.float32)
        * score_scale
    ).astype(jnp.bfloat16)
    keys_latent_grad = (
        keys_latent_grad
        + jnp.einsum("bthj,bthc->bjc", score_grad, query_latent, preferred_element_type=jnp.float32)
        * score_scale
    )
    qrope_grad = (
        jnp.einsum("bthj,bjr->bthr", score_grad, keys_rope, preferred_element_type=jnp.float32)
        * score_scale
    )
    keys_rope_grad = (
        jnp.einsum("bthj,bthr->bjr", score_grad, query_rope, preferred_element_type=jnp.float32)
        * score_scale
    )
    qnope_grad = jnp.einsum(
        "bthc,chn->bthn", qlat_grad, expand_key, preferred_element_type=jnp.float32
    )
    grad_key = jnp.einsum(
        "bthc,bthn->chn", qlat_grad, query_nope, preferred_element_type=jnp.float32
    )
    grad_expand = jnp.concatenate([grad_key, grad_value], axis=-1).reshape(LAT, H * (DN + DV))
    query_grad = jnp.concatenate(
        [qnope_grad, rotate(qrope_grad, rotation[:, :, None, :], -1.0)], axis=-1
    )
    query_grad = query_grad.astype(jnp.bfloat16).reshape(row_total, H * (DN + DR))
    grad_query = transposed_multiply(hidden_in, query_grad)
    hidden_grad = multiply_transposed(query_grad, w_query)
    own_latent_grad, own_rope_grad = (
        lax.psum_scatter(
            keys_latent_grad.astype(jnp.bfloat16), "ctx", scatter_dimension=1, tiled=True
        ).astype(jnp.float32),
        lax.psum_scatter(
            keys_rope_grad.astype(jnp.bfloat16), "ctx", scatter_dimension=1, tiled=True
        ).astype(jnp.float32),
    )
    latent_in_grad, grad_gain_latent = normalize_back(
        own_latent_grad.reshape(row_total, LAT), latent_normed, latent_inverse, gain_latent
    )
    rope_back = rotate(own_rope_grad, rotation, -1.0).reshape(row_total, DR)
    latent_grad = jnp.concatenate([latent_in_grad, rope_back], axis=-1).astype(jnp.bfloat16)
    grad_latent = transposed_multiply(hidden_in, latent_grad)
    hidden_grad = hidden_grad + multiply_transposed(latent_grad, w_latent)
    input_part, grad_gain_attn = normalize_back(hidden_grad, normed_in, inverse_in, gain_attn)
    input_grad = (input_part + residual_grad).reshape(trees, tok_loc, D)
    attn_total = (
        grad_gain_attn,
        grad_query,
        grad_latent,
        grad_gain_latent,
        grad_expand,
        grad_output,
        grad_gain_ffn,
        grad_router,
    )
    ffn_total = expert_grads + shared_grads
    attn_sums = (
        lax.psum_scatter(attn_total[0], ("fsdp", "ctx"), scatter_dimension=0, tiled=True),
        lax.psum_scatter(attn_total[1], ("fsdp", "ctx"), scatter_dimension=0, tiled=True),
        lax.psum_scatter(attn_total[2], ("fsdp", "ctx"), scatter_dimension=0, tiled=True),
        lax.psum_scatter(attn_total[3], ("fsdp", "ctx"), scatter_dimension=0, tiled=True),
        lax.psum_scatter(attn_total[4], ("fsdp", "ctx"), scatter_dimension=0, tiled=True),
        lax.psum_scatter(attn_total[5], ("fsdp", "ctx"), scatter_dimension=0, tiled=True),
        lax.psum_scatter(attn_total[6], ("fsdp", "ctx"), scatter_dimension=0, tiled=True),
        lax.psum_scatter(attn_total[7], ("fsdp", "ctx"), scatter_dimension=0, tiled=True),
    )
    ffn_sums = jax.tree.map(
        lambda part: part.astype(jnp.float32),
        lax.psum_scatter(for_sending(ffn_total), "fsdp", scatter_dimension=0, tiled=True),
    )
    return (
        output,
        input_grad,
        attn_sums[0],
        attn_sums[1],
        attn_sums[2],
        attn_sums[3],
        attn_sums[4],
        attn_sums[5],
        attn_sums[6],
        attn_sums[7],
        ffn_sums[0],
        ffn_sums[1],
        ffn_sums[2],
        ffn_sums[3],
        ffn_sums[4],
        ffn_sums[5],
    )


def solution(mesh):
    placed = (
        P("fsdp", "ctx", None),
        P("fsdp", "ctx", None),
        P("fsdp", None),
        P("fsdp", None, None),
        P("fsdp", "ctx", None),
        P(("fsdp", "ctx")),
        P(("fsdp", "ctx"), None),
        P(("fsdp", "ctx"), None),
        P(("fsdp", "ctx")),
        P(("fsdp", "ctx"), None),
        P(("fsdp", "ctx"), None),
        P(("fsdp", "ctx")),
        P(("fsdp", "ctx"), None),
        P("fsdp", "ctx"),
        P("fsdp", "ctx"),
        P("fsdp", "ctx"),
        P("fsdp", "ctx"),
        P("fsdp", "ctx"),
        P("fsdp", "ctx"),
    )
    return jax.shard_map(
        body,
        mesh=mesh,
        in_specs=placed,
        out_specs=(
            P("fsdp", "ctx", None),
            P("fsdp", "ctx", None),
            P(("fsdp", "ctx")),
            P(("fsdp", "ctx"), None),
            P(("fsdp", "ctx"), None),
            P(("fsdp", "ctx")),
            P(("fsdp", "ctx"), None),
            P(("fsdp", "ctx"), None),
            P(("fsdp", "ctx")),
            P(("fsdp", "ctx"), None),
            P("fsdp", "ctx"),
            P("fsdp", "ctx"),
            P("fsdp", "ctx"),
            P("fsdp", "ctx"),
            P("fsdp", "ctx"),
            P("fsdp", "ctx"),
        ),
        check_vma=False,
    )
```

profile of v0, /device:TPU:0, one launch (start us, length us, event | category | flops | bytes accessed | tf_op | source)
XLA Modules:
  0.0 2530.7 jit_solution(5762273835727014289)
XLA Ops:
  13.4 42.3 %all-reduce.7 = (bf16[2048]{0:T(1024)(128)(2,1)S(1)}, bf16[512]{0:T(512)(128)(2,1)S(1)}, bf16[2048]{0:T(1024)(128)(2,1)S(1)}) all-reduce(bf16[2048]{0:T(1024)(128)(2,1)S(1)} %dynamic-update-slice.1, bf16[512]{0:T(512)(128)(2,1)S(1)} %dynamic-update-slice.2, ...), channel_id=1, replica_groups=mesh['fsdp'=2,'ctx'=16] {'fsdp','ctx'}, use_global_device_ids=true, to_apply=%add | all-reduce | flops 4608 | bytes 18432
  56.9 14.8 all-gather.16.cloned.1.call-done
  79.4 22.1 all_gather.60
  101.6 34.5 %all-gather.14.cloned.1.call-done = bf16[512,4096]{1,0:T(8,128)(2,1)} async-done(((bf16[16,4096]{1,0:T(8,128)(2,1)}), bf16[512,4096]{1,0:T(8,128)(2,1)}) %all-gather.14.cloned.1.call-update) | async-done | bytes 4194320 | tf_op jit(solution)/shard_map/all_gather | solution.py:158
  142.5 91.0 %all-gather.12.cloned.1.call-done = bf16[2048,3072]{1,0:T(8,128)(2,1)} async-done(((bf16[64,3072]{1,0:T(8,128)(2,1)}), bf16[2048,3072]{1,0:T(8,128)(2,1)}) %all-gather.12.cloned.1.call-update) | async-done | bytes 12582928 | tf_op jit(solution)/shard_map/all_gather | solution.py:155
  233.6 16.7 copy.189
  250.3 9.0 fusion.52
  263.2 12.7 all-gather.18.cloned.1.call-done
  290.3 64.2 %all-gather.20.cloned.1.call-done = bf16[2048,2048]{1,0:T(8,128)(2,1)} async-done(((bf16[64,2048]{1,0:T(8,128)(2,1)}), bf16[2048,2048]{1,0:T(8,128)(2,1)}) %all-gather.20.cloned.1.call-update) | async-done | bytes 8388624 | tf_op jit(solution)/shard_map/all_gather | solution.py:159
  364.2 11.3 all_gather.68
  375.5 10.5 all_gather.69
  386.0 10.2 all_gather.70
  396.2 38.8 %all-gather.28.cloned.1.call-done = bf16[2,1024,2048]{2,1,0:T(8,128)(2,1)} async-done(((bf16[2,64,2048]{2,1,0:T(8,128)(2,1)}), bf16[2,1024,2048]{2,1,0:T(8,128)(2,1)}) %all-gather.28.cloned.1.call-update) | async-done | bytes 8388624 | tf_op jit(solution)/shard_map/all_gather | solution.py:283
  446.5 63.8 %all-gather.30.cloned.1.call-done = bf16[2,1024,2048]{2,1,0:T(8,128)(2,1)} async-done(((bf16[2,64,2048]{2,1,0:T(8,128)(2,1)}), bf16[2,1024,2048]{2,1,0:T(8,128)(2,1)}) %all-gather.30.cloned.1.call-update) | async-done | bytes 8388624 | tf_op jit(solution)/shard_map/all_gather | solution.py:284
  533.2 23.1 scatter_custom_fusion
  561.1 120.8 %all-gather = bf16[32,64,16]{1,2,0:T(8,128)(2,1)S(1)} all-gather(bf16[1,64,16]{1,2,0:T(8,128)(2,1)S(1)} %bitcast.277), channel_id=1, replica_groups=mesh['fsdp'=2,'ctx'=16] {'fsdp','ctx'}, dimensions={0}, use_global_device_ids=true | all-gather | bytes 67584 | tf_op jit(solution)/shard_map/all_gather | solution.py:161
  682.8 17.6 scatter_custom_fusion.1
  713.8 11.7 fusion.100
  725.5 11.7 fusion.99
  737.2 48.0 %all-to-all-done.2 = bf16[16,64,2048]{2,1,0:T(8,128)(2,1)} async-done(((bf16[16,64,2048]{2,1,0:T(8,128)(2,1)}), bf16[16,64,2048]{2,1,0:T(8,128)(2,1)}, u32[]{:S(2)}, u32[]{:S(2)}) %all-to-all-start.2) | async-done | bytes 4194336 | tf_op jit(solution)/shard_map/all_to_all | solution.py:244
  785.2 16.1 multiply_convert_fusion.2
  809.5 58.0 %all-to-all-start.1 = ((bf16[16,64,2048]{2,1,0:T(8,128)(2,1)}), bf16[16,64,2048]{2,1,0:T(8,128)(2,1)}, u32[]{:S(2)}, u32[]{:S(2)}) async-start(bf16[16,64,2048]{2,1,0:T(8,128)(2,1)} %bitcast.267), calls=%async_computation.1 | async-start | bytes 8388608 | tf_op jit(solution)/shard_map/all_to_all | solution.py:256
  867.6 9.8 fusion.104
  885.7 81.6 %all-to-all-done.1 = bf16[16,64,2048]{2,1,0:T(8,128)(2,1)} async-done(((bf16[16,64,2048]{2,1,0:T(8,128)(2,1)}), bf16[16,64,2048]{2,1,0:T(8,128)(2,1)}, u32[]{:S(2)}, u32[]{:S(2)}) %all-to-all-start.1) | async-done | bytes 4194336 | tf_op jit(solution)/shard_map/all_to_all | solution.py:256
  967.3 31.4 %all-to-all-start.3 = ((bf16[16,64,2048]{2,1,0:T(8,128)(2,1)}), bf16[16,64,2048]{2,1,0:T(8,128)(2,1)}, u32[]{:S(2)}, u32[]{:S(2)}) async-start(bf16[16,64,2048]{2,1,0:T(8,128)(2,1)} %bitcast.266), calls=%async_computation.4 | async-start | bytes 8388608 | tf_op jit(solution)/shard_map/all_to_all | solution.py:263
  998.7 9.2 gather_fusion
  1007.9 108.6 %all-to-all-done.3 = bf16[16,64,2048]{2,1,0:T(8,128)(2,1)} async-done(((bf16[16,64,2048]{2,1,0:T(8,128)(2,1)}), bf16[16,64,2048]{2,1,0:T(8,128)(2,1)}, u32[]{:S(2)}, u32[]{:S(2)}) %all-to-all-start.3) | async-done | bytes 4194336 | tf_op jit(solution)/shard_map/all_to_all | solution.py:263
  1116.5 9.9 gather_fusion.1
  1154.3 79.6 %reduce-scatter.18.cloned.1.call-done = f32[2,64,2048]{2,1,0:T(8,128)} async-done(((f32[2,1024,2048]{2,1,0:T(8,128)}), f32[2,64,2048]{2,1,0:T(8,128)}) %reduce-scatter.18.cloned.1.call-update) | async-done | bytes 1048592 | tf_op jit(solution)/shard_map/reduce_scatter | solution.py:290
  1289.2 11.2 convolution_convert_fusion.1
  1300.5 11.0 convolution_convert_fusion.2
  1311.5 11.0 convolution_convert_fusion
  1324.7 55.9 %reduce-scatter.22.cloned.1.call-done = bf16[2,64,512]{2,1,0:T(8,128)(2,1)} async-done(((bf16[2,1024,512]{2,1,0:T(8,128)(2,1)}), bf16[2,64,512]{2,1,0:T(8,128)(2,1)}) %reduce-scatter.22.cloned.1.call-update) | async-done | bytes 131088 | tf_op jit(solution)/shard_map/reduce_scatter | solution.py:357
  1402.2 8.9 copy.227
  1429.7 10.3 fusion.107
  1440.1 76.5 %reduce-scatter.46.cloned.1.call-done = f32[64,16]{1,0:T(8,128)} async-done(((f32[2048,16]{1,0:T(8,128)}), f32[64,16]{1,0:T(8,128)}) %reduce-scatter.46.cloned.1.call-update) | async-done | bytes 4112
  1518.0 13.8 reduce-scatter.44.cloned.1.call-done
  1533.7 17.0 reduce-scatter.42.cloned.1.call-done
  1552.6 17.6 reduce-scatter.40.cloned.1.call-done
  1572.1 72.4 %reduce-scatter.36.cloned.1.call-done = bf16[1024,1408]{1,0:T(8,128)(2,1)} async-done(((bf16[2048,1408]{1,0:T(8,128)(2,1)}), bf16[1024,1408]{1,0:T(8,128)(2,1)}) %reduce-scatter.36.cloned.1.call-update) | async-done | bytes 2883600 | tf_op jit(solution)/shard_map/reduce_scatter | solution.py:396
  1649.2 69.5 %reduce-scatter.34.cloned.1.call-done = bf16[1024,1408]{1,0:T(8,128)(2,1)} async-done(((bf16[2048,1408]{1,0:T(8,128)(2,1)}), bf16[1024,1408]{1,0:T(8,128)(2,1)}) %reduce-scatter.34.cloned.1.call-update) | async-done | bytes 2883600 | tf_op jit(solution)/shard_map/reduce_scatter | solution.py:396
  1723.4 69.0 %reduce-scatter.38.cloned.1.call-done = bf16[1024,1408]{1,0:T(8,128)(2,1)} async-done(((bf16[2048,1408]{1,0:T(8,128)(2,1)}), bf16[1024,1408]{1,0:T(8,128)(2,1)}) %reduce-scatter.38.cloned.1.call-update) | async-done | bytes 2883600 | tf_op jit(solution)/shard_map/reduce_scatter | solution.py:396
  1797.2 9.1 fusion.106
  1807.5 40.3 %all-reduce.6 = (f32[2048]{0:T(1024)S(1)}, f32[512]{0:T(512)S(1)}, f32[2048]{0:T(1024)S(1)}) all-reduce(f32[2048]{0:T(1024)S(1)} %get-tuple-element.31, f32[512]{0:T(512)S(1)} %copy-done.65, f32[2048]{0:T(1024)S(1)} %copy-done.60), channel_id=6, replica_groups=mesh['fsdp'=2,'ctx'=16] {'fsdp','ctx'}, use_global_device_ids=true, to_apply=%region_30.31.clone | all-reduce | flops 4608 | bytes 36864
  1850.9 88.1 %reduce-scatter.28.cloned.1.call-done = f32[64,576]{1,0:T(8,128)} async-done(((f32[2048,576]{1,0:T(8,128)}), f32[64,576]{1,0:T(8,128)}) %reduce-scatter.28.cloned.1.call-update) | async-done | bytes 147472 | tf_op jit(solution)/shard_map/reduce_scatter | solution.py:387
  1939.0 147.3 %reduce-scatter.30.cloned.1.call-done = f32[16,4096]{1,0:T(8,128)} async-done(((f32[512,4096]{1,0:T(8,128)}), f32[16,4096]{1,0:T(8,128)}) %reduce-scatter.30.cloned.1.call-update) | async-done | bytes 262160 | tf_op jit(solution)/shard_map/reduce_scatter | solution.py:389
  2086.3 180.6 %reduce-scatter.32.cloned.1.call-done = f32[64,2048]{1,0:T(8,128)} async-done(((f32[2048,2048]{1,0:T(8,128)}), f32[64,2048]{1,0:T(8,128)}) %reduce-scatter.32.cloned.1.call-update) | async-done | bytes 524304 | tf_op jit(solution)/shard_map/reduce_scatter | solution.py:390
  2266.9 256.8 %reduce-scatter.26.cloned.1.call-done = f32[64,3072]{1,0:T(8,128)} async-done(((f32[2048,3072]{1,0:T(8,128)}), f32[64,3072]{1,0:T(8,128)}) %reduce-scatter.26.cloned.1.call-update) | async-done | bytes 786448 | tf_op jit(solution)/shard_map/reduce_scatter | solution.py:386
  (373 shorter events, 269.5 us)
Async XLA Ops:
  7.2 69.6 %copy-start.61 = (s32[2,13,13]{2,0,1:T(2,128)S(1)}, s32[2,13,13]{2,0,1:T(2,128)}, u32[]{:S(2)}) copy-start(s32[2,13,13]{2,0,1:T(2,128)} %param.22) | copy-start | bytes 4060
  7.2 69.8 %copy-start.62 = (s32[2,1024]{1,0:T(2,128)S(1)}, s32[2,1024]{1,0:T(2,128)}, u32[]{:S(2)}) copy-start(s32[2,1024]{1,0:T(2,128)} %param.21) | copy-start | bytes 24580
  7.2 64.5 %all-gather.16.cloned.1.call-start = ((), (), s32[]{:S(2)}) async-start(), calls=%async_computation.21 | async-start | bytes 2703360 | tf_op jit(solution)/shard_map/all_gather | solution.py:156
  7.9 128.2 %all-gather.14.cloned.1.call-start = ((), (), s32[]{:S(2)}) async-start(), calls=%async_computation.20 | async-start | bytes 4325376 | tf_op jit(solution)/shard_map/all_gather | solution.py:158
  8.7 70.0 %copy-start.1 = (bf16[2,64,2048]{2,1,0:T(8,128)(2,1)S(1)}, bf16[2,64,2048]{2,1,0:T(8,128)(2,1)}, u32[]{:S(2)}) copy-start(bf16[2,64,2048]{2,1,0:T(8,128)(2,1)} %param.19) | copy-start | bytes 1572868
  8.7 224.9 %all-gather.12.cloned.1.call-start = ((), (), s32[]{:S(2)}) async-start(), calls=%async_computation.19 | async-start | bytes 12976128 | tf_op jit(solution)/shard_map/all_gather | solution.py:155
  9.4 266.4 %all-gather.18.cloned.1.call-start = ((), (), s32[]{:S(2)}) async-start(), calls=%async_computation.22 | async-start | bytes 2228224 | tf_op jit(solution)/shard_map/all_gather | solution.py:193
  10.8 63.9 %copy-start.66 = (f32[128]{0:T(128)}, f32[128]{0:T(128)S(1)}, u32[]{:S(2)}) copy-start(f32[128]{0:T(128)S(1)} %rsqrt.29) | copy-start | bytes 1540
  74.6 68.0 %copy-start.24 = (f32[128,576]{0,1:T(8,128)}, f32[128,576]{0,1:T(8,128)S(1)}, u32[]{:S(2)}) copy-start(f32[128,576]{0,1:T(8,128)S(1)} %fusion.98) | copy-start | bytes 884740
  76.1 278.4 %all-gather.20.cloned.1.call-start = ((), (), s32[]{:S(2)}) async-start(), calls=%async_computation.23 | async-start | bytes 8650752 | tf_op jit(solution)/shard_map/all_gather | solution.py:159
  76.7 358.2 %all-gather.28.cloned.1.call-start = ((), (), s32[]{:S(2)}) async-start(), calls=%async_computation.27 | async-start | bytes 8912896 | tf_op jit(solution)/shard_map/all_gather | solution.py:283
  76.8 282.6 %copy-start.55 = (f32[2048]{0:T(1024)}, f32[2048]{0:T(1024)S(1)}, u32[]{:S(2)}) copy-start(f32[2048]{0:T(1024)S(1)} %convert_element_type.216) | copy-start | bytes 24580
  77.4 65.2 %copy-start.73 = (f32[32]{0:T(128)}, f32[32]{0:T(128)S(1)}, u32[]{:S(2)}) copy-start(f32[32]{0:T(128)S(1)} %negate_power_fusion) | copy-start | bytes 388
  78.7 63.9 %copy-start.63 = (f32[2,64]{1,0:T(2,128)}, f32[2,64]{1,0:T(2,128)S(1)}, u32[]{:S(2)}) copy-start(f32[2,64]{1,0:T(2,128)S(1)} %add_convert_fusion.2) | copy-start | bytes 1540
  78.9 171.4 %copy-start.26 = (bf16[2,64,2048]{2,1,0:T(8,128)(2,1)}, bf16[2,64,2048]{2,1,0:T(8,128)(2,1)S(1)}, u32[]{:S(2)}) copy-start(bf16[2,64,2048]{2,1,0:T(8,128)(2,1)S(1)} %multiply_convert_fusion.12) | copy-start | bytes 1572868
  79.3 180.0 %copy-start.47 = (f32[2,64,32]{2,1,0:T(8,128)}, f32[2,64,32]{2,1,0:T(8,128)S(1)}, u32[]{:S(2)}) copy-start(f32[2,64,32]{2,1,0:T(8,128)S(1)} %get-tuple-element.60) | copy-start | bytes 49156
  101.6 178.5 %copy-start.32 = (bf16[2,1024,64]{2,1,0:T(8,128)(2,1)}, bf16[2,1024,64]{2,1,0:T(8,128)(2,1)S(1)}, u32[]{:S(2)}) copy-start(bf16[2,1024,64]{2,1,0:T(8,128)(2,1)S(1)} %all_gather.60) | copy-start | bytes 786436
  290.3 69.0 %copy-start.22 = (bf16[2,64,16,128]{3,2,1,0:T(8,128)(2,1)}, bf16[2,64,16,128]{3,2,1,0:T(8,128)(2,1)S(1)}, u32[]{:S(2)}) copy-start(bf16[2,64,16,128]{3,2,1,0:T(8,128)(2,1)S(1)} %copy.200) | copy-start | bytes 1572868
  361.3 149.0 %all-gather.30.cloned.1.call-start = ((), (), s32[]{:S(2)}) async-start(), calls=%async_computation.29 | async-start | bytes 8912896 | tf_op jit(solution)/shard_map/all_gather | solution.py:284
  362.1 351.8 %all-gather.24.cloned.1.call-start = ((), (), s32[]{:S(2)}) async-start(), calls=%async_computation.25 | async-start | bytes 8650752 | tf_op jit(solution)/shard_map/all_gather | solution.py:165
  362.8 362.7 %all-gather.22.cloned.1.call-start = ((), (), s32[]{:S(2)}) async-start(), calls=%async_computation.24 | async-start | bytes 8650752 | tf_op jit(solution)/shard_map/all_gather | solution.py:164
  363.6 373.6 %all-gather.26.cloned.1.call-start = ((), (), s32[]{:S(2)}) async-start(), calls=%async_computation.26 | async-start | bytes 8650752 | tf_op jit(solution)/shard_map/all_gather | solution.py:166
  364.1 786.7 %reduce-scatter.20.cloned.1.call-start = ((), (), s32[]{:S(2)}) async-start(), calls=%async_computation.30 | async-start | bytes 17825792 | tf_op jit(solution)/shard_map/reduce_scatter | solution.py:291
  556.3 125.8 %copy-start.30 = (bf16[2,64,2048]{2,1,0:T(8,128)(2,1)S(1)}, bf16[2,64,2048]{2,1,0:T(8,128)(2,1)}, u32[]{:S(2)}) copy-start(bf16[2,64,2048]{2,1,0:T(8,128)(2,1)} %param.20) | copy-start | bytes 1572868
  556.3 144.1 %all-to-all-start = ((bf16[16,64,2048]{2,1,0:T(8,128)(2,1)}), bf16[16,64,2048]{2,1,0:T(8,128)(2,1)}, u32[]{:S(2)}, u32[]{:S(2)}) async-start(bf16[16,64,2048]{2,1,0:T(8,128)(2,1)} %bitcast.258), calls=%async_computation | async-start | bytes 8388608 | tf_op jit(solution)/shard_map/all_to_all | solution.py:237
  700.5 84.7 %all-to-all-start.2 = ((bf16[16,64,2048]{2,1,0:T(8,128)(2,1)}), bf16[16,64,2048]{2,1,0:T(8,128)(2,1)}, u32[]{:S(2)}, u32[]{:S(2)}) async-start(bf16[16,64,2048]{2,1,0:T(8,128)(2,1)} %bitcast.257), calls=%async_computation.3 | async-start | bytes 8388608 | tf_op jit(solution)/shard_map/all_to_all | solution.py:244
  705.2 528.7 %reduce-scatter.18.cloned.1.call-start = ((), (), s32[]{:S(2)}) async-start(), calls=%async_computation.28 | async-start | bytes 17825792 | tf_op jit(solution)/shard_map/reduce_scatter | solution.py:290
  809.5 67.9 %slice-start.2 = ((s8[5767168]{0:T(1024)(128)(4,1)}), s8[1572864]{0:T(1024)(128)(4,1)S(1)}, s32[]{:S(2)}) async-start(s8[5767168]{0:T(1024)(128)(4,1)} %bitcast.284), calls=%async_computation.46 | async-start | bytes 3145728
  809.5 157.8 %all-to-all-start.1 = ((bf16[16,64,2048]{2,1,0:T(8,128)(2,1)}), bf16[16,64,2048]{2,1,0:T(8,128)(2,1)}, u32[]{:S(2)}, u32[]{:S(2)}) async-start(bf16[16,64,2048]{2,1,0:T(8,128)(2,1)} %bitcast.267), calls=%async_computation.1 | async-start | bytes 8388608 | tf_op jit(solution)/shard_map/all_to_all | solution.py:256
  967.3 149.2 %all-to-all-start.3 = ((bf16[16,64,2048]{2,1,0:T(8,128)(2,1)}), bf16[16,64,2048]{2,1,0:T(8,128)(2,1)}, u32[]{:S(2)}, u32[]{:S(2)}) async-start(bf16[16,64,2048]{2,1,0:T(8,128)(2,1)} %bitcast.266), calls=%async_computation.4 | async-start | bytes 8388608 | tf_op jit(solution)/shard_map/all_to_all | solution.py:263
  998.7 324.0 %reduce-scatter.24.cloned.1.call-start = ((), (), s32[]{:S(2)}) async-start(), calls=%async_computation.32 | async-start | bytes 557056 | tf_op jit(solution)/shard_map/reduce_scatter | solution.py:360
  1150.8 83.1 %copy-start.31 = (bf16[2,64,2048]{2,1,0:T(8,128)(2,1)S(1)}, bf16[2,64,2048]{2,1,0:T(8,128)(2,1)}, u32[]{:S(2)}) copy-start(bf16[2,64,2048]{2,1,0:T(8,128)(2,1)} %param.20) | copy-start | bytes 1572868
  1261.0 119.6 %reduce-scatter.22.cloned.1.call-start = ((), (), s32[]{:S(2)}) async-start(), calls=%async_computation.31 | async-start | bytes 2228224 | tf_op jit(solution)/shard_map/reduce_scatter | solution.py:357
  1269.1 247.5 %reduce-scatter.46.cloned.1.call-start = ((), (), s32[]{:S(2)}) async-start(), calls=%async_computation.43 | async-start | bytes 1081344
  1270.5 261.3 %reduce-scatter.44.cloned.1.call-start = ((), (), s32[]{:S(2)}) async-start(), calls=%async_computation.42 | async-start | bytes 1081344 | tf_op jit(solution)/shard_map/reduce_scatter | solution.py:396
  1276.9 273.8 %reduce-scatter.42.cloned.1.call-start = ((), (), s32[]{:S(2)}) async-start(), calls=%async_computation.41 | async-start | bytes 1081344 | tf_op jit(solution)/shard_map/reduce_scatter | solution.py:396
  1282.9 287.3 %reduce-scatter.40.cloned.1.call-start = ((), (), s32[]{:S(2)}) async-start(), calls=%async_computation.40 | async-start | bytes 1081344 | tf_op jit(solution)/shard_map/reduce_scatter | solution.py:396
  1289.2 355.3 %reduce-scatter.36.cloned.1.call-start = ((), (), s32[]{:S(2)}) async-start(), calls=%async_computation.38 | async-start | bytes 8650752 | tf_op jit(solution)/shard_map/reduce_scatter | solution.py:396
  1300.4 418.3 %reduce-scatter.34.cloned.1.call-start = ((), (), s32[]{:S(2)}) async-start(), calls=%async_computation.37 | async-start | bytes 8650752 | tf_op jit(solution)/shard_map/reduce_scatter | solution.py:396
  1311.5 481.0 %reduce-scatter.38.cloned.1.call-start = ((), (), s32[]{:S(2)}) async-start(), calls=%async_computation.39 | async-start | bytes 8650752 | tf_op jit(solution)/shard_map/reduce_scatter | solution.py:396
  1322.6 60.8 %copy-start.25 = (f32[128,576]{0,1:T(8,128)S(1)}, f32[128,576]{0,1:T(8,128)}, u32[]{:S(2)}) copy-start(f32[128,576]{0,1:T(8,128)} %copy-done.24) | copy-start | bytes 884740
  1322.6 60.8 %copy-start.59 = (f32[512]{0:T(512)S(1)}, f32[512]{0:T(512)}, u32[]{:S(2)}) copy-start(f32[512]{0:T(512)} %copy-done.58) | copy-start | bytes 6148
  1322.6 60.8 %copy-start.69 = (f32[128]{0:T(128)S(1)}, f32[128]{0:T(128)}, u32[]{:S(2)}) copy-start(f32[128]{0:T(128)} %copy-done.68) | copy-start | bytes 1540
  1322.6 61.7 %copy-start.29 = (bf16[128,2048]{1,0:T(8,128)(2,1)S(1)}, bf16[128,2048]{1,0:T(8,128)(2,1)}, u32[]{:S(2)}) copy-start(bf16[128,2048]{1,0:T(8,128)(2,1)} %copy-done.28) | copy-start | bytes 1572868
  1322.6 616.4 %reduce-scatter.28.cloned.1.call-start = ((), (), s32[]{:S(2)}) async-start(), calls=%async_computation.34 | async-start | bytes 5406720 | tf_op jit(solution)/shard_map/reduce_scatter | solution.py:387
  1387.5 698.8 %reduce-scatter.30.cloned.1.call-start = ((), (), s32[]{:S(2)}) async-start(), calls=%async_computation.35 | async-start | bytes 8650752 | tf_op jit(solution)/shard_map/reduce_scatter | solution.py:389
  1411.2 855.7 %reduce-scatter.32.cloned.1.call-start = ((), (), s32[]{:S(2)}) async-start(), calls=%async_computation.36 | async-start | bytes 17301504 | tf_op jit(solution)/shard_map/reduce_scatter | solution.py:390
  1420.7 1103.1 %reduce-scatter.26.cloned.1.call-start = ((), (), s32[]{:S(2)}) async-start(), calls=%async_computation.33 | async-start | bytes 25952256 | tf_op jit(solution)/shard_map/reduce_scatter | solution.py:386
  (64 other events, 397.8 us)
Sparse Core Ops, SparseCore 0:
  11.0 60.7 all-gather.15
  74.6 61.5 all-gather.13
  139.0 94.5 all-gather.11
  236.2 39.5 all-gather.17
  278.5 75.9 all-gather.19
  361.4 73.4 all-gather.27
  437.1 73.1 all-gather.29
  511.8 72.7 all-gather.23
  586.2 74.8 all-gather.21
  662.4 74.5 all-gather.25
  741.1 243.3 reduce-scatter.19
  988.5 245.3 reduce-scatter.17
  1261.1 54.7 reduce-scatter.23
  1320.0 60.6 reduce-scatter.21
  1382.7 133.8 reduce-scatter.45
  1518.8 12.9 reduce-scatter.43
  1533.9 16.7 reduce-scatter.41
  1553.5 16.6 reduce-scatter.39
  1573.1 71.3 reduce-scatter.35
  1647.3 71.3 reduce-scatter.33
  1721.0 71.3 reduce-scatter.37
  1795.4 143.5 reduce-scatter.27
  1942.0 144.2 reduce-scatter.29
  2089.1 177.7 reduce-scatter.31
  2275.0 248.6 reduce-scatter.25
where the time goes:
time: 2540 us; the launch traced here: 2530 us
  waiting for transfers between devices  1710 us (67%)
  matrix products  262 us (10%)
  blocking collectives  257 us (10%)
  local copies, waits for them, and re-layouts  107 us (4%)
  starting transfers between devices  101 us (4%)
  other arithmetic  80 us (3%)
    reduce_scatter x6, waiting for transfers between devices, body(): lax.psum_scatter(for_sending(ffn_total), 'fsdp', scatter_dimension=0, til...  259 us
    reduce_scatter x1, waiting for transfers between devices, body(): lax.psum_scatter(attn_total[1], ('fsdp', 'ctx'), scatter_dimension=0, til...  257 us
    reduce_scatter x1, waiting for transfers between devices, body(): lax.psum_scatter(attn_total[5], ('fsdp', 'ctx'), scatter_dimension=0, til...  181 us
    reduce_scatter x1, waiting for transfers between devices, body(): lax.psum_scatter(attn_total[4], ('fsdp', 'ctx'), scatter_dimension=0, til...  147 us
    all_gather x1, blocking collectives, body(): lax.all_gather(router, ('fsdp', 'ctx'), axis=0, tiled=True)  121 us
    all_to_all x1, waiting for transfers between devices, body(): lax.all_to_all(expert_back.astype(jnp.bfloat16).reshape(experts, trees *...  109 us
    all_gather x1, waiting for transfers between devices, body(): lax.all_gather(attn_q, ('fsdp', 'ctx'), axis=0, tiled=True)  91 us
    reduce_scatter x1, waiting for transfers between devices, body(): lax.psum_scatter(attn_total[2], ('fsdp', 'ctx'), scatter_dimension=0, til...  88.1 us
  transfers between devices with their start and end apart: 29, of which 23 were waited for; matrix products, arithmetic and copies ran while one was open for 16% of the time, Pallas kernels for 0%

commit v1 on v0

v1 whole, which is shorter than its diff:
```python
import functools
import math

import jax
import jax.numpy as jnp
from jax import lax
from jax.experimental import pallas as pl
from jax.experimental.pallas import tpu as pltpu
from jax.sharding import PartitionSpec as P

D = 2048
H = 16
DN = 128
DR = 64
DV = 128
LAT = 512
TOP = 6
SEGS = 13
PACK = 2048

MESH = pl.DeviceIdType.MESH
BF = jnp.bfloat16
F32 = jnp.float32

epsilon = 1e-06
rope_base = 10000.0


def multiply(left, right):
    return jnp.dot(left, right, preferred_element_type=F32)


def multiply_transposed(left, right):
    return lax.dot_general(left, right, (((1,), (1,)), ((), ())), preferred_element_type=F32)


def transposed_multiply(left, right):
    return lax.dot_general(left, right, (((0,), (0,)), ((), ())), preferred_element_type=F32)


def normalize(tensor_in, gain_vec):
    inverse = lax.rsqrt(jnp.mean(tensor_in * tensor_in, axis=-1, keepdims=True) + epsilon)
    normed = tensor_in * inverse
    return (normed, inverse, normed * gain_vec)


def normalize_back(grad_out, normed, inverse, gain_vec):
    weighted = grad_out * gain_vec
    centre = jnp.mean(weighted * normed, axis=-1, keepdims=True)
    return (inverse * (weighted - normed * centre), jnp.sum(grad_out * normed, axis=0))


def rotate(tensor_in, cosine, sine):
    half_width = tensor_in.shape[-1] // 2
    former = tensor_in[..., :half_width]
    latter = tensor_in[..., half_width:]
    return jnp.concatenate(
        [former * cosine - latter * sine, latter * cosine + former * sine], axis=-1
    )


def tree_mask(segment_ids, path_table, first_row, row_count):
    labels = jnp.arange(SEGS, dtype=jnp.int32)
    own_ids = lax.dynamic_slice_in_dim(segment_ids, first_row, row_count)
    own_hot = (own_ids[:, None] == labels[None, :]).astype(BF)
    all_hot = (segment_ids[:, None] == labels[None, :]).astype(BF)
    ancestry = multiply(own_hot, path_table.astype(BF)).astype(BF)
    related = multiply_transposed(ancestry, all_hot)
    places = jnp.arange(segment_ids.shape[0], dtype=jnp.int32)
    queries = first_row + jnp.arange(row_count, dtype=jnp.int32)
    allowed = (related > 0) & (places[None, :] <= queries[:, None])
    positions = jnp.sum(allowed.astype(jnp.int32), axis=1) - 1
    return (allowed, positions)


def three_parts(value):
    first = lax.reduce_precision(value, 8, 7)
    second = lax.reduce_precision(value - first, 8, 7)
    third = value - first - second
    return (first.astype(BF), second.astype(BF), third.astype(BF))


class Ring:
    def __init__(self, nf, nc):
        self.nf, self.chips = nf, nc // 2
        half = self.chips // 2
        if nf == 2:
            self.place = lambda p: (1 - p // half) * 2 * p + (p // half) * (4 * half - 1 - 2 * p)
            self.where = lambda j: (1 - j % 2) * (j // 2) + (j % 2) * (2 * half - 1 - j // 2)
        else:
            self.place = lambda p: (1 - p // half) * p + (p // half) * (3 * half - 1 - p)
            self.where = self.place

    def here(self):
        f, c = lax.axis_index("fsdp"), lax.axis_index("ctx")
        core = c % 2
        return f, c, core, self.where(c // 2), 1 - 2 * core

    def device(self, position, core):
        return self.place((position + 2 * self.chips) % self.chips) * 2 + core


def greet(ring, f, c, core, p, way, over_fsdp):
    barrier = pltpu.get_barrier_semaphore()
    targets = [(f, ring.device(p - way, core)), (f, c + 1 - 2 * core)]
    if over_fsdp:
        targets += [((f + k) % ring.nf, c) for k in range(1, ring.nf)]
    for target in targets:
        pl.semaphore_signal(barrier, inc=1, device_id=target, device_id_type=MESH)
    pl.semaphore_wait(barrier, len(targets))


def gather_kernel(ring, wide, leads, count, *refs):
    ins, outs = refs[:count], refs[count : 2 * count]
    own_sem, yss, yrs, rss, rrs, sss, srs = refs[2 * count :]
    f, c, core, p, way = ring.here()
    n, nf = ring.chips, ring.nf
    greet(ring, f, c, core, p, way, any(wide))
    to_next = (f, ring.device(p + way, core))
    to_twin = (f, c + 1 - 2 * core)
    started, own = [], []

    def remote(src, dst, ss, rs, dev):
        return pltpu.make_async_remote_copy(
            src_ref=src, dst_ref=dst, send_sem=ss, recv_sem=rs, device_id=dev, device_id_type=MESH
        )

    streams, late = [], []
    number = 0
    for i in range(count):
        if wide[i]:
            streams.append((number, i, f, ins[i]))
            number += 1
        else:
            for a in range(leads[i]):
                streams.append((number, i, a, ins[i].at[a]))
                number += 1
    first = len(streams)
    yn = 0
    for i in range(count):
        if wide[i]:
            for k in range(1, nf):
                late.append((number, i, (f - k + nf) % nf, k, yn))
                number += 1
                yn += 1

    def send_ring(s, number, i, lead, owner, src):
        cp = remote(src, outs[i].at[lead, owner], rss.at[s, number], rrs.at[s, number], to_next)
        cp.start()
        started.append(cp)

    def send_twin(s, number, i, lead, owner, src):
        cp = remote(src, outs[i].at[lead, owner], sss.at[s, number], srs.at[s, number], to_twin)
        cp.start()
        started.append(cp)

    for number, i, lead, k, y in late:
        cp = remote(ins[i], outs[i].at[f, c], yss.at[y], yrs.at[y], ((f + k) % nf, c))
        cp.start()
        started.append(cp)
    for number, i, lead, src in streams:
        send_ring(0, number, i, lead, c, src)
    for number, i, lead, src in streams:
        send_twin(0, number, i, lead, c, src)
        cp = pltpu.make_async_copy(src, outs[i].at[lead, c], own_sem.at[number])
        cp.start()
        own.append(cp)
    everything = [(number, i, lead) for number, i, lead, _ in streams]
    everything += [(number, i, lead) for number, i, lead, _, _ in late]
    for number, i, lead, k, y in late:
        here = outs[i].at[lead, c]
        remote(here, here, yss.at[y], yrs.at[y], to_next).wait_recv()
        send_ring(0, number, i, lead, c, here)
        send_twin(0, number, i, lead, c, here)
    for s in range(1, n):
        owner = ring.device(p - way * s, core)
        for number, i, lead in everything:
            here = outs[i].at[lead, owner]
            remote(here, here, rss.at[s - 1, number], rrs.at[s - 1, number], to_next).wait_recv()
            if s < n - 1:
                send_ring(s, number, i, lead, owner, here)
            send_twin(s, number, i, lead, owner, here)
    for s in range(n):
        owner = ring.device(p + way * s, 1 - core)
        for number, i, lead in everything:
            here = outs[i].at[lead, owner]
            remote(here, here, sss.at[s, number], srs.at[s, number], to_twin).wait_recv()
    for cp in own:
        cp.wait()
    for cp in started:
        cp.wait_send()


def ring_gather(ring, number, arrays, wide):
    n, nf = ring.chips, ring.nf
    leads = [1 if w else a.shape[0] for a, w in zip(arrays, wide)]
    shapes, streams, late, size = [], 0, 0, 0
    for a, w in zip(arrays, wide):
        if w:
            shapes.append(jax.ShapeDtypeStruct((nf, 2 * n) + a.shape, a.dtype))
            streams += nf
            late += nf - 1
        else:
            shapes.append(jax.ShapeDtypeStruct((a.shape[0], 2 * n) + a.shape[1:], a.dtype))
            streams += a.shape[0]
        size += shapes[-1].size * 2
    dma = pltpu.SemaphoreType.DMA
    return pl.pallas_call(
        functools.partial(gather_kernel, ring, tuple(wide), tuple(leads), len(arrays)),
        out_shape=shapes,
        in_specs=[pl.BlockSpec(memory_space=pl.ANY)] * len(arrays),
        out_specs=[pl.BlockSpec(memory_space=pl.ANY)] * len(arrays),
        scratch_shapes=[
            dma((streams,)),
            dma((max(1, late),)),
            dma((max(1, late),)),
            dma((n - 1, streams)),
            dma((n - 1, streams)),
            dma((n, streams)),
            dma((n, streams)),
        ],
        compiler_params=pltpu.CompilerParams(collective_id=number, has_side_effects=True),
        cost_estimate=pl.CostEstimate(flops=0, bytes_accessed=2 * size, transcendentals=0),
        name="ring_gather_%d" % number,
    )(*arrays)


def add_rows(shape, work):
    rows = shape[0]
    step = 16 if rows % 16 == 0 else rows

    def one(r, carry):
        work(pl.ds(pl.multiple_of(r * step, step), step))
        return carry

    lax.fori_loop(0, rows // step, one, 0)


def reduce_kernel(ring, wide, leads, count, *refs):
    ins, outs = refs[:count], refs[count : 2 * count]
    own, twin, got = (refs[(2 + k) * count : (3 + k) * count] for k in range(3))
    refs = refs[5 * count :]
    wides = sum(wide)
    finals, ygots = refs[:wides], refs[wides : 2 * wides]
    own_sem, tss, trs, rss, rrs, yss, yrs = refs[2 * wides :]
    f, c, core, p, way = ring.here()
    n, nf = ring.chips, ring.nf
    greet(ring, f, c, core, p, way, any(wide))
    to_next = (f, ring.device(p + way, core))
    to_twin = (f, c + 1 - 2 * core)

    def remote(src, dst, ss, rs, dev):
        return pltpu.make_async_remote_copy(
            src_ref=src, dst_ref=dst, send_sem=ss, recv_sem=rs, device_id=dev, device_id_type=MESH
        )

    streams = []
    for k in range(max(leads)):
        for i in range(count):
            if k < leads[i]:
                lead = (f + 1 + k) % nf if wide[i] else k
                streams.append((len(streams), i, k, lead))
    started, loads = [], {}
    for s in range(n):
        theirs = ring.device(p + way * (1 + s), 1 - core)
        mine = ring.device(p - way * (1 + s), core)
        for number, i, k, lead in streams:
            cp = remote(
                ins[i].at[lead, theirs], twin[i].at[s, k], tss.at[s, number], trs.at[s, number], to_twin
            )
            cp.start()
            started.append(cp)
            cp = pltpu.make_async_copy(
                ins[i].at[lead, mine], own[i].at[s, k], own_sem.at[s, number]
            )
            cp.start()
            loads[s, number] = cp

    def wait_parts(s, number, i, k):
        loads[s, number].wait()
        here = twin[i].at[s, k]
        remote(here, here, tss.at[s, number], trs.at[s, number], to_twin).wait_recv()

    def pass_on(s, number, i, k, src):
        cp = remote(src, got[i].at[s, k], rss.at[s, number], rrs.at[s, number], to_next)
        cp.start()
        started.append(cp)

    for s in range(n):
        for number, i, k, lead in streams:
            wait_parts(s, number, i, k)
            mine, other = own[i].at[s, k], twin[i].at[s, k]
            if s == 0:

                def start(rows, mine=mine, other=other):
                    mine[rows, :] = (mine[rows, :].astype(F32) + other[rows, :].astype(F32)).astype(BF)

                add_rows(mine.shape, start)
                pass_on(0, number, i, k, mine)
                continue
            came = got[i].at[s - 1, k]
            remote(came, came, rss.at[s - 1, number], rrs.at[s - 1, number], to_next).wait_recv()
            if s < n - 1:

                def middle(rows, mine=mine, other=other, came=came):
                    total = mine[rows, :].astype(F32) + other[rows, :].astype(F32)
                    came[rows, :] = (came[rows, :].astype(F32) + total).astype(BF)

                add_rows(mine.shape, middle)
                pass_on(s, number, i, k, came)
                continue
            if not wide[i]:
                target = outs[i].at[k]
            elif k == nf - 1:
                target = outs[i]
            else:
                target = finals[sum(wide[:i])].at[k]

            def last(rows, mine=mine, other=other, came=came, target=target):
                total = mine[rows, :].astype(F32) + other[rows, :].astype(F32)
                target[rows, :] = (came[rows, :].astype(F32) + total).astype(target.dtype)

            add_rows(mine.shape, last)
            if wide[i] and k < nf - 1:
                w = sum(wide[:i])
                cp = remote(target, ygots[w].at[k], yss.at[w, k], yrs.at[w, k], ((f + 1 + k) % nf, c))
                cp.start()
                started.append(cp)
    for i in range(count):
        if wide[i]:
            w = sum(wide[:i])
            for k in range(nf - 1):
                here = ygots[w].at[k]
                remote(here, here, yss.at[w, k], yrs.at[w, k], to_next).wait_recv()

                def finish(rows, here=here, target=outs[i]):
                    target[rows, :] = target[rows, :] + here[rows, :].astype(F32)

                add_rows(here.shape, finish)
    for cp in started:
        cp.wait_send()


def ring_reduce(ring, number, arrays, wide):
    n, nf = ring.chips, ring.nf
    leads = [a.shape[0] for a in arrays]
    streams = sum(leads)
    block = [a.shape[2:] for a in arrays]
    shapes = [
        jax.ShapeDtypeStruct(b if w else (l,) + b, F32) for b, w, l in zip(block, wide, leads)
    ]
    dma = pltpu.SemaphoreType.DMA
    scratch = [pltpu.VMEM((n, l) + b, BF) for b, l in zip(block, leads)] * 2
    scratch += [pltpu.VMEM((n - 1, l) + b, BF) for b, l in zip(block, leads)]
    scratch += [pltpu.VMEM((nf - 1,) + b, BF) for b, w in zip(block, wide) if w] * 2
    wides = max(1, sum(wide))
    size = sum(a.size * 2 for a in arrays)
    return pl.pallas_call(
        functools.partial(reduce_kernel, ring, tuple(wide), tuple(leads), len(arrays)),
        out_shape=shapes,
        in_specs=[pl.BlockSpec(memory_space=pl.ANY)] * len(arrays),
        out_specs=[pl.BlockSpec(memory_space=pltpu.VMEM)] * len(arrays),
        scratch_shapes=scratch
        + [
            dma((n, streams)),
            dma((n, streams)),
            dma((n, streams)),
            dma((n - 1, streams)),
            dma((n - 1, streams)),
            dma((wides, max(1, nf - 1))),
            dma((wides, max(1, nf - 1))),
        ],
        compiler_params=pltpu.CompilerParams(
            collective_id=number, has_side_effects=True, vmem_limit_bytes=56 << 20
        ),
        cost_estimate=pl.CostEstimate(flops=0, bytes_accessed=2 * size, transcendentals=0),
        name="ring_reduce_%d" % number,
    )(*arrays)


def body(
    tokens,
    out_grad,
    segments,
    path_mask,
    expert_ids,
    norm_attn,
    attn_q,
    attn_kva,
    norm_latent,
    attn_kvb,
    attn_out,
    norm_ffn,
    router,
    expert_gate,
    expert_up,
    expert_down,
    shared_gate,
    shared_up,
    shared_down,
):
    trees, tok_loc = tokens.shape[:2]
    row_total = trees * tok_loc
    nc, nf = lax.axis_size("ctx"), lax.axis_size("fsdp")
    mine, group = lax.axis_index("ctx"), lax.axis_index("fsdp")
    experts = nc
    ring = Ring(nf, nc)
    tree_len = tok_loc * nc
    group_rows = trees * tree_len
    first_row = mine * tok_loc
    capacity = min(tok_loc, tok_loc * TOP * 4 // (3 * experts))
    slot_total = nc * trees * capacity
    score_scale = 1.0 / math.sqrt(DN + DR)
    frequency = rope_base ** (-(jnp.arange(DR // 2, dtype=F32) * 2.0 / DR))
    labels = jnp.arange(experts, dtype=jnp.int32)
    both = ("fsdp", "ctx")
    part = D // nf

    def roll_in(x):
        return lax.dynamic_slice_in_dim(jnp.concatenate([x, x], axis=-1), group * part, D, x.ndim - 1)

    def roll_out(x):
        return lax.dynamic_slice_in_dim(
            jnp.concatenate([x, x], axis=-1), (nf - group) % nf * part, D, x.ndim - 1
        )

    def fetch(w):
        pieces = [w]
        for k in range(1, nf):
            pieces.append(lax.ppermute(w, "fsdp", [(i, (i - k) % nf) for i in range(nf)]))
        return pieces

    shared_w = jnp.concatenate([shared_gate, shared_up, shared_down], axis=1)
    fs = shared_gate.shape[1]
    e_gate, e_up, e_down = fetch(expert_gate), fetch(expert_up), fetch(expert_down)
    s_all = fetch(shared_w)

    small = jnp.concatenate(
        [
            norm_attn,
            norm_ffn,
            norm_latent,
            router.reshape(-1),
            expert_ids.astype(BF).reshape(-1),
        ]
    )
    small = jnp.pad(small, (0, PACK - small.shape[0])).reshape(16, PACK // 16)
    if nf == 2:
        w_latent, w_query, w_expand, small_all = ring_gather(
            ring, 0, [attn_kva, attn_q, attn_kvb, small], [True] * 4
        )
    else:
        w_latent, w_query, w_expand, small_all = (
            lax.all_gather(w, both, axis=0) for w in (attn_kva, attn_q, attn_kvb, small)
        )
    w_output = lax.all_gather(attn_out, both, axis=0, tiled=True)
    w_latent, w_query = w_latent.reshape(D, -1), w_query.reshape(D, -1)
    w_expand = w_expand.reshape(LAT, -1)
    small_all = small_all.reshape(nf * nc, PACK)
    r_one, r_lat, r_router = norm_attn.shape[0], norm_latent.shape[0], router.size
    cuts = [0, r_one, 2 * r_one, 2 * r_one + r_lat, 2 * r_one + r_lat + r_router]
    gain_attn = small_all[:, cuts[0] : cuts[1]].reshape(-1).astype(F32)
    gain_ffn = small_all[:, cuts[1] : cuts[2]].reshape(-1).astype(F32)
    gain_latent = small_all[:, cuts[2] : cuts[3]].reshape(-1).astype(F32)
    w_router = small_all[:, cuts[3] : cuts[4]].reshape(D, experts)
    ids_all = lax.dynamic_slice_in_dim(small_all.reshape(nf, nc, PACK), group, 1, 0)[0]
    ids_all = ids_all[:, cuts[4] : cuts[4] + expert_ids.size].reshape(nc, trees, tok_loc, TOP)
    ids_all = ids_all.transpose(1, 0, 2, 3).reshape(group_rows, TOP)

    upstream_low = out_grad.reshape(row_total, D)
    upstream = upstream_low.astype(F32)
    tree_grads = lax.all_gather(roll_in(out_grad), "ctx", axis=1, tiled=True).reshape(group_rows, D)

    def one_mask(segment_ids, path_table):
        return tree_mask(segment_ids, path_table, first_row, tok_loc)

    allowed, positions = jax.vmap(one_mask)(segments, path_mask)
    rotation = positions.astype(F32)[:, :, None] * frequency[None, None, :]
    cosine, sine = jnp.cos(rotation), jnp.sin(rotation)
    inputs = tokens.astype(F32).reshape(row_total, D)
    normed_in, inverse_in, gained_in = normalize(inputs, gain_attn)
    hidden_in = gained_in.astype(BF)
    latent_all = multiply(hidden_in, w_latent)
    latent_normed, latent_inverse, latent_gained = normalize(latent_all[:, :LAT], gain_latent)
    key_latent = latent_gained.astype(BF).reshape(trees, tok_loc, LAT)
    key_rope = rotate(latent_all[:, LAT:].reshape(trees, tok_loc, DR), cosine, sine).astype(BF)
    (keys,) = ring_gather(
        ring, 1, [jnp.concatenate([key_latent, key_rope], axis=-1)], [False]
    )
    keys = keys.reshape(trees, tree_len, LAT + DR)
    keys_latent = keys[:, :, :LAT]
    query_all = multiply(hidden_in, w_query).reshape(trees, tok_loc, H, DN + DR)
    query_nope = query_all[..., :DN].astype(BF)
    query_rope = rotate(
        query_all[..., DN:], cosine[:, :, None, :], sine[:, :, None, :]
    ).astype(BF)
    expand = w_expand.reshape(LAT, H, DN + DV)
    expand_key = expand[..., :DN]
    expand_value = expand[..., DN:]
    query_latent = jnp.einsum(
        "bthn,chn->bthc", query_nope, expand_key, preferred_element_type=F32
    ).astype(BF)
    query_cat = jnp.concatenate([query_latent, query_rope], axis=-1).reshape(
        trees, tok_loc * H, LAT + DR
    )

    def attention_scores():
        raw_scores = jnp.einsum("bqc,bjc->bqj", query_cat, keys, preferred_element_type=F32)
        raw_scores = raw_scores.reshape(trees, tok_loc, H, tree_len)
        scores = jnp.where(allowed[:, :, None, :], raw_scores * score_scale, -1e30)
        return scores.reshape(trees, tok_loc * H, tree_len)

    scores = attention_scores()
    highest = jnp.max(scores, axis=-1, keepdims=True)
    exp_total = jnp.sum(jnp.exp(scores - highest), axis=-1, keepdims=True)
    log_total = highest + jnp.log(exp_total)
    weights_low = jnp.exp(scores - log_total).astype(BF)
    mixed = jnp.einsum("bqj,bjc->bqc", weights_low, keys_latent, preferred_element_type=F32)
    mixed = mixed.astype(BF).reshape(trees, tok_loc, H, LAT)
    heads = (
        jnp.einsum("bthc,chv->bthv", mixed, expand_value, preferred_element_type=F32)
        .astype(BF)
        .reshape(row_total, H * DV)
    )
    residual = inputs + multiply(heads, w_output)
    normed_mid, inverse_mid, gained_mid = normalize(residual, gain_ffn)
    hidden_mid = gained_mid.astype(BF)
    expert_probs = jax.nn.softmax(multiply(hidden_mid, w_router), axis=-1)

    probs_parts = jnp.concatenate(three_parts(expert_probs), axis=-1)
    probs_parts = jnp.pad(probs_parts, ((0, 0), (0, 128 - 3 * experts)))
    tree_rows, tree_probs = ring_gather(
        ring,
        2,
        [roll_in(hidden_mid).reshape(trees, tok_loc, D), probs_parts.reshape(trees, tok_loc, 128)],
        [False, False],
    )
    tree_rows = tree_rows.reshape(group_rows, D)
    tree_probs = tree_probs.reshape(group_rows, 128)

    member = jnp.any(ids_all == mine.astype(BF), axis=1)
    lanes = 128
    blocks = group_rows // lanes
    grid = member.astype(BF).reshape(blocks, lanes)
    upper = (jnp.arange(lanes)[:, None] <= jnp.arange(lanes)[None, :]).astype(BF)
    within = multiply(grid, upper)
    lower = (jnp.arange(blocks)[:, None] > jnp.arange(blocks)[None, :]).astype(BF)
    before = multiply(lower, within[:, lanes - 1 :].astype(BF))
    slot = (within + before).astype(jnp.int32).reshape(-1) - 1
    slot = jnp.where(member, slot, -1)
    select = (slot[None, :] == jnp.arange(slot_total, dtype=jnp.int32)[:, None]).astype(BF)

    is_mine = labels[None, :] == mine
    own_parts = jnp.sum(
        jnp.where(
            is_mine[:, None, :], tree_probs[:, : 3 * experts].reshape(group_rows, 3, experts), 0
        ).astype(F32),
        axis=-1,
    )
    row_gate = jnp.sum(own_parts, axis=-1)
    slot_gate = jnp.sum(multiply(select, own_parts.astype(BF)), axis=-1)

    e_rows = multiply(select, tree_rows).astype(BF)
    e_raw = multiply(select, tree_grads).astype(BF)
    e_grads = (slot_gate[:, None] * e_raw.astype(F32)).astype(BF)

    def into(rows, pieces):
        total = multiply(rows[:, :part], pieces[0])
        for k in range(1, nf):
            total = total + multiply(rows[:, k * part : (k + 1) * part], pieces[k])
        return total

    def feed_forward(rows, grads, gate, up, down):
        gate_pre, up_pre = into(rows, gate), into(rows, up)
        sigmoid_gate = jax.nn.sigmoid(gate_pre)
        activated = gate_pre * sigmoid_gate
        hidden_act = (activated * up_pre).astype(BF)
        inner_grad = into(grads, down)
        gate_grad = (
            inner_grad * up_pre * sigmoid_gate * (1.0 + gate_pre * (1.0 - sigmoid_gate))
        ).astype(BF)
        up_grad = (inner_grad * activated).astype(BF)
        return hidden_act, gate_grad, up_grad

    def weight_grads(rows, grads, hidden_act, gate_grad, up_grad):
        def one(k):
            cut = slice(k * part, (k + 1) * part)
            return (
                transposed_multiply(rows[:, cut], gate_grad),
                transposed_multiply(rows[:, cut], up_grad),
                transposed_multiply(grads[:, cut], hidden_act),
            )

        return one

    s_gate = [w[:, :fs] for w in s_all]
    s_up = [w[:, fs : 2 * fs] for w in s_all]
    s_down = [w[:, 2 * fs :] for w in s_all]

    e_hidden, e_gg, e_ug = feed_forward(e_rows, e_grads, e_gate, e_up, e_down)
    s_hidden, s_gg, s_ug = feed_forward(tree_rows, tree_grads, s_gate, s_up, s_down)

    back_parts, out_parts, slot_delta = [], [], 0.0
    for k in range(nf):
        cut = slice(k * part, (k + 1) * part)
        e_back = (multiply_transposed(e_gg, e_gate[k]) + multiply_transposed(e_ug, e_up[k])).astype(BF)
        s_back = multiply_transposed(s_gg, s_gate[k]) + multiply_transposed(s_ug, s_up[k])
        back_parts.append((transposed_multiply(select, e_back) + s_back).astype(BF))
        e_out = multiply_transposed(e_hidden, e_down[k]).astype(BF)
        slot_delta = slot_delta + jnp.sum(
            e_raw[:, cut].astype(F32) * e_out.astype(F32), axis=-1
        )
        s_out = multiply_transposed(s_hidden, s_down[k])
        out_parts.append((row_gate[:, None] * transposed_multiply(select, e_out) + s_out).astype(BF))
    delta_parts = jnp.stack(three_parts(slot_delta), axis=-1)
    row_delta = transposed_multiply(select, delta_parts).astype(BF)
    delta_out = jnp.where(is_mine[:, None, :], row_delta[:, :, None], 0).reshape(group_rows, 3 * experts)
    delta_out = jnp.pad(delta_out, ((0, 0), (0, 128 - 3 * experts)))

    def by_owner(x):
        return x.reshape(trees, nc, tok_loc, x.shape[-1])

    sums = ring_reduce(
        ring, 3, [by_owner(x) for x in back_parts] + [by_owner(delta_out)], [False] * (nf + 1)
    )
    back_sum = roll_out(jnp.concatenate(sums[:nf], axis=-1).reshape(row_total, D))
    prob_delta = jnp.sum(
        sums[nf].reshape(row_total, 128)[:, : 3 * experts].reshape(row_total, 3, experts), axis=1
    )
    out_sum = lax.psum_scatter(
        jnp.concatenate(out_parts, axis=-1).reshape(trees, tree_len, D),
        "ctx",
        scatter_dimension=1,
        tiled=True,
    )
    out_sum = roll_out(out_sum.reshape(row_total, D).astype(F32))
    output = (residual + out_sum).astype(BF).reshape(trees, tok_loc, D)

    e_one = weight_grads(e_rows, e_grads, e_hidden, e_gg, e_ug)
    s_one = weight_grads(tree_rows, tree_grads, s_hidden, s_gg, s_ug)
    e_came, s_came = [], []
    for k in range(1, nf):
        perm = [(i, (i + k) % nf) for i in range(nf)]
        e_came.append([lax.ppermute(g.astype(BF), "fsdp", perm) for g in e_one(k)])
        s_came.append(
            lax.ppermute(jnp.concatenate(s_one(k), axis=1).astype(BF), "fsdp", perm)
        )
    e_sums, s_sum = list(e_one(0)), jnp.concatenate(s_one(0), axis=1)
    for k in range(nf - 1):
        e_sums = [a + b.astype(F32) for a, b in zip(e_sums, e_came[k])]
        s_sum = s_sum + s_came[k].astype(F32)
    s_sums = [s_sum[:, :fs], s_sum[:, fs : 2 * fs], s_sum[:, 2 * fs :]]

    logit_grad = (
        expert_probs * (prob_delta - jnp.sum(expert_probs * prob_delta, axis=-1, keepdims=True))
    ).astype(BF)
    grad_router = transposed_multiply(hidden_mid, logit_grad)
    mid_grad = back_sum + multiply_transposed(logit_grad, w_router)
    mid_input, grad_gain_ffn = normalize_back(mid_grad, normed_mid, inverse_mid, gain_ffn)
    residual_grad = upstream + mid_input
    residual_low = residual_grad.astype(BF)
    grad_output = transposed_multiply(heads, residual_low).astype(BF)
    out_total = lax.psum_scatter(grad_output, both, scatter_dimension=0, tiled=True).astype(F32)
    heads_grad = (
        multiply_transposed(residual_low, w_output).astype(BF).reshape(trees, tok_loc, H, DV)
    )
    mixed_grad = jnp.einsum(
        "bthv,chv->bthc", heads_grad, expand_value, preferred_element_type=F32
    ).astype(BF)
    mixed_grad_flat = mixed_grad.reshape(trees, tok_loc * H, LAT)
    scores = attention_scores()
    weights_full = jnp.exp(scores - log_total)
    prob_grad = jnp.einsum(
        "bqc,bjc->bqj", mixed_grad_flat, keys_latent, preferred_element_type=F32
    )
    score_grad = (
        weights_full * (prob_grad - jnp.sum(weights_full * prob_grad, axis=-1, keepdims=True))
    ).astype(BF)
    keys_grad = (
        jnp.einsum("bqj,bqc->bjc", score_grad, query_cat, preferred_element_type=F32) * score_scale
    )
    latent_part = jnp.einsum(
        "bqj,bqc->bjc", weights_full.astype(BF), mixed_grad_flat, preferred_element_type=F32
    )
    keys_grad = jnp.concatenate(
        [keys_grad[..., :LAT] + latent_part, keys_grad[..., LAT:]], axis=-1
    ).astype(BF)
    (own_keys_grad,) = ring_reduce(
        ring, 4, [keys_grad.reshape(trees, nc, tok_loc, LAT + DR)], [False]
    )
    query_cat_grad = (
        jnp.einsum("bqj,bjc->bqc", score_grad, keys, preferred_element_type=F32) * score_scale
    ).reshape(trees, tok_loc, H, LAT + DR)
    qlat_grad = query_cat_grad[..., :LAT].astype(BF)
    qrope_grad = query_cat_grad[..., LAT:]
    qnope_grad = jnp.einsum("bthc,chn->bthn", qlat_grad, expand_key, preferred_element_type=F32)
    grad_key = jnp.einsum("bthc,bthn->chn", qlat_grad, query_nope, preferred_element_type=F32)
    grad_value = jnp.einsum("bthc,bthv->chv", mixed, heads_grad, preferred_element_type=F32)
    grad_expand = jnp.concatenate([grad_key, grad_value], axis=-1).reshape(LAT, H * (DN + DV))
    query_grad = jnp.concatenate(
        [qnope_grad, rotate(qrope_grad, cosine[:, :, None, :], -sine[:, :, None, :])], axis=-1
    )
    query_grad = query_grad.astype(BF).reshape(row_total, H * (DN + DR))
    grad_query = transposed_multiply(hidden_in, query_grad)
    hidden_grad = multiply_transposed(query_grad, w_query)
    latent_in_grad, grad_gain_latent = normalize_back(
        own_keys_grad[..., :LAT].reshape(row_total, LAT), latent_normed, latent_inverse, gain_latent
    )
    rope_back = rotate(own_keys_grad[..., LAT:], cosine, -sine).reshape(row_total, DR)
    latent_grad = jnp.concatenate([latent_in_grad, rope_back], axis=-1).astype(BF)
    grad_latent = transposed_multiply(hidden_in, latent_grad)
    hidden_grad = hidden_grad + multiply_transposed(latent_grad, w_latent)
    input_part, grad_gain_attn = normalize_back(hidden_grad, normed_in, inverse_in, gain_attn)
    input_grad = (input_part + residual_grad).reshape(trees, tok_loc, D)

    grad_small = jnp.concatenate(
        [
            grad_gain_attn.reshape(nf * nc, r_one),
            grad_gain_ffn.reshape(nf * nc, r_one),
            grad_gain_latent.reshape(nf * nc, r_lat),
            grad_router.reshape(nf * nc, r_router),
        ],
        axis=1,
    ).astype(BF)
    grad_small = jnp.pad(grad_small, ((0, 0), (0, PACK - grad_small.shape[1])))
    parts = [
        grad_query.astype(BF).reshape(nf, nc, -1, w_query.shape[1]),
        grad_expand.astype(BF).reshape(nf, nc, -1, w_expand.shape[1]),
        grad_latent.astype(BF).reshape(nf, nc, -1, w_latent.shape[1]),
        grad_small.reshape(nf, nc, 16, PACK // 16),
    ]
    if nf == 2:
        t_query, t_expand, t_latent, t_small = ring_reduce(ring, 5, parts, [True] * 4)
    else:
        t_query, t_expand, t_latent, t_small = (
            lax.psum_scatter(
                x.reshape((nf * nc,) + x.shape[2:]), both, scatter_dimension=0, tiled=True
            )[0].astype(F32)
            for x in parts
        )
    t_small = t_small.reshape(PACK)
    return (
        output,
        input_grad,
        t_small[cuts[0] : cuts[1]],
        t_query,
        t_latent,
        t_small[cuts[2] : cuts[3]],
        t_expand,
        out_total,
        t_small[cuts[1] : cuts[2]],
        t_small[cuts[3] : cuts[4]].reshape(-1, experts),
        *e_sums,
        *s_sums,
    )


def solution(mesh):
    placed = (
        P("fsdp", "ctx", None),
        P("fsdp", "ctx", None),
        P("fsdp", None),
        P("fsdp", None, None),
        P("fsdp", "ctx", None),
        P(("fsdp", "ctx")),
        P(("fsdp", "ctx"), None),
        P(("fsdp", "ctx"), None),
        P(("fsdp", "ctx")),
        P(("fsdp", "ctx"), None),
        P(("fsdp", "ctx"), None),
        P(("fsdp", "ctx")),
        P(("fsdp", "ctx"), None),
        P("fsdp", "ctx"),
        P("fsdp", "ctx"),
        P("fsdp", "ctx"),
        P("fsdp", "ctx"),
        P("fsdp", "ctx"),
        P("fsdp", "ctx"),
    )
    return jax.shard_map(
        body,
        mesh=mesh,
        in_specs=placed,
        out_specs=(
            P("fsdp", "ctx", None),
            P("fsdp", "ctx", None),
            P(("fsdp", "ctx")),
            P(("fsdp", "ctx"), None),
            P(("fsdp", "ctx"), None),
            P(("fsdp", "ctx")),
            P(("fsdp", "ctx"), None),
            P(("fsdp", "ctx"), None),
            P(("fsdp", "ctx")),
            P(("fsdp", "ctx"), None),
            P("fsdp", "ctx"),
            P("fsdp", "ctx"),
            P("fsdp", "ctx"),
            P("fsdp", "ctx"),
            P("fsdp", "ctx"),
            P("fsdp", "ctx"),
        ),
        check_vma=False,
    )
```

time: 2540 us -> 1190 us (0.47)
  waiting for transfers between devices: 1710 us -> 63 us
  Pallas kernels: 0 us -> 596 us
  blocking collectives: 257 us -> 0 us
  starting transfers between devices: 101 us -> 10.1 us
  matrix products: 262 us -> 330 us
  other arithmetic: 80 us -> 42.6 us
    reduce_scatter x14 -> x2, waiting for transfers between devices: 1070 us -> 0.02 us  [the longest x1 0.02 us: body(): lax.psum_scatter(jnp.concatenate(out_parts, axis=-1).reshape(trees, tree_...]
    pallas_call x0 -> x6, Pallas kernels: none -> 596 us  [the longest x3 408 us: ring_gather(): pl.pallas_call(functools.partial(gather_kernel, ring, tuple(wide), tuple(...]
    all_gather x10 -> x2, waiting for transfers between devices: 320 us -> 0.01 us  [the longest x1 0.01 us: body(): lax.all_gather(roll_in(out_grad), 'ctx', axis=1, tiled=True)]
    all_to_all x4 -> x0, waiting for transfers between devices: 238 us -> none  [the longest x1 109 us: body(): lax.all_to_all(expert_back.astype(jnp.bfloat16).reshape(experts, trees *...]
    all_gather x5 -> x0, blocking collectives: 175 us -> none  [the longest x1 121 us: body(): lax.all_gather(router, ('fsdp', 'ctx'), axis=0, tiled=True)]
    all_to_all x4 -> x0, starting transfers between devices: 98.8 us -> none  [the longest x1 58 us: body(): lax.all_to_all(expert_result.astype(jnp.bfloat16).reshape(experts, trees...]
    unnamed x2 -> x0, blocking collectives: 82.6 us -> none
    unnamed x26 -> x4, waiting for transfers between devices: 82 us -> 0.74 us
  transfers between devices with their start and end apart: 29 -> 12, of which waited for: 23 -> 1; matrix products, arithmetic and copies ran while one was open for 16% -> 37% of each run, Pallas kernels for 0% -> 50%
where the time goes in v1:
time: 1190 us; the launch traced here: 1180 us
  Pallas kernels  596 us (50%)
  matrix products  330 us (28%)
  local copies, waits for them, and re-layouts  123 us (10%)
  waiting for transfers between devices  63 us (5%)
  other arithmetic  42.6 us (4%)
  between operations  16.2 us (1%)
    pallas_call x3, Pallas kernels, ring_gather(): pl.pallas_call(functools.partial(gather_kernel, ring, tuple(wide), tuple(...  408 us
    pallas_call x3, Pallas kernels, ring_reduce(): pl.pallas_call(functools.partial(reduce_kernel, ring, tuple(wide), tuple(...  188 us
    dot_general x21, matrix products, transposed_multiply(): lax.dot_general(left, right, (((0,), (0,)), ((), ())), preferred_element_...  116 us
    dot_general x21, matrix products, multiply(): return jnp.dot(left, right, preferred_element_type=F32)  100 us
    dot_general x15, matrix products, multiply_transposed(): lax.dot_general(left, right, (((1,), (1,)), ((), ())), preferred_element_...  75.1 us
    ppermute x3, waiting for transfers between devices, body(): e_came.append([lax.ppermute(g.astype(BF), 'fsdp', perm) for g in e_one(k)])  62.2 us
    unnamed x247, local copies, waits for them, and re-layouts  30.9 us
  transfers between devices with their start and end apart: 12, of which 1 were waited for; matrix products, arithmetic and copies ran while one was open for 37% of the time, Pallas kernels for 50%

profile of v1, /device:TPU:0, one launch (start us, length us, event | category | flops | bytes accessed | tf_op | source)
XLA Modules:
  0.0 1180.1 jit_solution(10799901704337223574)
XLA Ops:
  18.7 329.5 %ring_gather_0.1 = (bf16[2,16,64,576]{3,2,1,0:T(8,128)(2,1)}, bf16[2,16,64,3072]{3,2,1,0:T(8,128)(2,1)}, bf16[2,16,16,4096]{3,2,1,0:T(8,128)(2,1)}, bf16[2,16,16,128]{3,2,1,0:T(8,128)(2,1)}) custom-call(bf16[64,576]{1,0:T(8,128)(2,1)} %refs_0_.1, bf16[64,3072]{1,0:T(8,128)(2,1)} %refs_1_.1, bf16[16,4096]{1,0:T(8,128)(2,1)} %refs_2_.1, ...), custom_call_target="tpu_custom_call" | custom-call | bytes 38535168 | tf_op jit(solution)/shard_map/ring_gather_0/pallas_call | solution.py:208
  365.2 30.0 %ring_gather_1.1 = bf16[2,16,64,576]{3,2,1,0:T(8,128)(2,1)} custom-call(bf16[2,64,576]{2,1,0:T(8,128)(2,1)} %pad_maximum_fusion.8.refs_0_), custom_call_target="tpu_custom_call" | custom-call | bytes 4718592 | tf_op jit(solution)/shard_map/ring_gather_1/pallas_call | solution.py:208
  395.2 17.0 %copy.126 = bf16[3072,2048]{1,0:T(8,128)(2,1)} copy(bf16[3072,2048]{0,1:T(8,128)(2,1)} %bitcast.241) | data formatting | bytes 25165824 | tf_op jit(solution)/shard_map/dot_general | solution.py:30
  412.3 9.0 fusion.119
  442.6 4.9 fusion.27
  447.6 4.8 multiply_reduce_fusion.7
  456.8 48.1 %ring_gather_2.1 = (bf16[2,16,64,2048]{3,2,1,0:T(8,128)(2,1)}, bf16[2,16,64,128]{3,2,1,0:T(8,128)(2,1)}) custom-call(bf16[2,64,2048]{2,1,0:T(8,128)(2,1)} %bitcast.282, bf16[2,64,128]{2,1,0:T(8,128)(2,1)} %bitcast.299), custom_call_target="tpu_custom_call" | custom-call | bytes 17825792 | tf_op jit(solution)/shard_map/ring_gather_2/pallas_call | solution.py:208
  507.8 13.9 %multiply_convert_fusion.1 = (bf16[1024,2048]{0,1:T(8,128)(2,1)}, bf16[1024,2048]{0,1:T(8,128)(2,1)}) fusion(f32[1024]{0:T(1024)S(1)} %fusion.110, bf16[2048,2048]{1,0:T(8,128)(2,1)} %bitcast.308, s32[2048]{0:T(1024)S(1)} %bitcast_select_fusion.1), kind=kOutput, calls=%fused_computation.6 | convolution fusion | flops 8600420352 | bytes 16789504 | tf_op jit(solution)/shard_map/dot_general | solution.py:30
  521.7 10.6 fusion.19
  532.4 5.2 fusion.88
  544.1 5.4 fusion.60
  549.4 7.1 convolution_add_fusion.1
  556.5 7.0 convolution_add_fusion.2
  563.5 13.2 %multiply_convert_fusion.2 = (bf16[1024,1408]{1,0:T(8,128)(2,1)}, bf16[1024,1408]{1,0:T(8,128)(2,1)}, bf16[1024,1408]{1,0:T(8,128)(2,1)S(1)}) fusion(f32[1024,1408]{1,0:T(8,128)} %convolution_add_fusion.2, f32[1024,1408]{1,0:T(8,128)} %convolution_add_fusion.1, f32[1024,1408]{1,0:T(8,128)} %fusion.60, bf16[1024,1408]{1,0:T(8,128)(2,1)} %collective-permute-done.3, ...), kind=kOutput, calls=%fused_computation.26 | convolution fusion | flops 2975858688 | bytes 30932992 | tf_op jit(solution)/shard_map/dot_general | solution.py:30
  580.8 4.8 fusion.6
  585.7 6.5 multiply_reduce_fusion.1
  593.9 4.8 fusion.5
  611.8 4.6 add_convert_fusion.2
  616.4 8.4 pad_maximum_fusion
  624.8 12.3 %copy.185 = bf16[2048,2048]{1,0:T(8,128)(2,1)} copy(bf16[2048,2048]{0,1:T(8,128)(2,1)} %pad_maximum_fusion) | data formatting | bytes 16777216 | tf_op jit(solution)/shard_map/reshape | solution.py:631
  652.0 8.1 convolution_convert_fusion.2
  660.7 5.2 convolution_convert_fusion.4
  667.3 4.6 fusion.181
  672.0 5.7 fusion.126
  677.7 5.0 fusion.179
  682.6 6.8 fusion.182
  689.4 13.1 %fusion.2 = f32[2048,1024]{1,0:T(8,128)} fusion(s32[2048]{0:T(1024)S(1)} %bitcast_select_fusion.1, f32[1024,1024]{1,0:T(8,128)} %fusion.179, bf16[1024,1408]{1,0:T(8,128)(2,1)} %get-tuple-element.95, bf16[1024,1408]{1,0:T(8,128)(2,1)} %param.33), kind=kOutput, calls=%fused_computation.12 | convolution fusion | flops 7251951616 | bytes 18358272 | tf_op jit(solution)/shard_map/dot_general | solution.py:38
  702.6 9.4 add_convert_fusion.1
  711.9 13.3 %fusion.1 = f32[2048,1024]{1,0:T(8,128)} fusion(s32[2048]{0:T(1024)S(1)} %bitcast_select_fusion.1, f32[1024,1024]{1,0:T(8,128)} %fusion.182, bf16[1024,1408]{1,0:T(8,128)(2,1)} %get-tuple-element.95, bf16[1024,1408]{1,0:T(8,128)(2,1)} %collective-permute-done.1), kind=kOutput, calls=%fused_computation.11 | convolution fusion | flops 7251951616 | bytes 18358272 | tf_op jit(solution)/shard_map/dot_general | solution.py:38
  725.2 9.3 add_convert_fusion
  734.5 49.9 %ring_reduce_3.1 = (f32[2,64,1024]{2,1,0:T(8,128)}, f32[2,64,1024]{2,1,0:T(8,128)}, f32[2,64,128]{2,1,0:T(8,128)}) custom-call(bf16[2,16,64,1024]{3,2,1,0:T(8,128)(2,1)} %bitcast.250, bf16[2,16,64,1024]{3,2,1,0:T(8,128)(2,1)} %bitcast.251, bf16[2,16,64,128]{3,2,1,0:T(8,128)(2,1)} %bitcast.281), custom_call_target="tpu_custom_call" | custom-call | bytes 17825792 | tf_op jit(solution)/shard_map/ring_reduce_3/pallas_call | solution.py:358
  788.4 6.9 convolution_convert_fusion.3
  798.1 5.7 convolution_convert_fusion.1
  824.2 7.3 convert_add_fusion
  831.5 6.9 convert_add_fusion.2
  838.4 62.2 %collective-permute-done.5 = bf16[1024,1408]{1,0:T(8,128)(2,1)} collective-permute-done((bf16[1024,1408]{1,0:T(8,128)(2,1)}, bf16[1024,1408]{1,0:T(8,128)(2,1)}, u32[]{:S(2)}, u32[]{:S(2)}) %collective-permute-start.5) | collective-permute-done | bytes 2883616 | tf_op jit(solution)/shard_map/ppermute | solution.py:644
  900.6 7.1 convert_add_fusion.1
  923.2 4.5 broadcast_multiply_fusion
  929.8 5.9 fusion.10
  942.7 32.0 %ring_reduce_4.1 = f32[2,64,576]{2,1,0:T(8,128)} custom-call(bf16[2,16,64,576]{3,2,1,0:T(8,128)(2,1)} %pad_maximum_fusion.3.refs_0_), custom_call_target="tpu_custom_call" | custom-call | bytes 4718592 | tf_op jit(solution)/shard_map/ring_reduce_4/pallas_call | solution.py:358
  978.3 7.9 broadcast_multiply_fusion.1
  986.2 5.8 copy.152
  1005.1 4.7 fusion.78
  1014.8 7.9 copy.169
  1022.7 7.5 convert_element_type.384.refs_1_
  1030.4 9.0 fusion.184
  1049.9 6.7 convolution_convert_fusion
  1056.6 106.0 %ring_reduce_5.1 = (f32[64,3072]{1,0:T(8,128)}, f32[16,4096]{1,0:T(8,128)}, f32[64,576]{1,0:T(8,128)}, f32[16,128]{1,0:T(8,128)}) custom-call(bf16[2,16,64,3072]{3,2,1,0:T(8,128)(2,1)} %bitcast.238, bf16[2,16,16,4096]{3,2,1,0:T(8,128)(2,1)} %convert_element_type.384.refs_1_, bf16[2,16,64,576]{3,2,1,0:T(8,128)(2,1)} %bitcast.253, ...), custom_call_target="tpu_custom_call" | custom-call | bytes 38535168 | tf_op jit(solution)/shard_map/ring_reduce_5/pallas_call | solution.py:358
  (434 shorter events, 192.7 us)
Async XLA Ops:
  7.2 10.8 copy-start.87
  7.2 10.8 copy-start.88
  7.2 10.8 copy-start.86
  7.2 435.4 %all-gather.5.cloned.1.call-start = ((), (), s32[]{:S(2)}) async-start(), calls=%async_computation.4 | async-start | bytes 8912896 | tf_op jit(solution)/shard_map/all_gather | solution.py:472
  9.3 341.3 %copy-start.10 = (bf16[2,64,2048]{2,1,0:T(8,128)(2,1)S(1)}, bf16[2,64,2048]{2,1,0:T(8,128)(2,1)}, u32[]{:S(2)}) copy-start(bf16[2,64,2048]{2,1,0:T(8,128)(2,1)} %param.19) | copy-start | bytes 1572868
  9.3 342.1 %copy-start.69 = (s32[2,13,13]{2,0,1:T(2,128)S(1)}, s32[2,13,13]{2,0,1:T(2,128)}, u32[]{:S(2)}) copy-start(s32[2,13,13]{2,0,1:T(2,128)} %param.22) | copy-start | bytes 4060
  9.3 342.2 %copy-start.89 = (s32[2,1024]{1,0:T(2,128)S(1)}, s32[2,1024]{1,0:T(2,128)}, u32[]{:S(2)}) copy-start(s32[2,1024]{1,0:T(2,128)} %param.21) | copy-start | bytes 24580
  9.4 438.2 %all-gather.3.cloned.1.call-start = ((), (), s32[]{:S(2)}) async-start(), calls=%async_computation.2 | async-start | bytes 8650752 | tf_op jit(solution)/shard_map/all_gather | solution.py:456
  10.1 785.2 %reduce-scatter.3.cloned.1.call-start = ((), (), s32[]{:S(2)}) async-start(), calls=%async_computation.3 | async-start | bytes 8912896 | tf_op jit(solution)/shard_map/reduce_scatter | solution.py:630
  12.4 586.3 %collective-permute-start.2 = (bf16[1024,528]{0,1:T(8,128)(2,1)}, bf16[1024,528]{0,1:T(8,128)(2,1)}, u32[]{:S(2)}, u32[]{:S(2)}) collective-permute-start(bf16[1024,528]{0,1:T(8,128)(2,1)} %pad_maximum_fusion.4), channel_id=1, source_target_pairs={{0,16},{16,0},{1,17},{17,1},{2,18},{18,2},{3,19},{19,3},{4,20},{20... | collective-permute-start | bytes 3244040 | tf_op jit(solution)/shard_map/ppermute | solution.py:430
  15.4 541.1 %collective-permute-start = (bf16[1024,1408]{1,0:T(8,128)(2,1)}, bf16[1024,1408]{1,0:T(8,128)(2,1)}, u32[]{:S(2)}, u32[]{:S(2)}) collective-permute-start(bf16[1024,1408]{1,0:T(8,128)(2,1)} %param.32), channel_id=1, source_target_pairs={{0,16},{16,0},{1,17},{17,1},{2,18},{18,2},{3,19},{19,3},{4,20},{20... | collective-permute-start | bytes 8650760 | tf_op jit(solution)/shard_map/ppermute | solution.py:430
  15.4 534.0 %collective-permute-start.1 = (bf16[1024,1408]{1,0:T(8,128)(2,1)}, bf16[1024,1408]{1,0:T(8,128)(2,1)}, u32[]{:S(2)}, u32[]{:S(2)}) collective-permute-start(bf16[1024,1408]{1,0:T(8,128)(2,1)} %param.33), channel_id=1, source_target_pairs={{0,16},{16,0},{1,17},{17,1},{2,18},{18,2},{3,19},{19,3},{4,20},{20... | collective-permute-start | bytes 8650760 | tf_op jit(solution)/shard_map/ppermute | solution.py:430
  17.4 546.1 %collective-permute-start.3 = (bf16[1024,1408]{1,0:T(8,128)(2,1)}, bf16[1024,1408]{1,0:T(8,128)(2,1)}, u32[]{:S(2)}, u32[]{:S(2)}) collective-permute-start(bf16[1024,1408]{1,0:T(8,128)(2,1)} %param.34), channel_id=1, source_target_pairs={{0,16},{16,0},{1,17},{17,1},{2,18},{18,2},{3,19},{19,3},{4,20},{20... | collective-permute-start | bytes 8650760 | tf_op jit(solution)/shard_map/ppermute | solution.py:430
  360.4 92.1 %copy-start.62 = (f32[2048]{0:T(1024)}, f32[2048]{0:T(1024)S(1)}, u32[]{:S(2)}) copy-start(f32[2048]{0:T(1024)S(1)} %reshape.514) | copy-start | bytes 24580
  363.0 49.2 %copy-start.25 = (f32[128,576]{0,1:T(8,128)}, f32[128,576]{0,1:T(8,128)S(1)}, u32[]{:S(2)}) copy-start(f32[128,576]{0,1:T(8,128)S(1)} %fusion.178) | copy-start | bytes 884740
  364.0 48.2 %copy-start.83 = (f32[32]{0:T(128)}, f32[32]{0:T(128)S(1)}, u32[]{:S(2)}) copy-start(f32[32]{0:T(128)S(1)} %negate_power_fusion) | copy-start | bytes 388
  364.1 31.1 %copy-start.72 = (f32[2,64]{1,0:T(2,128)}, f32[2,64]{1,0:T(2,128)S(1)}, u32[]{:S(2)}) copy-start(f32[2,64]{1,0:T(2,128)S(1)} %add_convert_fusion.11) | copy-start | bytes 1540
  364.4 57.0 %copy-start.52 = (f32[2,64,32]{2,1,0:T(8,128)}, f32[2,64,32]{2,1,0:T(8,128)S(1)}, u32[]{:S(2)}) copy-start(f32[2,64,32]{2,1,0:T(8,128)S(1)} %get-tuple-element.130) | copy-start | bytes 49156
  395.2 17.1 %copy-start.15 = (bf16[2,64,2048]{2,1,0:T(8,128)(2,1)S(1)}, bf16[2,64,2048]{2,1,0:T(8,128)(2,1)}, u32[]{:S(2)}) copy-start(bf16[2,64,2048]{2,1,0:T(8,128)(2,1)} %copy-done.14) | copy-start | bytes 1572868
  424.9 15.5 %copy-start.3 = (bf16[512,16,128]{2,1,0:T(8,128)(2,1)}, bf16[512,16,128]{2,1,0:T(8,128)(2,1)S(1)}, u32[]{:S(2)}) copy-start(bf16[512,16,128]{2,1,0:T(8,128)(2,1)S(1)} %get-tuple-element.100) | copy-start | bytes 6291460
  452.4 55.4 %copy-start.77 = (f32[128]{0:T(128)}, f32[128]{0:T(128)S(1)}, u32[]{:S(2)}) copy-start(f32[128]{0:T(128)S(1)} %add_rsqrt_fusion.1) | copy-start | bytes 1540
  506.3 15.4 %slice-start.6 = ((s8[8388608]{0:T(1024)(128)(4,1)}), s8[4194304]{0:T(1024)(128)(4,1)S(1)}, s32[]{:S(2)}) async-start(s8[8388608]{0:T(1024)(128)(4,1)} %bitcast.319), calls=%async_computation.12 | async-start | bytes 8388608
  507.8 13.9 %slice-start.7 = ((s8[8388608]{0:T(1024)(128)(4,1)}), s8[4194304]{0:T(1024)(128)(4,1)S(1)}, s32[]{:S(2)}) async-start(s8[8388608]{0:T(1024)(128)(4,1)} %bitcast.319), calls=%async_computation.13 | async-start | bytes 8388608
  608.4 28.8 %copy-start.36 = (bf16[2048,176]{0,1:T(8,128)(2,1)}, bf16[2048,176]{0,1:T(8,128)(2,1)S(1)}, u32[]{:S(2)}) copy-start(bf16[2048,176]{0,1:T(8,128)(2,1)S(1)} %get-tuple-element.104) | copy-start | bytes 2162692
  608.4 94.2 %copy-start.34 = (bf16[2048,176]{0,1:T(8,128)(2,1)}, bf16[2048,176]{0,1:T(8,128)(2,1)S(1)}, u32[]{:S(2)}) copy-start(bf16[2048,176]{0,1:T(8,128)(2,1)S(1)} %get-tuple-element.102) | copy-start | bytes 2162692
  608.4 116.8 %copy-start.32 = (bf16[2048,176]{0,1:T(8,128)(2,1)}, bf16[2048,176]{0,1:T(8,128)(2,1)S(1)}, u32[]{:S(2)}) copy-start(bf16[2048,176]{0,1:T(8,128)(2,1)S(1)} %get-tuple-element.103) | copy-start | bytes 2162692
  637.1 530.8 %reduce-scatter.5.cloned.1.call-start = ((), (), s32[]{:S(2)}) async-start(), calls=%async_computation.5 | async-start | bytes 8650752 | tf_op jit(solution)/shard_map/reduce_scatter | solution.py:663
  647.9 171.3 %collective-permute-start.7 = (bf16[1024,528]{0,1:T(8,128)(2,1)}, bf16[1024,528]{0,1:T(8,128)(2,1)}, u32[]{:S(2)}, u32[]{:S(2)}) collective-permute-start(bf16[1024,528]{0,1:T(8,128)(2,1)} %pad_maximum_fusion.5), channel_id=1, source_target_pairs={{0,16},{16,0},{1,17},{17,1},{2,18},{18,2},{3,19},{19,3},{4,20},{20... | collective-permute-start | bytes 3244040 | tf_op jit(solution)/shard_map/ppermute | solution.py:646
  660.1 162.4 %collective-permute-start.6 = (bf16[1024,1408]{1,0:T(8,128)(2,1)}, bf16[1024,1408]{1,0:T(8,128)(2,1)}, u32[]{:S(2)}, u32[]{:S(2)}) collective-permute-start(bf16[1024,1408]{1,0:T(8,128)(2,1)} %convolution_convert_fusion.2), channel_id=1, source_target_pairs={{0,16},{16,0},{1,17},{17,1},{2,18},{18,2},{3,19},{19,3},{4,20},{20... | collective-permute-start | bytes 8650760 | tf_op jit(solution)/shard_map/ppermute | solution.py:644
  665.9 165.6 %collective-permute-start.4 = (bf16[1024,1408]{1,0:T(8,128)(2,1)}, bf16[1024,1408]{1,0:T(8,128)(2,1)}, u32[]{:S(2)}, u32[]{:S(2)}) collective-permute-start(bf16[1024,1408]{1,0:T(8,128)(2,1)} %convolution_convert_fusion.4), channel_id=1, source_target_pairs={{0,16},{16,0},{1,17},{17,1},{2,18},{18,2},{3,19},{19,3},{4,20},{20... | collective-permute-start | bytes 8650760 | tf_op jit(solution)/shard_map/ppermute | solution.py:644
  689.4 13.1 %copy-start.48 = (bf16[1024,176]{0,1:T(8,128)(2,1)S(1)}, bf16[1024,176]{0,1:T(8,128)(2,1)}, u32[]{:S(2)}) copy-start(bf16[1024,176]{0,1:T(8,128)(2,1)} %param.36) | copy-start | bytes 1081348
  734.5 50.9 %copy-start.58 = (f32[128,16]{0,1:T(8,128)S(1)}, f32[128,16]{0,1:T(8,128)}, u32[]{:S(2)}) copy-start(f32[128,16]{0,1:T(8,128)} %copy-done.57) | copy-start | bytes 24580
  734.5 50.9 %copy-start.71 = (f32[128]{0:T(128)S(1)}, f32[128]{0:T(128)}, u32[]{:S(2)}) copy-start(f32[128]{0:T(128)} %copy-done.70) | copy-start | bytes 1540
  734.5 50.9 %copy-start.75 = (f32[128]{0:T(128)S(1)}, f32[128]{0:T(128)}, u32[]{:S(2)}) copy-start(f32[128]{0:T(128)} %copy-done.74) | copy-start | bytes 1540
  734.5 52.4 %copy-start.6 = (f32[128,2048]{1,0:T(8,128)S(1)}, f32[128,2048]{1,0:T(8,128)}, u32[]{:S(2)}) copy-start(f32[128,2048]{1,0:T(8,128)} %copy-done.5) | copy-start | bytes 3145732
  734.5 52.4 %copy-start.29 = (bf16[2048,16]{1,0:T(8,128)(2,1)S(1)}, bf16[2048,16]{1,0:T(8,128)(2,1)}, u32[]{:S(2)}) copy-start(bf16[2048,16]{1,0:T(8,128)(2,1)} %reshape.461) | copy-start | bytes 196612
  734.5 52.4 %copy-start.63 = (f32[2048]{0:T(1024)S(1)}, f32[2048]{0:T(1024)}, u32[]{:S(2)}) copy-start(f32[2048]{0:T(1024)} %copy-done.62) | copy-start | bytes 24580
  734.5 52.4 %copy-start.78 = (f32[128]{0:T(128)S(1)}, f32[128]{0:T(128)}, u32[]{:S(2)}) copy-start(f32[128]{0:T(128)} %copy-done.77) | copy-start | bytes 1540
  808.9 91.6 %collective-permute-start.5 = (bf16[1024,1408]{1,0:T(8,128)(2,1)}, bf16[1024,1408]{1,0:T(8,128)(2,1)}, u32[]{:S(2)}, u32[]{:S(2)}) collective-permute-start(bf16[1024,1408]{1,0:T(8,128)(2,1)} %convolution_convert_fusion.3), channel_id=1, source_target_pairs={{0,16},{16,0},{1,17},{17,1},{2,18},{18,2},{3,19},{19,3},{4,20},{20... | collective-permute-start | bytes 8650760 | tf_op jit(solution)/shard_map/ppermute | solution.py:644
  831.5 69.1 %copy-start.103 = (bf16[1024,1408]{1,0:T(8,128)(2,1)S(1)}, bf16[1024,1408]{1,0:T(8,128)(2,1)}, u32[]{:S(2)}) copy-start(bf16[1024,1408]{1,0:T(8,128)(2,1)} %get-tuple-element.95) | copy-start | bytes 8650756
  831.5 76.2 %slice-start.2 = ((s8[8388608]{0:T(1024)(128)(4,1)}), s8[4194304]{0:T(1024)(128)(4,1)S(1)}, s32[]{:S(2)}) async-start(s8[8388608]{0:T(1024)(128)(4,1)} %bitcast.239), calls=%async_computation.8 | async-start | bytes 8388608
  838.4 69.3 %slice-start.3 = ((s8[8388608]{0:T(1024)(128)(4,1)}), s8[4194304]{0:T(1024)(128)(4,1)S(1)}, s32[]{:S(2)}) async-start(s8[8388608]{0:T(1024)(128)(4,1)} %bitcast.239), calls=%async_computation.9 | async-start | bytes 8388608
  942.7 33.2 %copy-start.73 = (f32[2,64]{1,0:T(2,128)S(1)}, f32[2,64]{1,0:T(2,128)}, u32[]{:S(2)}) copy-start(f32[2,64]{1,0:T(2,128)} %copy-done.72) | copy-start | bytes 1540
  942.7 33.2 %copy-start.84 = (f32[32]{0:T(128)S(1)}, f32[32]{0:T(128)}, u32[]{:S(2)}) copy-start(f32[32]{0:T(128)} %copy-done.83) | copy-start | bytes 388
  942.7 35.3 %copy-start.26 = (f32[128,576]{0,1:T(8,128)S(1)}, f32[128,576]{0,1:T(8,128)}, u32[]{:S(2)}) copy-start(f32[128,576]{0,1:T(8,128)} %copy-done.25) | copy-start | bytes 884740
  942.7 35.3 %copy-start.67 = (f32[512]{0:T(512)S(1)}, f32[512]{0:T(512)}, u32[]{:S(2)}) copy-start(f32[512]{0:T(512)} %copy-done.66) | copy-start | bytes 6148
  942.7 35.3 %copy-start.80 = (f32[128]{0:T(128)S(1)}, f32[128]{0:T(128)}, u32[]{:S(2)}) copy-start(f32[128]{0:T(128)} %copy-done.79) | copy-start | bytes 1540
  1056.6 110.0 %copy-start.31 = (f32[128,2048]{1,0:T(8,128)S(1)}, f32[128,2048]{1,0:T(8,128)}, u32[]{:S(2)}) copy-start(f32[128,2048]{1,0:T(8,128)} %get-tuple-element.146) | copy-start | bytes 3145732
  (80 other events, 357.7 us)
Sparse Core Ops, SparseCore 0:
  10.8 82.8 all-gather.4
  96.5 94.2 all-gather.2
  637.2 104.9 reduce-scatter.2
  803.9 151.7 reduce-scatter.4

commit v2 on v1

--- a/solution.py
+++ b/solution.py
@@ -110,9 +110,10 @@
     pl.semaphore_wait(barrier, len(targets))
 
 
-def gather_kernel(ring, wide, leads, count, *refs):
-    ins, outs = refs[:count], refs[count : 2 * count]
-    own_sem, yss, yrs, rss, rrs, sss, srs = refs[2 * count :]
+def gather_kernel(ring, wide, leads, count, swaps, *refs):
+    swap_ins, swap_outs = refs[count : count + swaps], refs[2 * count + swaps : 2 * (count + swaps)]
+    ins, outs = refs[:count], refs[count + swaps : 2 * count + swaps]
+    own_sem, yss, yrs, rss, rrs, sss, srs, wss, wrs = refs[2 * (count + swaps) :]
     f, c, core, p, way = ring.here()
     n, nf = ring.chips, ring.nf
     greet(ring, f, c, core, p, way, any(wide))
@@ -172,6 +173,11 @@
         remote(here, here, yss.at[y], yrs.at[y], to_next).wait_recv()
         send_ring(0, number, i, lead, c, here)
         send_twin(0, number, i, lead, c, here)
+    swapped = []
+    for i in range(swaps):
+        cp = remote(swap_ins[i], swap_outs[i], wss.at[i], wrs.at[i], ((f + 1) % nf, c))
+        cp.start()
+        swapped.append(cp)
     for s in range(1, n):
         owner = ring.device(p - way * s, core)
         for number, i, lead in everything:
@@ -189,9 +195,11 @@
         cp.wait()
     for cp in started:
         cp.wait_send()
-
-
-def ring_gather(ring, number, arrays, wide):
+    for cp in swapped:
+        cp.wait()
+
+
+def ring_gather(ring, number, arrays, wide, swaps=()):
     n, nf = ring.chips, ring.nf
     leads = [1 if w else a.shape[0] for a, w in zip(arrays, wide)]
     shapes, streams, late, size = [], 0, 0, 0
@@ -205,11 +213,14 @@
             streams += a.shape[0]
         size += shapes[-1].size * 2
     dma = pltpu.SemaphoreType.DMA
+    shapes += [jax.ShapeDtypeStruct(a.shape, a.dtype) for a in swaps]
     return pl.pallas_call(
-        functools.partial(gather_kernel, ring, tuple(wide), tuple(leads), len(arrays)),
+        functools.partial(
+            gather_kernel, ring, tuple(wide), tuple(leads), len(arrays), len(swaps)
+        ),
         out_shape=shapes,
-        in_specs=[pl.BlockSpec(memory_space=pl.ANY)] * len(arrays),
-        out_specs=[pl.BlockSpec(memory_space=pl.ANY)] * len(arrays),
+        in_specs=[pl.BlockSpec(memory_space=pl.ANY)] * len(shapes),
+        out_specs=[pl.BlockSpec(memory_space=pl.ANY)] * len(shapes),
         scratch_shapes=[
             dma((streams,)),
             dma((max(1, late),)),
@@ -218,11 +229,13 @@
             dma((n - 1, streams)),
             dma((n, streams)),
             dma((n, streams)),
+            dma((max(1, len(swaps)),)),
+            dma((max(1, len(swaps)),)),
         ],
         compiler_params=pltpu.CompilerParams(collective_id=number, has_side_effects=True),
         cost_estimate=pl.CostEstimate(flops=0, bytes_accessed=2 * size, transcendentals=0),
         name="ring_gather_%d" % number,
-    )(*arrays)
+    )(*arrays, *swaps)
 
 
 def add_rows(shape, work):
@@ -432,9 +445,6 @@
 
     shared_w = jnp.concatenate([shared_gate, shared_up, shared_down], axis=1)
     fs = shared_gate.shape[1]
-    e_gate, e_up, e_down = fetch(expert_gate), fetch(expert_up), fetch(expert_down)
-    s_all = fetch(shared_w)
-
     small = jnp.concatenate(
         [
             norm_attn,
@@ -446,14 +456,21 @@
     )
     small = jnp.pad(small, (0, PACK - small.shape[0])).reshape(16, PACK // 16)
     if nf == 2:
-        w_latent, w_query, w_expand, small_all = ring_gather(
-            ring, 0, [attn_kva, attn_q, attn_kvb, small], [True] * 4
+        w_latent, w_query, w_expand, small_all, w_output, other_gate, other_shared = ring_gather(
+            ring, 0, [attn_kva, attn_q, attn_kvb, small, attn_out], [True] * 5, [expert_gate, shared_w]
+        )
+        e_gate, s_all = [expert_gate, other_gate], [shared_w, other_shared]
+        later_up, later_down, later_grads, small_all = lax.optimization_barrier(
+            (expert_up, expert_down, out_grad, small_all)
         )
     else:
-        w_latent, w_query, w_expand, small_all = (
-            lax.all_gather(w, both, axis=0) for w in (attn_kva, attn_q, attn_kvb, small)
+        w_latent, w_query, w_expand, small_all, w_output = (
+            lax.all_gather(w, both, axis=0) for w in (attn_kva, attn_q, attn_kvb, small, attn_out)
         )
-    w_output = lax.all_gather(attn_out, both, axis=0, tiled=True)
+        e_gate, s_all = fetch(expert_gate), fetch(shared_w)
+        later_up, later_down, later_grads = expert_up, expert_down, out_grad
+    e_up, e_down = fetch(later_up), fetch(later_down)
+    w_output = w_output.reshape(H * DV, D)
     w_latent, w_query = w_latent.reshape(D, -1), w_query.reshape(D, -1)
     w_expand = w_expand.reshape(LAT, -1)
     small_all = small_all.reshape(nf * nc, PACK)
@@ -469,7 +486,7 @@
 
     upstream_low = out_grad.reshape(row_total, D)
     upstream = upstream_low.astype(F32)
-    tree_grads = lax.all_gather(roll_in(out_grad), "ctx", axis=1, tiled=True).reshape(group_rows, D)
+    tree_grads = lax.all_gather(roll_in(later_grads), "ctx", axis=1, tiled=True).reshape(group_rows, D)
 
     def one_mask(segment_ids, path_table):
         return tree_mask(segment_ids, path_table, first_row, tok_loc)
@@ -489,7 +506,8 @@
     )
     keys = keys.reshape(trees, tree_len, LAT + DR)
     keys_latent = keys[:, :, :LAT]
-    query_all = multiply(hidden_in, w_query).reshape(trees, tok_loc, H, DN + DR)
+    query_all = lax.optimization_barrier(multiply(hidden_in, w_query))
+    query_all = query_all.reshape(trees, tok_loc, H, DN + DR)
     query_nope = query_all[..., :DN].astype(BF)
     query_rope = rotate(
         query_all[..., DN:], cosine[:, :, None, :], sine[:, :, None, :]
@@ -539,16 +557,26 @@
     tree_probs = tree_probs.reshape(group_rows, 128)
 
     member = jnp.any(ids_all == mine.astype(BF), axis=1)
-    lanes = 128
-    blocks = group_rows // lanes
-    grid = member.astype(BF).reshape(blocks, lanes)
-    upper = (jnp.arange(lanes)[:, None] <= jnp.arange(lanes)[None, :]).astype(BF)
-    within = multiply(grid, upper)
-    lower = (jnp.arange(blocks)[:, None] > jnp.arange(blocks)[None, :]).astype(BF)
-    before = multiply(lower, within[:, lanes - 1 :].astype(BF))
-    slot = (within + before).astype(jnp.int32).reshape(-1) - 1
-    slot = jnp.where(member, slot, -1)
-    select = (slot[None, :] == jnp.arange(slot_total, dtype=jnp.int32)[:, None]).astype(BF)
+    blocks = trees * nc
+    bundle = 4 if blocks % 4 == 0 else 1
+    bundles = blocks // bundle
+    grid = member.astype(BF).reshape(blocks, tok_loc)
+    upper = (jnp.arange(tok_loc)[:, None] <= jnp.arange(tok_loc)[None, :]).astype(BF)
+    slot = multiply(grid, upper).astype(jnp.int32) - 1
+    slot = slot + (jnp.arange(blocks, dtype=jnp.int32) % bundle * capacity)[:, None]
+    slot = jnp.where(grid > 0, slot, -1).reshape(bundles, bundle * tok_loc)
+    spots = jnp.arange(bundle * capacity, dtype=jnp.int32)
+    select = (slot[:, None, :] == spots[None, :, None]).astype(BF)
+
+    def take(x):
+        x = x.reshape(bundles, bundle * tok_loc, x.shape[-1])
+        y = jnp.einsum("gst,gtd->gsd", select, x, preferred_element_type=F32)
+        return y.reshape(slot_total, x.shape[-1])
+
+    def put(x):
+        x = x.reshape(bundles, bundle * capacity, x.shape[-1])
+        y = jnp.einsum("gst,gsd->gtd", select, x, preferred_element_type=F32)
+        return y.reshape(group_rows, x.shape[-1])
 
     is_mine = labels[None, :] == mine
     own_parts = jnp.sum(
@@ -558,10 +586,10 @@
         axis=-1,
     )
     row_gate = jnp.sum(own_parts, axis=-1)
-    slot_gate = jnp.sum(multiply(select, own_parts.astype(BF)), axis=-1)
-
-    e_rows = multiply(select, tree_rows).astype(BF)
-    e_raw = multiply(select, tree_grads).astype(BF)
+    slot_gate = jnp.sum(take(own_parts.astype(BF)), axis=-1)
+
+    e_rows = take(tree_rows).astype(BF)
+    e_raw = take(tree_grads).astype(BF)
     e_grads = (slot_gate[:, None] * e_raw.astype(F32)).astype(BF)
 
     def into(rows, pieces):
@@ -605,15 +633,15 @@
         cut = slice(k * part, (k + 1) * part)
         e_back = (multiply_transposed(e_gg, e_gate[k]) + multiply_transposed(e_ug, e_up[k])).astype(BF)
         s_back = multiply_transposed(s_gg, s_gate[k]) + multiply_transposed(s_ug, s_up[k])
-        back_parts.append((transposed_multiply(select, e_back) + s_back).astype(BF))
+        back_parts.append((put(e_back) + s_back).astype(BF))
         e_out = multiply_transposed(e_hidden, e_down[k]).astype(BF)
         slot_delta = slot_delta + jnp.sum(
             e_raw[:, cut].astype(F32) * e_out.astype(F32), axis=-1
         )
         s_out = multiply_transposed(s_hidden, s_down[k])
-        out_parts.append((row_gate[:, None] * transposed_multiply(select, e_out) + s_out).astype(BF))
+        out_parts.append((row_gate[:, None] * put(e_out) + s_out).astype(BF))
     delta_parts = jnp.stack(three_parts(slot_delta), axis=-1)
-    row_delta = transposed_multiply(select, delta_parts).astype(BF)
+    row_delta = put(delta_parts).astype(BF)
     delta_out = jnp.where(is_mine[:, None, :], row_delta[:, :, None], 0).reshape(group_rows, 3 * experts)
     delta_out = jnp.pad(delta_out, ((0, 0), (0, 128 - 3 * experts)))
 
@@ -627,13 +655,12 @@
     prob_delta = jnp.sum(
         sums[nf].reshape(row_total, 128)[:, : 3 * experts].reshape(row_total, 3, experts), axis=1
     )
-    out_sum = lax.psum_scatter(
-        jnp.concatenate(out_parts, axis=-1).reshape(trees, tree_len, D),
-        "ctx",
-        scatter_dimension=1,
-        tiled=True,
-    )
-    out_sum = roll_out(out_sum.reshape(row_total, D).astype(F32))
+    out_sum = [
+        lax.psum_scatter(x.reshape(trees, tree_len, part), "ctx", scatter_dimension=1, tiled=True)
+        for x in out_parts
+    ]
+    out_sum = jnp.concatenate(out_sum, axis=-1).reshape(row_total, D).astype(F32)
+    out_sum = roll_out(out_sum)
     output = (residual + out_sum).astype(BF).reshape(trees, tok_loc, D)
 
     e_one = weight_grads(e_rows, e_grads, e_hidden, e_gg, e_ug)
@@ -645,12 +672,6 @@
         s_came.append(
             lax.ppermute(jnp.concatenate(s_one(k), axis=1).astype(BF), "fsdp", perm)
         )
-    e_sums, s_sum = list(e_one(0)), jnp.concatenate(s_one(0), axis=1)
-    for k in range(nf - 1):
-        e_sums = [a + b.astype(F32) for a, b in zip(e_sums, e_came[k])]
-        s_sum = s_sum + s_came[k].astype(F32)
-    s_sums = [s_sum[:, :fs], s_sum[:, fs : 2 * fs], s_sum[:, 2 * fs :]]
-
     logit_grad = (
         expert_probs * (prob_delta - jnp.sum(expert_probs * prob_delta, axis=-1, keepdims=True))
     ).astype(BF)
@@ -739,6 +760,17 @@
             for x in parts
         )
     t_small = t_small.reshape(PACK)
+    t_small, e_came, s_came, e_gg, e_ug, e_hidden, s_gg, s_ug, s_hidden = lax.optimization_barrier(
+        (t_small, e_came, s_came, e_gg, e_ug, e_hidden, s_gg, s_ug, s_hidden)
+    )
+    e_one = weight_grads(e_rows, e_grads, e_hidden, e_gg, e_ug)
+    s_one = weight_grads(tree_rows, tree_grads, s_hidden, s_gg, s_ug)
+    e_sums, s_sum = list(e_one(0)), jnp.concatenate(s_one(0), axis=1)
+    for k in range(nf - 1):
+        e_sums = [a + b.astype(F32) for a, b in zip(e_sums, e_came[k])]
+        s_sum = s_sum + s_came[k].astype(F32)
+    s_sums = [s_sum[:, :fs], s_sum[:, fs : 2 * fs], s_sum[:, 2 * fs :]]
+
     return (
         output,
         input_grad,

time: 1190 us -> 924 us (0.78)
  Pallas kernels: 596 us -> 459 us
  waiting for transfers between devices: 63 us -> 0.1 us
  matrix products: 330 us -> 280 us
    pallas_call x3, Pallas kernels: 408 us -> 242 us  [ring_gather(): pl.pallas_call(functools.partial(gather_kernel, ring, tuple(wide), tuple(...]
    ppermute x3, waiting for transfers between devices: 62.2 us -> 0.01 us  [body(): e_came.append([lax.ppermute(g.astype(BF), 'fsdp', perm) for g in e_one(k)])]
    dot_general x21 -> x16, matrix products: 116 us -> 71.6 us  [transposed_multiply(): lax.dot_general(left, right, (((0,), (0,)), ((), ())), preferred_element_...]
    dot_general x21 -> x17, matrix products: 100 us -> 70.2 us  [multiply(): return jnp.dot(left, right, preferred_element_type=F32)]
    pallas_call x3, Pallas kernels: 188 us -> 217 us  [ring_reduce(): pl.pallas_call(functools.partial(reduce_kernel, ring, tuple(wide), tuple(...]
    dot_general x1 -> x0, local copies, waits for them, and re-layouts: 17 us -> none  [multiply(): return jnp.dot(left, right, preferred_element_type=F32)]
    dot_general x0 -> x8, matrix products: none -> 14.2 us  [the longest x5 11.4 us: put(): y = jnp.einsum('gst,gsd->gtd', select, x, preferred_element_type=F32)]
    unnamed x247 -> x271, local copies, waits for them, and re-layouts: 30.9 us -> 44.3 us
  transfers between devices with their start and end apart: 12 -> 10, of which waited for: 1 -> 0; matrix products, arithmetic and copies ran while one was open for 37% -> 40% of each run, Pallas kernels for 50% -> 34%
where the time goes in v2:
time: 924 us; the launch traced here: 915 us
  Pallas kernels  459 us (50%)
  matrix products  280 us (30%)
  local copies, waits for them, and re-layouts  114 us (12%)
  other arithmetic  40.1 us (4%)
  between operations  15.9 us (2%)
    pallas_call x3, Pallas kernels, ring_gather(): pl.pallas_call(functools.partial(gather_kernel, ring, tuple(wide), tuple(...  242 us
    pallas_call x3, Pallas kernels, ring_reduce(): pl.pallas_call(functools.partial(reduce_kernel, ring, tuple(wide), tuple(...  217 us
    dot_general x17, matrix products, multiply_transposed(): lax.dot_general(left, right, (((1,), (1,)), ((), ())), preferred_element_...  86 us
    dot_general x16, matrix products, transposed_multiply(): lax.dot_general(left, right, (((0,), (0,)), ((), ())), preferred_element_...  71.6 us
    dot_general x17, matrix products, multiply(): return jnp.dot(left, right, preferred_element_type=F32)  70.2 us
    unnamed x271, local copies, waits for them, and re-layouts  44.3 us
  transfers between devices with their start and end apart: 10, of which 0 were waited for; matrix products, arithmetic and copies ran while one was open for 40% of the time, Pallas kernels for 34%

profile of v2, /device:TPU:0, one launch (start us, length us, event | category | flops | bytes accessed | tf_op | source)
XLA Modules:
  0.0 915.5 jit_solution(8805593326068633937)
XLA Ops:
  17.1 146.7 %ring_gather_0.1 = (bf16[2,16,64,576]{3,2,1,0:T(8,128)(2,1)}, bf16[2,16,64,3072]{3,2,1,0:T(8,128)(2,1)}, bf16[2,16,16,4096]{3,2,1,0:T(8,128)(2,1)}, bf16[2,16,16...) custom-call(bf16[64,576]{1,0:T(8,128)(2,1)} %refs_0_.1, ...), custom_call_target="tpu_custom_call" | custom-call | bytes 55312384 | tf_op jit(solution)/shard_map/ring_gather_0/pallas_call | solution.py:217
  172.4 7.8 fusion.160
  186.6 5.7 copy.256
  208.2 45.9 %ring_gather_1.1 = bf16[2,16,64,576]{3,2,1,0:T(8,128)(2,1)} custom-call(bf16[2,64,576]{2,1,0:T(8,128)(2,1)} %pad_maximum_fusion.8.refs_0_), custom_call_target="tpu_custom_call" | custom-call | bytes 4718592 | tf_op jit(solution)/shard_map/ring_gather_1/pallas_call | solution.py:217
  254.8 4.7 copy.190
  259.6 3.7 fusion.156
  272.3 5.0 multiply_reduce_fusion.7
  281.3 49.3 %ring_gather_2.1 = (bf16[2,16,64,2048]{3,2,1,0:T(8,128)(2,1)}, bf16[2,16,64,128]{3,2,1,0:T(8,128)(2,1)}) custom-call(bf16[2,64,2048]{2,1,0:T(8,128)(2,1)} %bitcast.322, bf16[2,64,128]{2,1,0:T(8,128)(2,1)} %bitcast.343), custom_call_target="tpu_custom_call" | custom-call | bytes 17825792 | tf_op jit(solution)/shard_map/ring_gather_2/pallas_call | solution.py:217
  333.4 4.0 fusion.21
  354.2 5.4 convolution_add_fusion.2
  359.7 7.1 convolution_add_fusion.1
  366.7 4.0 fusion.11
  376.0 5.2 fusion.45
  381.2 12.6 %multiply_convert_fusion.2 = (bf16[1024,1408]{1,0:T(8,128)(2,1)}, bf16[1024,1408]{1,0:T(8,128)(2,1)}, bf16[1024,1408]{1,0:T(8,128)(2,1)}) fusion(f32[1024,1408]{1,0:T(8,128)} %convolution_add_fusion.2, f32[1024,1408]{1,0:T(8,128)} %convolution_add_fusion.1, f32[1024,1408]{1,0:T(8,128)} %fusion.45, bf16[1024,1408]{1,0:T(8,128)(2,1)} %collective-permute-done.1, ...), kind=kOutput, calls=%fused_computation.22 | convolution fusion | flops 2975858688 | bytes 30932992 | tf_op jit(solution)/shard_map/dot_general | solution.py:30
  393.7 5.7 convolution_convert_fusion.11
  420.7 4.6 fusion.163
  425.3 5.6 fusion.115
  432.2 6.0 multiply_reduce_fusion.1
  439.5 4.1 fusion.3
  443.7 5.0 fusion.164
  448.7 5.0 fusion.162
  455.5 7.8 add_convert_fusion.1
  463.3 6.5 add_convert_fusion
  474.4 5.5 fusion.92
  479.9 7.1 fusion.1
  487.0 4.9 fusion
  491.9 69.8 %ring_reduce_3.1 = (f32[2,64,1024]{2,1,0:T(8,128)}, f32[2,64,1024]{2,1,0:T(8,128)}, f32[2,64,128]{2,1,0:T(8,128)}) custom-call(bf16[2,16,64,1024]{3,2,1,0:T(8,128)(2,1)} %bitcast.281, bf16[2,16,64,1024]{3,2,1,0:T(8,128)(2,1)} %bitcast.282, bf16[2,16,64,128]{3,2,1,0:T(8,128)(2,1)} %bitcast.321), custom_call_target="tpu_custom_call" | custom-call | bytes 17825792 | tf_op jit(solution)/shard_map/ring_reduce_3/pallas_call | solution.py:371
  567.0 7.6 convolution_convert_fusion.4
  575.5 4.8 convolution_convert_fusion.6
  581.5 5.0 convolution_convert_fusion.5
  591.3 5.7 convolution_convert_fusion.1
  597.0 6.3 fusion.80
  612.1 3.8 multiply_convert_fusion
  615.9 4.9 broadcast_multiply_fusion
  623.0 5.9 fusion.8
  635.8 39.3 %ring_reduce_4.1 = f32[2,64,576]{2,1,0:T(8,128)} custom-call(bf16[2,16,64,576]{3,2,1,0:T(8,128)(2,1)} %pad_maximum_fusion.2.refs_0_), custom_call_target="tpu_custom_call" | custom-call | bytes 4718592 | tf_op jit(solution)/shard_map/ring_reduce_4/pallas_call | solution.py:371
  678.3 8.0 broadcast_multiply_fusion.1
  686.3 5.8 copy.210
  706.5 9.2 %fusion.165 = f32[128,2048]{1,0:T(8,128)S(1)} fusion(bf16[128,3072]{1,0:T(8,128)(2,1)} %convert_element_type.403, bf16[2048,3072]{1,0:T(8,128)(2,1)} %bitcast.251), kind=kOutput, calls=%fused_computation.298 | convolution fusion | flops 1610612736 | bytes 14417920 | tf_op jit(solution)/shard_map/dot_general | solution.py:34
  718.4 4.0 fusion.58
  730.4 4.3 copy.225
  734.7 7.8 copy.224
  742.6 7.5 convert_element_type.405.refs_1_
  750.1 6.6 convolution_convert_fusion
  756.7 107.6 %ring_reduce_5.1 = (f32[64,3072]{1,0:T(8,128)}, f32[16,4096]{1,0:T(8,128)}, f32[64,576]{1,0:T(8,128)}, f32[16,128]{1,0:T(8,128)}) custom-call(bf16[2,16,64,3072]{3,2,1,0:T(8,128)(2,1)} %bitcast.252, bf16[2,16,16,4096]{3,2,1,0:T(8,128)(2,1)} %convert_element_type.405.refs_1_, bf16[2,16,64,576]{3,2,1,0:T(8,128)(2,1)} %bitcast.287, ...), custom_call_target="tpu_custom_call" | custom-call | bytes 38535168 | tf_op jit(solution)/shard_map/ring_reduce_5/pallas_call | solution.py:371
  884.3 6.8 convert_add_fusion
  891.1 6.8 convert_add_fusion.1
  897.9 6.8 convert_add_fusion.2
  (452 shorter events, 190.6 us)
Async XLA Ops:
  7.2 359.6 %all-gather.2.cloned.1.call-start = ((), (), s32[]{:S(2)}) async-start(), calls=%async_computation.5 | async-start | bytes 8912896 | tf_op jit(solution)/shard_map/all_gather | solution.py:489
  17.1 146.7 %copy-start.54 = (bf16[2,64,2048]{2,1,0:T(8,128)(2,1)S(1)}, bf16[2,64,2048]{2,1,0:T(8,128)(2,1)}, u32[]{:S(2)}) copy-start(bf16[2,64,2048]{2,1,0:T(8,128)(2,1)} %param.20) | copy-start | bytes 1572868
  17.1 151.1 %copy-start.12 = (bf16[2,64,2048]{2,1,0:T(8,128)(2,1)S(1)}, bf16[2,64,2048]{2,1,0:T(8,128)(2,1)}, u32[]{:S(2)}) copy-start(bf16[2,64,2048]{2,1,0:T(8,128)(2,1)} %param.19) | copy-start | bytes 1572868
  164.9 422.5 %reduce-scatter.4.cloned.1.call-start = ((), (), s32[]{:S(2)}) async-start(), calls=%async_computation.3 | async-start | bytes 4456448 | tf_op jit(solution)/shard_map/reduce_scatter | solution.py:659
  165.0 194.7 %collective-permute-start = (bf16[1024,1408]{1,0:T(8,128)(2,1)}, bf16[1024,1408]{1,0:T(8,128)(2,1)}, u32[]{:S(2)}, u32[]{:S(2)}) collective-permute-start(bf16[1024,1408]{1,0:T(8,128)(2,1)} %param.33), channel_id=1, source_target_pairs={{0,16},{16,0},{1,17},{17,1},{2,18},{18,2},{3,19},{19,3},{4,20},{20... | collective-permute-start | bytes 8650760 | tf_op jit(solution)/shard_map/ppermute | solution.py:443
  165.5 215.6 %collective-permute-start.1 = (bf16[1024,1408]{1,0:T(8,128)(2,1)}, bf16[1024,1408]{1,0:T(8,128)(2,1)}, u32[]{:S(2)}, u32[]{:S(2)}) collective-permute-start(bf16[1024,1408]{1,0:T(8,128)(2,1)} %param.34), channel_id=1, source_target_pairs={{0,16},{16,0},{1,17},{17,1},{2,18},{18,2},{3,19},{19,3},{4,20},{20... | collective-permute-start | bytes 8650760 | tf_op jit(solution)/shard_map/ppermute | solution.py:443
  168.0 13.5 %copy-start.69 = (bf16[4,8,16,128]{3,1,2,0:T(8,128)(2,1)}, bf16[4,8,16,128]{3,1,2,0:T(8,128)(2,1)S(1)}, u32[]{:S(2)}) copy-start(bf16[4,8,16,128]{3,1,2,0:T(8,128)(2,1)S(1)} %copy.304) | copy-start | bytes 393220
  172.3 34.9 %copy-start.30 = (f32[128,576]{0,1:T(8,128)}, f32[128,576]{0,1:T(8,128)S(1)}, u32[]{:S(2)}) copy-start(f32[128,576]{0,1:T(8,128)S(1)} %fusion.161) | copy-start | bytes 884740
  172.4 9.9 %copy-start.68 = (bf16[2,16,16,128]{3,2,1,0:T(8,128)(2,1)S(1)}, bf16[2,16,16,128]{3,2,1,0:T(8,128)(2,1)}, u32[]{:S(2)}) copy-start(bf16[2,16,16,128]{3,2,1,0:T(8,128)(2,1)} %get-tuple-element.49) | copy-start | bytes 393220
  172.4 10.7 %copy-start.86 = (s32[2,13,13]{2,0,1:T(2,128)S(1)}, s32[2,13,13]{2,0,1:T(2,128)}, u32[]{:S(2)}) copy-start(s32[2,13,13]{2,0,1:T(2,128)} %param.22) | copy-start | bytes 4060
  201.1 69.1 %copy-start.7 = (bf16[512,16,128]{2,1,0:T(8,128)(2,1)}, bf16[512,16,128]{2,1,0:T(8,128)(2,1)S(1)}, u32[]{:S(2)}) copy-start(bf16[512,16,128]{2,1,0:T(8,128)(2,1)S(1)} %get-tuple-element.152) | copy-start | bytes 6291460
  206.3 47.9 %copy-start.67 = (pred[2,64,1024]{2,1,0:T(8,128)(4,1)S(1)}, pred[2,64,1024]{2,1,0:T(8,128)(4,1)}, u32[]{:S(2)}) copy-start(pred[2,64,1024]{2,1,0:T(8,128)(4,1)} %get-tuple-element.146) | copy-start | bytes 393220
  207.1 47.7 %copy-start.83 = (f32[512]{0:T(512)}, f32[512]{0:T(512)S(1)}, u32[]{:S(2)}) copy-start(f32[512]{0:T(512)S(1)} %reshape.584) | copy-start | bytes 6148
  207.2 47.6 %copy-start.95 = (f32[128]{0:T(128)}, f32[128]{0:T(128)S(1)}, u32[]{:S(2)}) copy-start(f32[128]{0:T(128)S(1)} %add_rsqrt_fusion.2) | copy-start | bytes 1540
  277.3 54.5 %copy-start.70 = (bf16[2,16,2048]{2,1,0:T(8,128)(2,1)S(1)}, bf16[2,16,2048]{2,1,0:T(8,128)(2,1)}, u32[]{:S(2)}) copy-start(bf16[2,16,2048]{2,1,0:T(8,128)(2,1)} %reshape_reshape.13) | copy-start | bytes 393220
  278.5 58.9 %copy-start.27 = (bf16[128,2048]{1,0:T(8,128)(2,1)}, bf16[128,2048]{1,0:T(8,128)(2,1)S(1)}, u32[]{:S(2)}) copy-start(bf16[128,2048]{1,0:T(8,128)(2,1)S(1)} %multiply_convert_fusion.9) | copy-start | bytes 1572868
  278.5 54.9 %copy-start.56 = (bf16[1024,528]{1,0:T(8,128)(2,1)S(1)}, bf16[1024,528]{1,0:T(8,128)(2,1)}, u32[]{:S(2)}) copy-start(bf16[1024,528]{1,0:T(8,128)(2,1)} %get-tuple-element.58) | copy-start | bytes 3244036
  278.8 53.0 %copy-start.73 = (f32[128,16]{0,1:T(8,128)}, f32[128,16]{0,1:T(8,128)S(1)}, u32[]{:S(2)}) copy-start(f32[128,16]{0,1:T(8,128)S(1)} %get-tuple-element.193) | copy-start | bytes 24580
  278.8 53.0 %copy-start.87 = (f32[128]{0:T(128)}, f32[128]{0:T(128)S(1)}, u32[]{:S(2)}) copy-start(f32[128]{0:T(128)S(1)} %get-tuple-element.192) | copy-start | bytes 1540
  343.6 16.1 %copy-start.18 = (bf16[8,128,2048]{2,1,0:T(8,128)(2,1)}, bf16[8,128,2048]{2,1,0:T(8,128)(2,1)S(1)}, u32[]{:S(2)}) copy-start(bf16[8,128,2048]{2,1,0:T(8,128)(2,1)S(1)} %convolution_convert_fusion.3) | copy-start | bytes 12582916
  404.2 8.0 copy-start.42
  404.2 21.1 %copy-start.32 = (bf16[2048,176]{0,1:T(8,128)(2,1)}, bf16[2048,176]{0,1:T(8,128)(2,1)S(1)}, u32[]{:S(2)}) copy-start(bf16[2048,176]{0,1:T(8,128)(2,1)S(1)} %get-tuple-element.74) | copy-start | bytes 2162692
  404.2 35.3 %copy-start.46 = (bf16[2048,176]{0,1:T(8,128)(2,1)}, bf16[2048,176]{0,1:T(8,128)(2,1)S(1)}, u32[]{:S(2)}) copy-start(bf16[2048,176]{0,1:T(8,128)(2,1)S(1)} %get-tuple-element.76) | copy-start | bytes 2162692
  407.9 179.6 %reduce-scatter.6.cloned.1.call-start = ((), (), s32[]{:S(2)}) async-start(), calls=%async_computation.4 | async-start | bytes 4456448 | tf_op jit(solution)/shard_map/reduce_scatter | solution.py:659
  419.9 444.5 %collective-permute-start.5 = (bf16[1024,528]{0,1:T(8,128)(2,1)}, bf16[1024,528]{0,1:T(8,128)(2,1)}, u32[]{:S(2)}, u32[]{:S(2)}) collective-permute-start(bf16[1024,528]{0,1:T(8,128)(2,1)} %pad_maximum_fusion.4), channel_id=1, source_target_pairs={{0,16},{16,0},{1,17},{17,1},{2,18},{18,2},{3,19},{19,3},{4,20},{20... | collective-permute-start | bytes 3244040 | tf_op jit(solution)/shard_map/ppermute | solution.py:673
  453.7 451.1 %reduce-scatter.8.cloned.1.call-start = ((), (), s32[]{:S(2)}) async-start(), calls=%async_computation.6 | async-start | bytes 8650752 | tf_op jit(solution)/shard_map/reduce_scatter | solution.py:684
  471.3 8.6 slice-start.4
  474.4 12.6 %slice-start.2 = ((s8[8388608]{0:T(1024)(128)(4,1)}), s8[4194304]{0:T(1024)(128)(4,1)S(1)}, s32[]{:S(2)}) async-start(s8[8388608]{0:T(1024)(128)(4,1)} %bitcast.255), calls=%async_computation.9 | async-start | bytes 8388608
  491.9 70.9 %copy-start.74 = (f32[128,16]{0,1:T(8,128)S(1)}, f32[128,16]{0,1:T(8,128)}, u32[]{:S(2)}) copy-start(f32[128,16]{0,1:T(8,128)} %copy-done.73) | copy-start | bytes 24580
  491.9 70.9 %copy-start.88 = (f32[128]{0:T(128)S(1)}, f32[128]{0:T(128)}, u32[]{:S(2)}) copy-start(f32[128]{0:T(128)} %copy-done.87) | copy-start | bytes 1540
  491.9 70.9 %copy-start.92 = (f32[128]{0:T(128)S(1)}, f32[128]{0:T(128)}, u32[]{:S(2)}) copy-start(f32[128]{0:T(128)} %copy-done.91) | copy-start | bytes 1540
  491.9 71.0 %copy-start.28 = (bf16[128,2048]{1,0:T(8,128)(2,1)S(1)}, bf16[128,2048]{1,0:T(8,128)(2,1)}, u32[]{:S(2)}) copy-start(bf16[128,2048]{1,0:T(8,128)(2,1)} %copy-done.27) | copy-start | bytes 1572868
  567.0 8.4 copy-start.19
  567.0 8.4 copy-start.113
  574.7 289.7 %collective-permute-start.4 = (bf16[1024,1408]{1,0:T(8,128)(2,1)}, bf16[1024,1408]{1,0:T(8,128)(2,1)}, u32[]{:S(2)}, u32[]{:S(2)}) collective-permute-start(bf16[1024,1408]{1,0:T(8,128)(2,1)} %convolution_convert_fusion.4), channel_id=1, source_target_pairs={{0,16},{16,0},{1,17},{17,1},{2,18},{18,2},{3,19},{19,3},{4,20},{20... | collective-permute-start | bytes 8650760 | tf_op jit(solution)/shard_map/ppermute | solution.py:671
  580.3 284.1 %collective-permute-start.2 = (bf16[1024,1408]{1,0:T(8,128)(2,1)}, bf16[1024,1408]{1,0:T(8,128)(2,1)}, u32[]{:S(2)}, u32[]{:S(2)}) collective-permute-start(bf16[1024,1408]{1,0:T(8,128)(2,1)} %convolution_convert_fusion.6), channel_id=1, source_target_pairs={{0,16},{16,0},{1,17},{17,1},{2,18},{18,2},{3,19},{19,3},{4,20},{20... | collective-permute-start | bytes 8650760 | tf_op jit(solution)/shard_map/ppermute | solution.py:671
  586.5 277.9 %collective-permute-start.3 = (bf16[1024,1408]{1,0:T(8,128)(2,1)}, bf16[1024,1408]{1,0:T(8,128)(2,1)}, u32[]{:S(2)}, u32[]{:S(2)}) collective-permute-start(bf16[1024,1408]{1,0:T(8,128)(2,1)} %convolution_convert_fusion.5), channel_id=1, source_target_pairs={{0,16},{16,0},{1,17},{17,1},{2,18},{18,2},{3,19},{19,3},{4,20},{20... | collective-permute-start | bytes 8650760 | tf_op jit(solution)/shard_map/ppermute | solution.py:671
  635.8 41.1 %copy-start.90 = (f32[2,64]{1,0:T(2,128)S(1)}, f32[2,64]{1,0:T(2,128)}, u32[]{:S(2)}) copy-start(f32[2,64]{1,0:T(2,128)} %copy-done.89) | copy-start | bytes 1540
  635.8 41.1 %copy-start.99 = (f32[32]{0:T(128)S(1)}, f32[32]{0:T(128)}, u32[]{:S(2)}) copy-start(f32[32]{0:T(128)} %negate_power_fusion) | copy-start | bytes 388
  706.4 9.3 %copy-start.50 = (f32[128,512]{0,1:T(8,128)S(1)}, f32[128,512]{0,1:T(8,128)}, u32[]{:S(2)}) copy-start(f32[128,512]{0,1:T(8,128)} %copy.220) | copy-start | bytes 786436
  706.4 9.5 %copy-start.13 = (bf16[2,64,2048]{2,1,0:T(8,128)(2,1)S(1)}, bf16[2,64,2048]{2,1,0:T(8,128)(2,1)}, u32[]{:S(2)}) copy-start(bf16[2,64,2048]{2,1,0:T(8,128)(2,1)} %param.19) | copy-start | bytes 1572868
  706.4 9.5 %copy-start.17 = (bf16[2,16,64,576]{3,2,1,0:T(8,128)(2,1)S(1)}, bf16[2,16,64,576]{3,2,1,0:T(8,128)(2,1)}, u32[]{:S(2)}) copy-start(bf16[2,16,64,576]{3,2,1,0:T(8,128)(2,1)} %get-tuple-element.51) | copy-start | bytes 7077892
  706.5 9.5 %copy-start.77 = (f32[2048]{0:T(1024)S(1)}, f32[2048]{0:T(1024)}, u32[]{:S(2)}) copy-start(f32[2048]{0:T(1024)} %copy-done.76) | copy-start | bytes 24580
  706.5 9.5 %copy-start.100 = (f32[128]{0:T(128)S(1)}, f32[128]{0:T(128)}, u32[]{:S(2)}) copy-start(f32[128]{0:T(128)} %rsqrt.31) | copy-start | bytes 1540
  756.7 111.7 %copy-start.33 = (bf16[2048,176]{0,1:T(8,128)(2,1)S(1)}, bf16[2048,176]{0,1:T(8,128)(2,1)}, u32[]{:S(2)}) copy-start(bf16[2048,176]{0,1:T(8,128)(2,1)} %copy-done.32) | copy-start | bytes 2162692
  897.9 8.6 copy-start.64
  897.9 9.4 %copy-start.75 = (f32[64,576]{1,0:T(8,128)S(1)}, f32[64,576]{1,0:T(8,128)}, u32[]{:S(2)}) copy-start(f32[64,576]{1,0:T(8,128)} %get-tuple-element.219) | copy-start | bytes 442372
  897.9 10.1 %copy-start.72 = (f32[16,4096]{1,0:T(8,128)S(1)}, f32[16,4096]{1,0:T(8,128)}, u32[]{:S(2)}) copy-start(f32[16,4096]{1,0:T(8,128)} %get-tuple-element.221) | copy-start | bytes 786436
  (88 other events, 325.4 us)
Sparse Core Ops, SparseCore 0:
  165.0 76.8 all-gather.1
  408.0 71.6 reduce-scatter.3
  484.6 81.4 reduce-scatter.5
  597.1 152.1 reduce-scatter.7

commit v3 on v2

--- a/solution.py
+++ b/solution.py
@@ -391,6 +391,182 @@
     )(*arrays)
 
 
+def expert_kernel(nf, experts, fp, bundle_slots, *refs):
+    x_ref, g_ref, probs_ref, slot_ref, column_ref = refs[:5]
+    weights, refs = refs[5 : 5 + 4 * nf], refs[5 + 4 * nf :]
+    back_ref, out_ref, delta_ref, rows_ref, grads_ref, hid_ref, gg_ref, ug_ref, act_ref = refs[:9]
+    w_gate, w_up, w_down, w_shared, pre_gate, pre_up, pre_in, pre_s, raw, sems = refs[9:]
+    mine = lax.axis_index("ctx")
+    held = (w_gate, w_up, w_down, w_shared)
+    part = w_gate.shape[0] // nf
+    wide = w_gate.shape[0]
+    copies = [
+        [
+            pltpu.make_async_copy(
+                weights[4 * k + i], held[i].at[pl.ds(k * part, part)], sems.at[i, k]
+            )
+            for k in range(nf)
+        ]
+        for i in range(4)
+    ]
+    first = pl.program_id(0) == 0
+
+    def ready(i):
+        @pl.when(first)
+        def _():
+            for cp in copies[i]:
+                cp.wait()
+
+    @pl.when(first)
+    def _():
+        for i in (3, 0, 1, 2):
+            for cp in copies[i]:
+                cp.start()
+
+    def nt(left, right):
+        return lax.dot_general(left, right, (((1,), (1,)), ((), ())), preferred_element_type=F32)
+
+    bundles, _, rows = slot_ref.shape
+    lane = lax.broadcasted_iota(jnp.int32, (rows, 128), 1)
+    own_lane = (lane % experts == mine) & (lane < 3 * experts)
+    puts, row_gates = [], []
+    for b in range(bundles):
+        cut, spot = pl.ds(b * rows, rows), pl.ds(b * bundle_slots, bundle_slots)
+        takes = (
+            slot_ref[b] == lax.broadcasted_iota(jnp.int32, (bundle_slots, rows), 0)
+        ).astype(F32).astype(BF)
+        puts.append(
+            (
+                column_ref[cut, :] == lax.broadcasted_iota(jnp.int32, (rows, bundle_slots), 1)
+            ).astype(F32).astype(BF)
+        )
+        own = jnp.where(own_lane, probs_ref[cut, :].astype(F32), 0.0)
+        row_gates.append(jnp.sum(own, axis=1, keepdims=True))
+        gate = jnp.sum(multiply(takes, own.astype(BF)), axis=1, keepdims=True)
+        for start in range(0, wide, 512):
+            piece = pl.ds(start, 512)
+            rows_ref[spot, piece] = multiply(takes, x_ref[cut, piece]).astype(BF)
+            taken = multiply(takes, g_ref[cut, piece])
+            raw[spot, piece] = taken.astype(BF)
+            grads_ref[spot, piece] = (gate * taken).astype(BF)
+
+    ready(3)
+    pre_s[:, : 2 * fp] = multiply(x_ref[...], w_shared[:, : 2 * fp])
+    pre_s[:, 2 * fp :] = multiply(g_ref[...], w_shared[:, 2 * fp :])
+
+    def activate(gate_pre, up_pre, inner):
+        sig = jax.nn.sigmoid(gate_pre)
+        activated = gate_pre * sig
+        hidden = activated * up_pre
+        gate_grad = inner * up_pre * sig * (1.0 + gate_pre * (1.0 - sig))
+        return hidden.astype(BF), gate_grad.astype(BF), (inner * activated).astype(BF)
+
+    step = 32
+
+    def shared_rows(r, carry):
+        at = pl.ds(pl.multiple_of(r * step, step), step)
+        for start in range(0, fp, 128):
+            cuts = [pl.ds(i * fp + start, 128) for i in range(3)]
+            hidden, gate_grad, up_grad = activate(*(pre_s[at, c] for c in cuts))
+            act_ref[at, cuts[0]] = gate_grad
+            act_ref[at, cuts[1]] = up_grad
+            act_ref[at, cuts[2]] = hidden
+        return carry
+
+    lax.fori_loop(0, pre_s.shape[0] // step, shared_rows, 0)
+
+    ready(0)
+    pre_gate[...] = multiply(rows_ref[...], w_gate[...])
+    ready(1)
+    pre_up[...] = multiply(rows_ref[...], w_up[...])
+    ready(2)
+    pre_in[...] = multiply(grads_ref[...], w_down[...])
+
+    def expert_rows(r, carry):
+        at = pl.ds(pl.multiple_of(r * step, step), step)
+        for start in range(0, hid_ref.shape[1], 128):
+            c = pl.ds(start, 128)
+            hidden, gate_grad, up_grad = activate(pre_gate[at, c], pre_up[at, c], pre_in[at, c])
+            hid_ref[at, c] = hidden
+            gg_ref[at, c] = gate_grad
+            ug_ref[at, c] = up_grad
+        return carry
+
+    lax.fori_loop(0, hid_ref.shape[0] // step, expert_rows, 0)
+
+    delta = 0.0
+    for start in range(0, wide, 512):
+        piece = pl.ds(start, 512)
+        e_back = nt(gg_ref[...], w_gate[piece, :]) + nt(ug_ref[...], w_up[piece, :])
+        e_back = e_back.astype(BF)
+        e_out = nt(hid_ref[...], w_down[piece, :]).astype(BF)
+        delta = delta + jnp.sum(
+            raw[:, piece].astype(F32) * e_out.astype(F32), axis=1, keepdims=True
+        )
+        for b in range(bundles):
+            cut = pl.ds(b * rows, rows)
+            spot = slice(b * bundle_slots, (b + 1) * bundle_slots)
+            s_back = nt(act_ref[cut, : 2 * fp], w_shared[piece, : 2 * fp])
+            back_ref[cut, piece] = (multiply(puts[b], e_back[spot]) + s_back).astype(BF)
+            s_out = nt(act_ref[cut, 2 * fp :], w_shared[piece, 2 * fp :])
+            out_ref[cut, piece] = (row_gates[b] * multiply(puts[b], e_out[spot]) + s_out).astype(BF)
+    for b in range(bundles):
+        own = delta[b * bundle_slots : (b + 1) * bundle_slots]
+        high = own.astype(BF).astype(F32)
+        middle = (own - high).astype(BF).astype(F32)
+        low = own - high - middle
+        spread = jnp.where(lane[:bundle_slots] < experts, high, jnp.where(lane[:bundle_slots] < 2 * experts, middle, low))
+        spread = jnp.where(own_lane[:bundle_slots], spread, 0.0).astype(BF)
+        delta_ref[pl.ds(b * rows, rows), :] = multiply(puts[b], spread).astype(BF)
+
+
+def run_experts(nf, experts, capacity, tok_loc, tree_rows, tree_grads, tree_probs, slot, weights):
+    rows, wide = tree_rows.shape
+    bundles, per = slot.shape
+    bundle_slots = capacity * (per // tok_loc)
+    hidden, fp = weights[0][0].shape[1], weights[0][3].shape[1] // 3
+    group = 2 if bundles % 2 == 0 else 1
+    steps = bundles // group
+    block, slots = rows // steps, group * bundle_slots
+    flat = [w for piece in weights for w in piece]
+    by_row = lambda width: pl.BlockSpec((block, width), lambda i: (i, 0))
+    by_slot = lambda width: pl.BlockSpec((slots, width), lambda i: (i, 0))
+    any_spec = pl.BlockSpec(memory_space=pl.ANY)
+    shape = lambda n, width: jax.ShapeDtypeStruct((n, width), BF)
+    total = steps * slots
+    flops = 2 * (6 * total * wide * hidden + 6 * rows * wide * fp + 4 * rows * bundle_slots * wide)
+    return pl.pallas_call(
+        functools.partial(expert_kernel, nf, experts, fp, bundle_slots),
+        grid=(steps,),
+        out_shape=[shape(rows, wide), shape(rows, wide), shape(rows, 128)]
+        + [shape(total, wide)] * 2
+        + [shape(total, hidden)] * 3
+        + [shape(rows, 3 * fp)],
+        in_specs=[
+            by_row(wide),
+            by_row(wide),
+            by_row(128),
+            pl.BlockSpec((group, 1, per), lambda i: (i, 0, 0)),
+            pl.BlockSpec((block, 1), lambda i: (i, 0)),
+        ]
+        + [any_spec] * len(flat),
+        out_specs=[by_row(wide), by_row(wide), by_row(128)]
+        + [by_slot(wide)] * 2
+        + [by_slot(hidden)] * 3
+        + [by_row(3 * fp)],
+        scratch_shapes=[pltpu.VMEM((wide, hidden), BF)] * 3
+        + [pltpu.VMEM((wide, 3 * fp), BF)]
+        + [pltpu.VMEM((slots, hidden), F32)] * 3
+        + [pltpu.VMEM((block, 3 * fp), F32), pltpu.VMEM((slots, wide), BF)]
+        + [pltpu.SemaphoreType.DMA((4, nf))],
+        compiler_params=pltpu.CompilerParams(vmem_limit_bytes=61 << 20),
+        cost_estimate=pl.CostEstimate(
+            flops=flops, bytes_accessed=10 * rows * wide, transcendentals=total * hidden
+        ),
+        name="experts",
+    )(tree_rows, tree_grads, tree_probs, slot[:, None, :], slot.reshape(rows, 1), *flat)
+
+
 def body(
     tokens,
     out_grad,
@@ -443,8 +619,11 @@
             pieces.append(lax.ppermute(w, "fsdp", [(i, (i - k) % nf) for i in range(nf)]))
         return pieces
 
-    shared_w = jnp.concatenate([shared_gate, shared_up, shared_down], axis=1)
     fs = shared_gate.shape[1]
+    fp = -(-fs // 128) * 128
+    shared_w = jnp.concatenate(
+        [jnp.pad(w, ((0, 0), (0, fp - fs))) for w in (shared_gate, shared_up, shared_down)], axis=1
+    )
     small = jnp.concatenate(
         [
             norm_attn,
@@ -565,113 +744,51 @@
     slot = multiply(grid, upper).astype(jnp.int32) - 1
     slot = slot + (jnp.arange(blocks, dtype=jnp.int32) % bundle * capacity)[:, None]
     slot = jnp.where(grid > 0, slot, -1).reshape(bundles, bundle * tok_loc)
-    spots = jnp.arange(bundle * capacity, dtype=jnp.int32)
-    select = (slot[:, None, :] == spots[None, :, None]).astype(BF)
-
-    def take(x):
-        x = x.reshape(bundles, bundle * tok_loc, x.shape[-1])
-        y = jnp.einsum("gst,gtd->gsd", select, x, preferred_element_type=F32)
-        return y.reshape(slot_total, x.shape[-1])
-
-    def put(x):
-        x = x.reshape(bundles, bundle * capacity, x.shape[-1])
-        y = jnp.einsum("gst,gsd->gtd", select, x, preferred_element_type=F32)
-        return y.reshape(group_rows, x.shape[-1])
-
-    is_mine = labels[None, :] == mine
-    own_parts = jnp.sum(
-        jnp.where(
-            is_mine[:, None, :], tree_probs[:, : 3 * experts].reshape(group_rows, 3, experts), 0
-        ).astype(F32),
-        axis=-1,
-    )
-    row_gate = jnp.sum(own_parts, axis=-1)
-    slot_gate = jnp.sum(take(own_parts.astype(BF)), axis=-1)
-
-    e_rows = take(tree_rows).astype(BF)
-    e_raw = take(tree_grads).astype(BF)
-    e_grads = (slot_gate[:, None] * e_raw.astype(F32)).astype(BF)
-
-    def into(rows, pieces):
-        total = multiply(rows[:, :part], pieces[0])
-        for k in range(1, nf):
-            total = total + multiply(rows[:, k * part : (k + 1) * part], pieces[k])
-        return total
-
-    def feed_forward(rows, grads, gate, up, down):
-        gate_pre, up_pre = into(rows, gate), into(rows, up)
-        sigmoid_gate = jax.nn.sigmoid(gate_pre)
-        activated = gate_pre * sigmoid_gate
-        hidden_act = (activated * up_pre).astype(BF)
-        inner_grad = into(grads, down)
-        gate_grad = (
-            inner_grad * up_pre * sigmoid_gate * (1.0 + gate_pre * (1.0 - sigmoid_gate))
-        ).astype(BF)
-        up_grad = (inner_grad * activated).astype(BF)
-        return hidden_act, gate_grad, up_grad
-
-    def weight_grads(rows, grads, hidden_act, gate_grad, up_grad):
-        def one(k):
-            cut = slice(k * part, (k + 1) * part)
-            return (
-                transposed_multiply(rows[:, cut], gate_grad),
-                transposed_multiply(rows[:, cut], up_grad),
-                transposed_multiply(grads[:, cut], hidden_act),
-            )
-
-        return one
-
-    s_gate = [w[:, :fs] for w in s_all]
-    s_up = [w[:, fs : 2 * fs] for w in s_all]
-    s_down = [w[:, 2 * fs :] for w in s_all]
-
-    e_hidden, e_gg, e_ug = feed_forward(e_rows, e_grads, e_gate, e_up, e_down)
-    s_hidden, s_gg, s_ug = feed_forward(tree_rows, tree_grads, s_gate, s_up, s_down)
-
-    back_parts, out_parts, slot_delta = [], [], 0.0
-    for k in range(nf):
+    back, out_part, delta_out, e_rows, e_grads, e_hidden, e_gg, e_ug, s_act = run_experts(
+        nf,
+        experts,
+        capacity,
+        tok_loc,
+        tree_rows,
+        tree_grads,
+        tree_probs,
+        slot,
+        list(zip(e_gate, e_up, e_down, s_all)),
+    )
+
+    def weight_grads(k, e_gg, e_ug, e_hidden, s_act):
         cut = slice(k * part, (k + 1) * part)
-        e_back = (multiply_transposed(e_gg, e_gate[k]) + multiply_transposed(e_ug, e_up[k])).astype(BF)
-        s_back = multiply_transposed(s_gg, s_gate[k]) + multiply_transposed(s_ug, s_up[k])
-        back_parts.append((put(e_back) + s_back).astype(BF))
-        e_out = multiply_transposed(e_hidden, e_down[k]).astype(BF)
-        slot_delta = slot_delta + jnp.sum(
-            e_raw[:, cut].astype(F32) * e_out.astype(F32), axis=-1
+        return (
+            transposed_multiply(e_rows[:, cut], e_gg),
+            transposed_multiply(e_rows[:, cut], e_ug),
+            transposed_multiply(e_grads[:, cut], e_hidden),
+            transposed_multiply(tree_rows[:, cut], s_act[:, : 2 * fp]),
+            transposed_multiply(tree_grads[:, cut], s_act[:, 2 * fp :]),
         )
-        s_out = multiply_transposed(s_hidden, s_down[k])
-        out_parts.append((row_gate[:, None] * put(e_out) + s_out).astype(BF))
-    delta_parts = jnp.stack(three_parts(slot_delta), axis=-1)
-    row_delta = put(delta_parts).astype(BF)
-    delta_out = jnp.where(is_mine[:, None, :], row_delta[:, :, None], 0).reshape(group_rows, 3 * experts)
-    delta_out = jnp.pad(delta_out, ((0, 0), (0, 128 - 3 * experts)))
 
     def by_owner(x):
         return x.reshape(trees, nc, tok_loc, x.shape[-1])
 
-    sums = ring_reduce(
-        ring, 3, [by_owner(x) for x in back_parts] + [by_owner(delta_out)], [False] * (nf + 1)
-    )
-    back_sum = roll_out(jnp.concatenate(sums[:nf], axis=-1).reshape(row_total, D))
+    back_sum, delta_sum = ring_reduce(
+        ring, 3, [by_owner(back), by_owner(delta_out)], [False] * 2
+    )
+    back_sum, out_part = lax.optimization_barrier((back_sum, out_part))
+    back_sum = roll_out(back_sum.reshape(row_total, D))
     prob_delta = jnp.sum(
-        sums[nf].reshape(row_total, 128)[:, : 3 * experts].reshape(row_total, 3, experts), axis=1
-    )
-    out_sum = [
-        lax.psum_scatter(x.reshape(trees, tree_len, part), "ctx", scatter_dimension=1, tiled=True)
-        for x in out_parts
-    ]
-    out_sum = jnp.concatenate(out_sum, axis=-1).reshape(row_total, D).astype(F32)
-    out_sum = roll_out(out_sum)
+        delta_sum.reshape(row_total, 128)[:, : 3 * experts].reshape(row_total, 3, experts), axis=1
+    )
+    out_sum = lax.psum_scatter(
+        out_part.reshape(trees, tree_len, D), "ctx", scatter_dimension=1, tiled=True
+    )
+    out_sum = roll_out(out_sum.reshape(row_total, D).astype(F32))
     output = (residual + out_sum).astype(BF).reshape(trees, tok_loc, D)
 
-    e_one = weight_grads(e_rows, e_grads, e_hidden, e_gg, e_ug)
-    s_one = weight_grads(tree_rows, tree_grads, s_hidden, s_gg, s_ug)
-    e_came, s_came = [], []
+    came = []
     for k in range(1, nf):
         perm = [(i, (i + k) % nf) for i in range(nf)]
-        e_came.append([lax.ppermute(g.astype(BF), "fsdp", perm) for g in e_one(k)])
-        s_came.append(
-            lax.ppermute(jnp.concatenate(s_one(k), axis=1).astype(BF), "fsdp", perm)
-        )
+        grads = weight_grads(k, e_gg, e_ug, e_hidden, s_act)
+        came.append([lax.ppermute(g.astype(BF), "fsdp", perm) for g in grads])
+
     logit_grad = (
         expert_probs * (prob_delta - jnp.sum(expert_probs * prob_delta, axis=-1, keepdims=True))
     ).astype(BF)
@@ -760,17 +877,14 @@
             for x in parts
         )
     t_small = t_small.reshape(PACK)
-    t_small, e_came, s_came, e_gg, e_ug, e_hidden, s_gg, s_ug, s_hidden = lax.optimization_barrier(
-        (t_small, e_came, s_came, e_gg, e_ug, e_hidden, s_gg, s_ug, s_hidden)
-    )
-    e_one = weight_grads(e_rows, e_grads, e_hidden, e_gg, e_ug)
-    s_one = weight_grads(tree_rows, tree_grads, s_hidden, s_gg, s_ug)
-    e_sums, s_sum = list(e_one(0)), jnp.concatenate(s_one(0), axis=1)
-    for k in range(nf - 1):
-        e_sums = [a + b.astype(F32) for a, b in zip(e_sums, e_came[k])]
-        s_sum = s_sum + s_came[k].astype(F32)
-    s_sums = [s_sum[:, :fs], s_sum[:, fs : 2 * fs], s_sum[:, 2 * fs :]]
-
+    t_small, came, e_gg, e_ug, e_hidden, s_act = lax.optimization_barrier(
+        (t_small, came, e_gg, e_ug, e_hidden, s_act)
+    )
+    ffn_sums = list(weight_grads(0, e_gg, e_ug, e_hidden, s_act))
+    for one in came:
+        ffn_sums = [a + b.astype(F32) for a, b in zip(ffn_sums, one)]
+    e_sums = ffn_sums[:3]
+    s_sums = [ffn_sums[3][:, :fs], ffn_sums[3][:, fp : fp + fs], ffn_sums[4][:, :fs]]
     return (
         output,
         input_grad,

time: 924 us -> 904 us (0.978)
  matrix products: 280 us -> 152 us
  waiting for transfers between devices: 0.1 us -> 65.4 us
  Pallas kernels: 459 us -> 522 us
  local copies, waits for them, and re-layouts: 114 us -> 102 us
    pallas_call x0 -> x1, Pallas kernels: none -> 79.1 us  [run_experts(): pl.pallas_call(functools.partial(expert_kernel, nf, experts, fp, bundle_s...]
    reduce_scatter x2 -> x1, waiting for transfers between devices: 0.01 us -> 65.4 us  [body(): lax.psum_scatter(out_part.reshape(trees, tree_len, D), 'ctx', scatter_dim...]
    dot_general x17 -> x5, matrix products: 86 us -> 23.2 us  [multiply_transposed(): lax.dot_general(left, right, (((1,), (1,)), ((), ())), preferred_element_...]
    dot_general x17 -> x5, matrix products: 70.2 us -> 14.8 us  [multiply(): return jnp.dot(left, right, preferred_element_type=F32)]
    pallas_call x3, Pallas kernels: 217 us -> 193 us  [ring_reduce(): pl.pallas_call(functools.partial(reduce_kernel, ring, tuple(wide), tuple(...]
    dot_general x8 -> x0, matrix products: 14.2 us -> none  [the longest x5 11.4 us: put(): y = jnp.einsum('gst,gsd->gtd', select, x, preferred_element_type=F32)]
    unnamed x271 -> x158, local copies, waits for them, and re-layouts: 44.3 us -> 31.3 us
    dot_general x16 -> x14, matrix products: 71.6 us -> 72.3 us  [transposed_multiply(): lax.dot_general(left, right, (((0,), (0,)), ((), ())), preferred_element_...]
  transfers between devices with their start and end apart: 10 -> 10, of which waited for: 0 -> 1; matrix products, arithmetic and copies ran while one was open for 40% -> 29% of each run, Pallas kernels for 34% -> 28%
where the time goes in v3:
time: 904 us; the launch traced here: 897 us
  Pallas kernels  522 us (58%)
  matrix products  152 us (17%)
  local copies, waits for them, and re-layouts  102 us (11%)
  waiting for transfers between devices  65.4 us (7%)
  other arithmetic  32.9 us (4%)
  between operations  15.3 us (2%)
    pallas_call x3, Pallas kernels, ring_gather(): pl.pallas_call(functools.partial(gather_kernel, ring, tuple(wide), tuple(...  250 us
    pallas_call x3, Pallas kernels, ring_reduce(): pl.pallas_call(functools.partial(reduce_kernel, ring, tuple(wide), tuple(...  193 us
    pallas_call x1, Pallas kernels, run_experts(): pl.pallas_call(functools.partial(expert_kernel, nf, experts, fp, bundle_s...  79.1 us
    dot_general x14, matrix products, transposed_multiply(): lax.dot_general(left, right, (((0,), (0,)), ((), ())), preferred_element_...  72.3 us
    reduce_scatter x1, waiting for transfers between devices, body(): lax.psum_scatter(out_part.reshape(trees, tree_len, D), 'ctx', scatter_dim...  65.4 us
    unnamed x158, local copies, waits for them, and re-layouts  31.3 us
    dot_general x5, matrix products, multiply_transposed(): lax.dot_general(left, right, (((1,), (1,)), ((), ())), preferred_element_...  23.2 us
  transfers between devices with their start and end apart: 10, of which 1 were waited for; matrix products, arithmetic and copies ran while one was open for 29% of the time, Pallas kernels for 28%

profile of v3, /device:TPU:0, one launch (start us, length us, event | category | flops | bytes accessed | tf_op | source)
XLA Modules:
  0.0 896.9 jit_solution(1807571787390580584)
XLA Ops:
  16.7 146.7 %ring_gather_0.1 = (bf16[2,16,64,576]{3,2,1,0:T(8,128)(2,1)}, bf16[2,16,64,3072]{3,2,1,0:T(8,128)(2,1)}, bf16[2,16,16,4096]{3,2,1,0:T(8,128)(2,1)}, bf16[2,16,16...) custom-call(bf16[64,576]{1,0:T(8,128)(2,1)} %refs_0_.1, ...), custom_call_target="tpu_custom_call" | custom-call | bytes 55312384 | tf_op jit(solution)/shard_map/ring_gather_0/pallas_call | solution.py:217
  168.3 3.9 copy.136
  172.3 3.4 copy.196
  177.3 3.0 fusion.111
  180.8 6.4 fusion.110
  193.8 54.8 %ring_gather_1.1 = bf16[2,16,64,576]{3,2,1,0:T(8,128)(2,1)} custom-call(bf16[2,64,576]{2,1,0:T(8,128)(2,1)} %pad_maximum_fusion.4.refs_0_), custom_call_target="tpu_custom_call" | custom-call | bytes 4718592 | tf_op jit(solution)/shard_map/ring_gather_1/pallas_call | solution.py:217
  256.2 3.7 fusion.106
  263.1 3.7 convolution_convert_fusion.8
  271.0 2.8 copy.138
  275.3 5.0 multiply_reduce_fusion.5
  283.7 48.0 %ring_gather_2.1 = (bf16[2,16,64,2048]{3,2,1,0:T(8,128)(2,1)}, bf16[2,16,64,128]{3,2,1,0:T(8,128)(2,1)}) custom-call(bf16[2,64,2048]{2,1,0:T(8,128)(2,1)} %bitcast.203, bf16[2,64,128]{2,1,0:T(8,128)(2,1)} %bitcast.220), custom_call_target="tpu_custom_call" | custom-call | bytes 17825792 | tf_op jit(solution)/shard_map/ring_gather_2/pallas_call | solution.py:217
  331.7 79.1 %experts.1 = (bf16[2048,2048]{1,0:T(8,128)(2,1)}, bf16[2048,2048]{1,0:T(8,128)(2,1)}, bf16[2048,128]{1,0:T(8,128)(2,1)}, bf16[1024,2048]{1,0:T(8,128)(2,1)}, bf1...) custom-call(bf16[2048,2048]{1,0:T(8,128)(2,1)} %bitcast.232, ...), custom_call_target="tpu_custom_call" | custom-call | flops 52613349376 | bytes 41943040 | tf_op jit(solution)/shard_map/experts/pallas_call | solution.py:538
  410.9 48.9 %ring_reduce_3.1 = (f32[2,64,2048]{2,1,0:T(8,128)}, f32[2,64,128]{2,1,0:T(8,128)}) custom-call(bf16[2,16,64,2048]{3,2,1,0:T(8,128)(2,1)} %bitcast.186, bf16[2,16,64,128]{3,2,1,0:T(8,128)(2,1)} %bitcast.212), custom_call_target="tpu_custom_call" | custom-call | bytes 17825792 | tf_op jit(solution)/shard_map/ring_reduce_3/pallas_call | solution.py:371
  460.8 3.2 multiply_reduce_fusion.1
  465.3 5.4 fusion.46
  472.0 7.0 fusion.41
  479.4 4.9 convolution_convert_fusion.2
  486.0 4.9 convolution_convert_fusion.3
  491.2 5.2 convolution_convert_fusion.4
  498.2 65.4 %reduce-scatter.3.cloned.1.call-done = bf16[2,64,2048]{2,1,0:T(8,128)(2,1)} async-done(((bf16[2,1024,2048]{2,1,0:T(8,128)(2,1)}), bf16[2,64,2048]{2,1,0:T(8,128)(2,1)}) %reduce-scatter.3.cloned.1.call-update) | async-done | bytes 524304 | tf_op jit(solution)/shard_map/reduce_scatter | solution.py:780
  563.6 3.1 convert_add_fusion.4
  567.7 5.6 convolution_convert_fusion.1
  573.3 6.6 fusion.49
  588.5 3.8 multiply_convert_fusion
  592.3 4.8 broadcast_multiply_fusion
  599.3 5.9 fusion.9
  605.2 4.0 copy.157
  609.5 3.5 pad_maximum_fusion.2.refs_0_
  613.0 36.8 %ring_reduce_4.1 = f32[2,64,576]{2,1,0:T(8,128)} custom-call(bf16[2,16,64,576]{3,2,1,0:T(8,128)(2,1)} %pad_maximum_fusion.2.refs_0_), custom_call_target="tpu_custom_call" | custom-call | bytes 4718592 | tf_op jit(solution)/shard_map/ring_reduce_4/pallas_call | solution.py:371
  650.9 7.1 broadcast_multiply_fusion.1
  658.0 5.8 copy.149
  663.7 2.5 slice.221
  675.3 2.6 convert_element_type.258
  679.5 5.9 fusion.34
  685.4 4.1 fusion.33
  689.5 8.9 fusion.112
  698.6 6.5 convolution_convert_fusion
  705.4 4.0 multiply_reduce_fusion.2
  711.7 7.9 copy.163
  719.6 7.5 convert_element_type.260.refs_1_
  730.2 4.3 copy.164
  734.5 107.3 %ring_reduce_5.1 = (f32[64,3072]{1,0:T(8,128)}, f32[16,4096]{1,0:T(8,128)}, f32[64,576]{1,0:T(8,128)}, f32[16,128]{1,0:T(8,128)}) custom-call(bf16[2,16,64,3072]{3,2,1,0:T(8,128)(2,1)} %bitcast.164, bf16[2,16,16,4096]{3,2,1,0:T(8,128)(2,1)} %convert_element_type.260.refs_1_, bf16[2,16,64,576]{3,2,1,0:T(8,128)(2,1)} %bitcast.176, ...), custom_call_target="tpu_custom_call" | custom-call | bytes 38535168 | tf_op jit(solution)/shard_map/ring_reduce_5/pallas_call | solution.py:371
  843.9 3.8 fusion.1
  849.9 5.4 convert_add_fusion.3
  862.2 2.6 multiply_add_fusion
  864.8 7.5 convert_add_fusion.2
  872.3 7.0 convert_add_fusion.1
  879.4 6.8 convert_add_fusion
  (291 shorter events, 94.6 us)
Async XLA Ops:
  7.2 324.5 %all-gather.2.cloned.1.call-start = ((), (), s32[]{:S(2)}) async-start(), calls=%async_computation.2 | async-start | bytes 8912896 | tf_op jit(solution)/shard_map/all_gather | solution.py:668
  16.7 146.7 %copy-start.31 = (bf16[2,64,2048]{2,1,0:T(8,128)(2,1)S(1)}, bf16[2,64,2048]{2,1,0:T(8,128)(2,1)}, u32[]{:S(2)}) copy-start(bf16[2,64,2048]{2,1,0:T(8,128)(2,1)} %param.20) | copy-start | bytes 1572868
  16.7 150.0 %copy-start.46 = (s32[2,13,13]{2,0,1:T(2,128)S(1)}, s32[2,13,13]{2,0,1:T(2,128)}, u32[]{:S(2)}) copy-start(s32[2,13,13]{2,0,1:T(2,128)} %param.22) | copy-start | bytes 4060
  16.7 150.0 %copy-start.55 = (s32[2,1024]{1,0:T(2,128)S(1)}, s32[2,1024]{1,0:T(2,128)}, u32[]{:S(2)}) copy-start(s32[2,1024]{1,0:T(2,128)} %param.21) | copy-start | bytes 24580
  164.6 399.0 %reduce-scatter.3.cloned.1.call-start = ((), (), s32[]{:S(2)}) async-start(), calls=%async_computation.3 | async-start | bytes 8912896 | tf_op jit(solution)/shard_map/reduce_scatter | solution.py:780
  164.6 167.1 %collective-permute-start = (bf16[1024,1408]{1,0:T(8,128)(2,1)}, bf16[1024,1408]{1,0:T(8,128)(2,1)}, u32[]{:S(2)}, u32[]{:S(2)}) collective-permute-start(bf16[1024,1408]{1,0:T(8,128)(2,1)} %refs_6_), channel_id=1, source_target_pairs={{0,16},{16,0},{1,17},{17,1},{2,18},{18,2},{3,19},{19,3},{4,20},{20... | collective-permute-start | bytes 8650760 | tf_op jit(solution)/shard_map/ppermute | solution.py:619
  165.2 166.5 %collective-permute-start.1 = (bf16[1024,1408]{1,0:T(8,128)(2,1)}, bf16[1024,1408]{1,0:T(8,128)(2,1)}, u32[]{:S(2)}, u32[]{:S(2)}) collective-permute-start(bf16[1024,1408]{1,0:T(8,128)(2,1)} %refs_7_), channel_id=1, source_target_pairs={{0,16},{16,0},{1,17},{17,1},{2,18},{18,2},{3,19},{19,3},{4,20},{20... | collective-permute-start | bytes 8650760 | tf_op jit(solution)/shard_map/ppermute | solution.py:619
  167.7 4.6 copy-start.26
  177.2 10.0 %copy-start.9 = (bf16[2,64,2048]{2,1,0:T(8,128)(2,1)}, bf16[2,64,2048]{2,1,0:T(8,128)(2,1)S(1)}, u32[]{:S(2)}) copy-start(bf16[2,64,2048]{2,1,0:T(8,128)(2,1)S(1)} %multiply_convert_fusion.3) | copy-start | bytes 1572868
  180.3 6.9 copy-start.20
  180.5 6.7 copy-start.49
  189.5 59.1 %copy-start.11 = (f32[2,64,16,192]{3,2,1,0:T(8,128)S(1)}, f32[2,64,16,192]{3,2,1,0:T(8,128)}, u32[]{:S(2)}) copy-start(f32[2,64,16,192]{3,2,1,0:T(8,128)} %reshape.386) | copy-start | bytes 4718596
  192.7 56.3 %copy-start.52 = (f32[32]{0:T(128)}, f32[32]{0:T(128)S(1)}, u32[]{:S(2)}) copy-start(f32[32]{0:T(128)S(1)} %negate_power_fusion) | copy-start | bytes 388
  192.7 56.3 %copy-start.47 = (f32[2,64]{1,0:T(2,128)}, f32[2,64]{1,0:T(2,128)S(1)}, u32[]{:S(2)}) copy-start(f32[2,64]{1,0:T(2,128)S(1)} %add_convert_fusion.3) | copy-start | bytes 1540
  193.1 56.0 %copy-start.34 = (f32[2,64,32]{2,1,0:T(8,128)}, f32[2,64,32]{2,1,0:T(8,128)S(1)}, u32[]{:S(2)}) copy-start(f32[2,64,32]{2,1,0:T(8,128)S(1)} %get-tuple-element.190) | copy-start | bytes 49156
  275.3 5.0 copy-start.12
  275.3 6.1 copy-start.25
  459.8 426.3 %reduce-scatter.5.cloned.1.call-start = ((), (), s32[]{:S(2)}) async-start(), calls=%async_computation.4 | async-start | bytes 8650752 | tf_op jit(solution)/shard_map/reduce_scatter | solution.py:801
  465.3 6.7 copy-start.56
  470.7 8.7 copy-start.57
  470.7 8.7 copy-start.61
  470.7 371.2 %collective-permute-start.6 = (bf16[1024,256]{1,0:T(8,128)(2,1)}, bf16[1024,256]{1,0:T(8,128)(2,1)}, u32[]{:S(2)}, u32[]{:S(2)}) collective-permute-start(bf16[1024,256]{1,0:T(8,128)(2,1)} %fusion.46), channel_id=1, source_target_pairs={{0,16},{16,0},{1,17},{17,1},{2,18},{18,2},{3,19},{19,3},{4,20},{20... | collective-permute-start | bytes 1572872 | tf_op jit(solution)/shard_map/ppermute | solution.py:790
  479.1 362.8 %collective-permute-start.5 = (bf16[1024,512]{1,0:T(8,128)(2,1)}, bf16[1024,512]{1,0:T(8,128)(2,1)}, u32[]{:S(2)}, u32[]{:S(2)}) collective-permute-start(bf16[1024,512]{1,0:T(8,128)(2,1)} %fusion.41), channel_id=1, source_target_pairs={{0,16},{16,0},{1,17},{17,1},{2,18},{18,2},{3,19},{19,3},{4,20},{20... | collective-permute-start | bytes 3145736 | tf_op jit(solution)/shard_map/ppermute | solution.py:790
  479.4 6.6 copy-start.59
  479.4 6.6 copy-start.63
  484.3 357.6 %collective-permute-start.4 = (bf16[1024,1408]{1,0:T(8,128)(2,1)}, bf16[1024,1408]{1,0:T(8,128)(2,1)}, u32[]{:S(2)}, u32[]{:S(2)}) collective-permute-start(bf16[1024,1408]{1,0:T(8,128)(2,1)} %convolution_convert_fusion.2), channel_id=1, source_target_pairs={{0,16},{16,0},{1,17},{17,1},{2,18},{18,2},{3,19},{19,3},{4,20},{20... | collective-permute-start | bytes 8650760 | tf_op jit(solution)/shard_map/ppermute | solution.py:790
  486.0 5.2 copy-start.65
  490.9 351.0 %collective-permute-start.3 = (bf16[1024,1408]{1,0:T(8,128)(2,1)}, bf16[1024,1408]{1,0:T(8,128)(2,1)}, u32[]{:S(2)}, u32[]{:S(2)}) collective-permute-start(bf16[1024,1408]{1,0:T(8,128)(2,1)} %convolution_convert_fusion.3), channel_id=1, source_target_pairs={{0,16},{16,0},{1,17},{17,1},{2,18},{18,2},{3,19},{19,3},{4,20},{20... | collective-permute-start | bytes 8650760 | tf_op jit(solution)/shard_map/ppermute | solution.py:790
  496.5 71.2 %copy-start.13 = (bf16[2,64,16,128]{3,2,1,0:T(8,128)(2,1)S(1)}, bf16[2,64,16,128]{3,2,1,0:T(8,128)(2,1)}, u32[]{:S(2)}) copy-start(bf16[2,64,16,128]{3,2,1,0:T(8,128)(2,1)} %copy-done.12) | copy-start | bytes 1572868
  496.5 345.4 %collective-permute-start.2 = (bf16[1024,1408]{1,0:T(8,128)(2,1)}, bf16[1024,1408]{1,0:T(8,128)(2,1)}, u32[]{:S(2)}, u32[]{:S(2)}) collective-permute-start(bf16[1024,1408]{1,0:T(8,128)(2,1)} %convolution_convert_fusion.4), channel_id=1, source_target_pairs={{0,16},{16,0},{1,17},{17,1},{2,18},{18,2},{3,19},{19,3},{4,20},{20... | collective-permute-start | bytes 8650760 | tf_op jit(solution)/shard_map/ppermute | solution.py:790
  583.4 5.1 copy-start.18
  592.3 7.0 copy-start.19
  677.9 7.5 copy-start.23
  689.5 9.0 copy-start.10
  698.5 6.5 copy-start.41
  698.5 6.7 copy-start.51
  698.5 6.8 copy-start.8
  698.5 6.8 copy-start.32
  698.5 6.8 copy-start.40
  698.5 6.8 copy-start.54
  855.4 6.9 copy-start.6
  864.8 7.5 copy-start.60
  864.8 7.5 copy-start.64
  872.3 7.0 copy-start.58
  872.3 7.0 copy-start.62
  879.3 8.6 copy-start.33
  879.3 9.4 %copy-start.38 = (f32[64,576]{1,0:T(8,128)S(1)}, f32[64,576]{1,0:T(8,128)}, u32[]{:S(2)}) copy-start(f32[64,576]{1,0:T(8,128)} %get-tuple-element.224) | copy-start | bytes 442372
  879.3 10.1 %copy-start.37 = (f32[16,4096]{1,0:T(8,128)S(1)}, f32[16,4096]{1,0:T(8,128)}, u32[]{:S(2)}) copy-start(f32[16,4096]{1,0:T(8,128)} %get-tuple-element.226) | copy-start | bytes 786436
  (31 other events, 82.6 us)
Sparse Core Ops, SparseCore 0:
  164.7 79.4 all-gather.1
  460.0 103.5 reduce-scatter.2
  573.5 150.9 reduce-scatter.4

commit v4 on v3

--- a/solution.py
+++ b/solution.py
@@ -249,16 +249,108 @@
     lax.fori_loop(0, rows // step, one, 0)
 
 
-def reduce_kernel(ring, wide, leads, count, *refs):
-    ins, outs = refs[:count], refs[count : 2 * count]
-    own, twin, got = (refs[(2 + k) * count : (3 + k) * count] for k in range(3))
-    refs = refs[5 * count :]
+class Products:
+    tile = 256
+
+    def __init__(self, cuts, pairs, lefts, rights, outs, held, *rest):
+        self.cuts, self.pairs, self.lefts, self.rights, self.outs = cuts, pairs, lefts, rights, outs
+        self.held = held
+        self.tiles, self.stage, self.load_sem, self.tile_sem, self.store_sem = rest
+        self.units = [
+            (j, m) for j in range(len(pairs)) for m in range(0, cuts[pairs[j][0]][1], self.tile)
+        ]
+        self.done, self.loaded, self.stores = 0, set(), [None, None]
+        self.ship, self.shipped = {}, []
+
+    def deliver(self):
+        for j in sorted(self.ship):
+            last = max(i for i, unit in enumerate(self.units) if unit[0] == j)
+            if self.done > last + 2 or (self.done == len(self.units) and self.stores == []):
+                cp = self.ship.pop(j)()
+                cp.start()
+                self.shipped.append(cp)
+
+    def fetch(self, number):
+        j, m = self.units[number]
+        left = self.pairs[j][0]
+        source, slot = self.lefts[left], number % 2
+        return pltpu.make_async_copy(
+            source.at[:, pl.ds(self.cuts[left][0] + m, self.tile)],
+            self.tiles.at[slot, pl.ds(0, source.shape[0]), :],
+            self.tile_sem.at[slot],
+        )
+
+    def start(self):
+        self.fetch(0).start()
+        self.loads = []
+        for i, source in enumerate(self.rights):
+            cp = pltpu.make_async_copy(source, self.held[i], self.load_sem.at[i])
+            cp.start()
+            self.loads.append(cp)
+
+    def run(self, upto):
+        while self.done < min(upto, len(self.units)):
+            j, m = self.units[self.done]
+            left, right, first, width = self.pairs[j]
+            if right not in self.loaded:
+                self.loads[right].wait()
+                self.loaded.add(right)
+            self.fetch(self.done).wait()
+            if self.done + 1 < len(self.units):
+                self.fetch(self.done + 1).start()
+            slot = self.done % 2
+            value = lax.dot_general(
+                self.tiles[slot, pl.ds(0, self.lefts[left].shape[0]), :],
+                self.held[right][:, pl.ds(first, width)],
+                (((0,), (0,)), ((), ())),
+                preferred_element_type=F32,
+            )
+            if self.stores[slot] is not None:
+                self.stores[slot].wait()
+            self.stage[slot, :, pl.ds(0, width)] = value.astype(BF)
+            cp = pltpu.make_async_copy(
+                self.stage.at[slot, :, pl.ds(0, width)],
+                self.outs[j].at[pl.ds(m, self.tile), :],
+                self.store_sem.at[slot],
+            )
+            cp.start()
+            self.stores[slot] = cp
+            self.done += 1
+            self.deliver()
+
+    def finish(self):
+        self.run(len(self.units))
+        for cp in self.stores:
+            if cp is not None:
+                cp.wait()
+        self.stores = []
+        self.deliver()
+        for cp in self.shipped:
+            cp.wait()
+
+
+def reduce_kernel(ring, wide, leads, count, cuts, pairs, ships, *refs):
+    njobs = len(pairs)
+    nleft = len(cuts)
+    nright = 1 + max([p[1] for p in pairs], default=-1)
+    nops = nleft + nright
+    ins, sources, refs = refs[:count], refs[count : count + nops], refs[count + nops :]
+    outs, job_outs, refs = refs[:count], refs[count : count + njobs], refs[count + njobs :]
+    ship_outs, refs = refs[: len(ships)], refs[len(ships) :]
+    own, twin, got = (refs[k * count : (1 + k) * count] for k in range(3))
+    refs = refs[3 * count :]
     wides = sum(wide)
     finals, ygots = refs[:wides], refs[wides : 2 * wides]
-    own_sem, tss, trs, rss, rrs, yss, yrs = refs[2 * wides :]
+    own_sem, tss, trs, rss, rrs, yss, yrs = refs[2 * wides : 2 * wides + 7]
+    refs = refs[2 * wides + 7 :]
+    jobs = None
+    if njobs:
+        jobs = Products(
+            cuts, pairs, sources[:nleft], sources[nleft:], job_outs, refs[:nright], *refs[nright : nright + 5]
+        )
     f, c, core, p, way = ring.here()
     n, nf = ring.chips, ring.nf
-    greet(ring, f, c, core, p, way, any(wide))
+    greet(ring, f, c, core, p, way, any(wide) or len(ships) > 0)
     to_next = (f, ring.device(p + way, core))
     to_twin = (f, c + 1 - 2 * core)
 
@@ -289,6 +381,13 @@
             cp.start()
             loads[s, number] = cp
 
+    if jobs:
+        for w, j in enumerate(ships):
+            jobs.ship[j] = functools.partial(
+                remote, job_outs[j], ship_outs[w], refs[-2].at[w], refs[-1].at[w], ((f + 1) % nf, c)
+            )
+        jobs.start()
+
     def wait_parts(s, number, i, k):
         loads[s, number].wait()
         here = twin[i].at[s, k]
@@ -299,8 +398,12 @@
         cp.start()
         started.append(cp)
 
+    turn, turns = 0, (n - 1) * len(streams)
     for s in range(n):
         for number, i, k, lead in streams:
+            if jobs and s > 0:
+                jobs.run(-(-len(jobs.units) * turn // turns))
+                turn += 1
             wait_parts(s, number, i, k)
             mine, other = own[i].at[s, k], twin[i].at[s, k]
             if s == 0:
@@ -350,13 +453,16 @@
                     target[rows, :] = target[rows, :] + here[rows, :].astype(F32)
 
                 add_rows(here.shape, finish)
+    if jobs:
+        jobs.finish()
     for cp in started:
         cp.wait_send()
 
 
-def ring_reduce(ring, number, arrays, wide):
+def ring_reduce(ring, number, arrays, wide, lefts=(), rights=(), cuts=(), pairs=(), ships=()):
     n, nf = ring.chips, ring.nf
     leads = [a.shape[0] for a in arrays]
+    more = [jax.ShapeDtypeStruct((cuts[l][1], width), BF) for l, _, _, width in pairs]
     streams = sum(leads)
     block = [a.shape[2:] for a in arrays]
     shapes = [
@@ -366,13 +472,28 @@
     scratch = [pltpu.VMEM((n, l) + b, BF) for b, l in zip(block, leads)] * 2
     scratch += [pltpu.VMEM((n - 1, l) + b, BF) for b, l in zip(block, leads)]
     scratch += [pltpu.VMEM((nf - 1,) + b, BF) for b, w in zip(block, wide) if w] * 2
+    more += [more[j] for j in ships]
     wides = max(1, sum(wide))
-    size = sum(a.size * 2 for a in arrays)
+    extra = []
+    if pairs:
+        extra = [pltpu.VMEM(a.shape, BF) for a in rights]
+        extra += [
+            pltpu.VMEM((2, max(a.shape[0] for a in lefts), Products.tile), BF),
+            pltpu.VMEM((2, Products.tile, max(p[3] for p in pairs)), BF),
+            dma((len(rights),)),
+            dma((2,)),
+            dma((2,)),
+        ]
+    if ships:
+        extra += [dma((len(ships),)), dma((len(ships),))]
     return pl.pallas_call(
-        functools.partial(reduce_kernel, ring, tuple(wide), tuple(leads), len(arrays)),
-        out_shape=shapes,
-        in_specs=[pl.BlockSpec(memory_space=pl.ANY)] * len(arrays),
-        out_specs=[pl.BlockSpec(memory_space=pltpu.VMEM)] * len(arrays),
+        functools.partial(
+            reduce_kernel, ring, tuple(wide), tuple(leads), len(arrays), tuple(cuts), tuple(pairs), tuple(ships)
+        ),
+        out_shape=shapes + more,
+        in_specs=[pl.BlockSpec(memory_space=pl.ANY)] * (len(arrays) + len(lefts) + len(rights)),
+        out_specs=[pl.BlockSpec(memory_space=pltpu.VMEM)] * len(arrays)
+        + [pl.BlockSpec(memory_space=pl.ANY)] * len(more),
         scratch_shapes=scratch
         + [
             dma((n, streams)),
@@ -382,13 +503,14 @@
             dma((n - 1, streams)),
             dma((wides, max(1, nf - 1))),
             dma((wides, max(1, nf - 1))),
-        ],
+        ]
+        + extra,
         compiler_params=pltpu.CompilerParams(
-            collective_id=number, has_side_effects=True, vmem_limit_bytes=56 << 20
+            collective_id=number, has_side_effects=True, vmem_limit_bytes=60 << 20
         ),
-        cost_estimate=pl.CostEstimate(flops=0, bytes_accessed=2 * size, transcendentals=0),
+        cost_estimate=pl.CostEstimate(flops=0, bytes_accessed=1 << 20, transcendentals=0),
         name="ring_reduce_%d" % number,
-    )(*arrays)
+    )(*arrays, *lefts, *rights)
 
 
 def expert_kernel(nf, experts, fp, bundle_slots, *refs):
@@ -567,6 +689,164 @@
     )(tree_rows, tree_grads, tree_probs, slot[:, None, :], slot.reshape(rows, 1), *flat)
 
 
+def nt(left, right):
+    return lax.dot_general(left, right, (((1,), (1,)), ((), ())), preferred_element_type=F32)
+
+
+def tn(left, right):
+    return lax.dot_general(left, right, (((0,), (0,)), ((), ())), preferred_element_type=F32)
+
+
+HEADS = 4
+
+
+def attend_kernel(scale, nope, rope, keys, allowed, expand, tokens, w_hbm, cat, lse, mixed, heads, residual, w_out, sem):
+    trees, tok = cat.shape[0], cat.shape[2]
+    copy = pltpu.make_async_copy(w_hbm, w_out, sem)
+    copy.start()
+    for h in range(H):
+        low = nt(nope[:, h * DN : (h + 1) * DN], expand[:, h * (DN + DV) : h * (DN + DV) + DN])
+        low = low.astype(BF)
+        for b in range(trees):
+            rows = slice(b * tok, (b + 1) * tok)
+            cat[b, h, :, :LAT] = low[rows]
+            cat[b, h, :, LAT:] = rope[rows, h * 128 : (h + 1) * 128]
+
+    def group(i, carry):
+        b, g = i // (H // HEADS), i % (H // HEADS) * HEADS
+        query = cat[b, pl.ds(g, HEADS)].reshape(HEADS * tok, -1)
+        scores = nt(query, keys[b]) * scale
+        scores = scores.reshape(HEADS, tok, -1)
+        scores = jnp.where(allowed[b][None] > 0, scores, -1e30)
+        highest = jnp.max(scores, axis=-1, keepdims=True)
+        raised = jnp.exp(scores - highest)
+        total = jnp.sum(raised, axis=-1, keepdims=True)
+        lse[b, pl.ds(g, HEADS)] = highest + jnp.log(total)
+        probs = (raised * (1.0 / total)).astype(BF).reshape(HEADS * tok, -1)
+        mix = multiply(probs, keys[b, :, :LAT]).astype(BF)
+        mixed[b, pl.ds(g, HEADS)] = mix.reshape(HEADS, tok, LAT)
+        return carry
+
+    lax.fori_loop(0, trees * (H // HEADS), group, 0)
+    for h in range(H):
+        mix = jnp.concatenate([mixed[b, h] for b in range(trees)], axis=0)
+        value = expand[:, h * (DN + DV) + DN : (h + 1) * (DN + DV)]
+        heads[:, h * DV : (h + 1) * DV] = multiply(mix, value).astype(BF)
+    copy.wait()
+    for start in range(0, D, 512):
+        cut = slice(start, start + 512)
+        residual[:, cut] = tokens[:, cut].astype(F32) + multiply(heads[...], w_out[:, cut])
+
+
+def attend(nope, rope, keys, allowed, expand, tokens, w_output, tok, scale):
+    rows = tokens.shape[0]
+    trees = rows // tok
+    vmem = pl.BlockSpec(memory_space=pltpu.VMEM)
+    length, width = keys.shape[1:]
+    return pl.pallas_call(
+        functools.partial(attend_kernel, scale),
+        out_shape=[
+            jax.ShapeDtypeStruct((trees, H, tok, width), BF),
+            jax.ShapeDtypeStruct((trees, H, tok, 1), F32),
+            jax.ShapeDtypeStruct((trees, H, tok, LAT), BF),
+            jax.ShapeDtypeStruct((rows, H * DV), BF),
+            jax.ShapeDtypeStruct((rows, D), F32),
+        ],
+        in_specs=[vmem] * 6 + [pl.BlockSpec(memory_space=pl.ANY)],
+        out_specs=[vmem] * 5,
+        scratch_shapes=[pltpu.VMEM(w_output.shape, BF), pltpu.SemaphoreType.DMA],
+        compiler_params=pltpu.CompilerParams(vmem_limit_bytes=56 << 20),
+        cost_estimate=pl.CostEstimate(
+            flops=2 * rows * H * length * 1152, bytes_accessed=30 << 20, transcendentals=rows * H * length
+        ),
+        name="attend",
+    )(nope, rope, keys, allowed, expand, tokens, w_output)
+
+
+def attend_back_kernel(
+    scale, grad, w_out, expand, cat, keys, lse, allowed, mixed, nope, keys_grad, nope_grad, rope_grad,
+    expand_grad, heads_grad, mix_grad, low_probs, score_grad, cat_grad,
+):
+    trees, tok = cat.shape[0], cat.shape[2]
+    for start in range(0, H * DV, 512):
+        heads_grad[:, start : start + 512] = nt(grad[...], w_out[start : start + 512, :]).astype(BF)
+    for h in range(H):
+        value = expand[:, h * (DN + DV) + DN : (h + 1) * (DN + DV)]
+        own = heads_grad[:, h * DV : (h + 1) * DV]
+        back = nt(own, value).astype(BF)
+        for b in range(trees):
+            mix_grad[b, h] = back[b * tok : (b + 1) * tok]
+        mix = jnp.concatenate([mixed[b, h] for b in range(trees)], axis=0)
+        expand_grad[:, h * (DN + DV) + DN : (h + 1) * (DN + DV)] = tn(mix, own).astype(BF)
+    for b in range(trees):
+
+        def group(i, carry, b=b):
+            g = i * HEADS
+            rows = pl.ds(pl.multiple_of(g * tok, HEADS * tok), HEADS * tok)
+            query = cat[b, pl.ds(g, HEADS)].reshape(HEADS * tok, -1)
+            mix = mix_grad[b, pl.ds(g, HEADS)].reshape(HEADS * tok, -1)
+            scores = (nt(query, keys[b]) * scale).reshape(HEADS, tok, -1)
+            probs = jnp.where(
+                allowed[b][None] > 0, jnp.exp(scores - lse[b, pl.ds(g, HEADS)]), 0.0
+            ).reshape(HEADS * tok, -1)
+            prob_grad = nt(mix, keys[b, :, :LAT])
+            centre = jnp.sum(probs * prob_grad, axis=-1, keepdims=True)
+            low_probs[rows, :] = probs.astype(BF)
+            own = (probs * (prob_grad - centre)).astype(BF)
+            score_grad[rows, :] = own
+            back = (multiply(own, keys[b]) * scale).reshape(HEADS, tok, -1)
+            cat_grad[b, pl.ds(g, HEADS)] = back[..., :LAT].astype(BF)
+            for k in range(HEADS):
+                rope_grad[b, g + k] = back[k, :, LAT:]
+            return carry
+
+        lax.fori_loop(0, H // HEADS, group, 0)
+        query = cat[b].reshape(H * tok, -1)
+        mix = mix_grad[b].reshape(H * tok, -1)
+        length = keys.shape[1]
+        for start in range(0, length, 256):
+            cut = slice(start, start + 256)
+            total = tn(score_grad[:, cut], query) * scale
+            keys_grad[b, cut, :LAT] = (total[:, :LAT] + tn(low_probs[:, cut], mix)).astype(BF)
+            keys_grad[b, cut, LAT:] = total[:, LAT:].astype(BF)
+    for h in range(H):
+        low = jnp.concatenate([cat_grad[b, h] for b in range(trees)], axis=0)
+        key = expand[:, h * (DN + DV) : h * (DN + DV) + DN]
+        nope_grad[:, h * DN : (h + 1) * DN] = multiply(low, key)
+        expand_grad[:, h * (DN + DV) : h * (DN + DV) + DN] = tn(
+            low, nope[:, h * DN : (h + 1) * DN]
+        ).astype(BF)
+
+
+def attend_back(grad, w_output, expand, cat, keys, lse, allowed, mixed, nope, scale):
+    trees, _, tok, width = cat.shape
+    length, rows = keys.shape[1], grad.shape[0]
+    vmem = pl.BlockSpec(memory_space=pltpu.VMEM)
+    return pl.pallas_call(
+        functools.partial(attend_back_kernel, scale),
+        out_shape=[
+            jax.ShapeDtypeStruct(keys.shape, BF),
+            jax.ShapeDtypeStruct((rows, H * DN), F32),
+            jax.ShapeDtypeStruct((trees, H, tok, width - LAT), F32),
+            jax.ShapeDtypeStruct(expand.shape, BF),
+        ],
+        in_specs=[vmem] * 9,
+        out_specs=[vmem] * 4,
+        scratch_shapes=[
+            pltpu.VMEM((rows, H * DV), BF),
+            pltpu.VMEM((trees, H, tok, LAT), BF),
+            pltpu.VMEM((H * tok, length), BF),
+            pltpu.VMEM((H * tok, length), BF),
+            pltpu.VMEM((trees, H, tok, LAT), BF),
+        ],
+        compiler_params=pltpu.CompilerParams(vmem_limit_bytes=60 << 20),
+        cost_estimate=pl.CostEstimate(
+            flops=0, bytes_accessed=1 << 20, transcendentals=0
+        ),
+        name="attend_back",
+    )(grad, w_output, expand, cat, keys, lse, allowed, mixed, nope)
+
+
 def body(
     tokens,
     out_grad,
@@ -680,46 +960,30 @@
     latent_normed, latent_inverse, latent_gained = normalize(latent_all[:, :LAT], gain_latent)
     key_latent = latent_gained.astype(BF).reshape(trees, tok_loc, LAT)
     key_rope = rotate(latent_all[:, LAT:].reshape(trees, tok_loc, DR), cosine, sine).astype(BF)
+    key_pad = jnp.zeros((trees, tok_loc, 128 - DR), BF)
     (keys,) = ring_gather(
-        ring, 1, [jnp.concatenate([key_latent, key_rope], axis=-1)], [False]
-    )
-    keys = keys.reshape(trees, tree_len, LAT + DR)
-    keys_latent = keys[:, :, :LAT]
+        ring, 1, [jnp.concatenate([key_latent, key_rope, key_pad], axis=-1)], [False]
+    )
+    keys = keys.reshape(trees, tree_len, LAT + 128)
     query_all = lax.optimization_barrier(multiply(hidden_in, w_query))
     query_all = query_all.reshape(trees, tok_loc, H, DN + DR)
-    query_nope = query_all[..., :DN].astype(BF)
+    query_nope = query_all[..., :DN].astype(BF).reshape(row_total, H * DN)
     query_rope = rotate(
         query_all[..., DN:], cosine[:, :, None, :], sine[:, :, None, :]
     ).astype(BF)
-    expand = w_expand.reshape(LAT, H, DN + DV)
-    expand_key = expand[..., :DN]
-    expand_value = expand[..., DN:]
-    query_latent = jnp.einsum(
-        "bthn,chn->bthc", query_nope, expand_key, preferred_element_type=F32
-    ).astype(BF)
-    query_cat = jnp.concatenate([query_latent, query_rope], axis=-1).reshape(
-        trees, tok_loc * H, LAT + DR
-    )
-
-    def attention_scores():
-        raw_scores = jnp.einsum("bqc,bjc->bqj", query_cat, keys, preferred_element_type=F32)
-        raw_scores = raw_scores.reshape(trees, tok_loc, H, tree_len)
-        scores = jnp.where(allowed[:, :, None, :], raw_scores * score_scale, -1e30)
-        return scores.reshape(trees, tok_loc * H, tree_len)
-
-    scores = attention_scores()
-    highest = jnp.max(scores, axis=-1, keepdims=True)
-    exp_total = jnp.sum(jnp.exp(scores - highest), axis=-1, keepdims=True)
-    log_total = highest + jnp.log(exp_total)
-    weights_low = jnp.exp(scores - log_total).astype(BF)
-    mixed = jnp.einsum("bqj,bjc->bqc", weights_low, keys_latent, preferred_element_type=F32)
-    mixed = mixed.astype(BF).reshape(trees, tok_loc, H, LAT)
-    heads = (
-        jnp.einsum("bthc,chv->bthv", mixed, expand_value, preferred_element_type=F32)
-        .astype(BF)
-        .reshape(row_total, H * DV)
-    )
-    residual = inputs + multiply(heads, w_output)
+    query_rope = jnp.pad(query_rope, ((0, 0), (0, 0), (0, 0), (0, 128 - DR)))
+    allowed = allowed.astype(F32)
+    query_cat, log_total, mixed, heads, residual = attend(
+        query_nope,
+        query_rope.reshape(row_total, H * 128),
+        keys,
+        allowed,
+        w_expand,
+        tokens.reshape(row_total, D),
+        w_output,
+        tok_loc,
+        score_scale,
+    )
     normed_mid, inverse_mid, gained_mid = normalize(residual, gain_ffn)
     hidden_mid = gained_mid.astype(BF)
     expert_probs = jax.nn.softmax(multiply(hidden_mid, w_router), axis=-1)
@@ -759,19 +1023,44 @@
     def weight_grads(k, e_gg, e_ug, e_hidden, s_act):
         cut = slice(k * part, (k + 1) * part)
         return (
+            transposed_multiply(tree_rows[:, cut], s_act[:, : 2 * fp]),
+            transposed_multiply(tree_grads[:, cut], s_act[:, 2 * fp :]),
             transposed_multiply(e_rows[:, cut], e_gg),
             transposed_multiply(e_rows[:, cut], e_ug),
             transposed_multiply(e_grads[:, cut], e_hidden),
-            transposed_multiply(tree_rows[:, cut], s_act[:, : 2 * fp]),
-            transposed_multiply(tree_grads[:, cut], s_act[:, 2 * fp :]),
-        )
+        )
+
+    job_arrays = [e_rows, e_grads, tree_rows, tree_grads], [e_gg, e_ug, e_hidden, s_act]
+    job_pairs = [
+        (2, 3, 0, 2 * fp),
+        (3, 3, 2 * fp, fp),
+        (0, 0, 0, e_gg.shape[1]),
+        (0, 1, 0, e_gg.shape[1]),
+        (1, 2, 0, e_gg.shape[1]),
+    ]
+
+    def job_cuts(k):
+        return [(k * part, part)] * 4
 
     def by_owner(x):
         return x.reshape(trees, nc, tok_loc, x.shape[-1])
 
-    back_sum, delta_sum = ring_reduce(
-        ring, 3, [by_owner(back), by_owner(delta_out)], [False] * 2
-    )
+    if nf == 2:
+        back_sum, delta_sum, *sent = ring_reduce(
+            ring,
+            3,
+            [by_owner(back), by_owner(delta_out)],
+            [False] * 2,
+            *job_arrays,
+            job_cuts(1),
+            job_pairs,
+            (0, 1),
+        )
+        there, sent = sent[5:], sent[2:5]
+    else:
+        back_sum, delta_sum = ring_reduce(
+            ring, 3, [by_owner(back), by_owner(delta_out)], [False] * 2
+        )
     back_sum, out_part = lax.optimization_barrier((back_sum, out_part))
     back_sum = roll_out(back_sum.reshape(row_total, D))
     prob_delta = jnp.sum(
@@ -780,14 +1069,14 @@
     out_sum = lax.psum_scatter(
         out_part.reshape(trees, tree_len, D), "ctx", scatter_dimension=1, tiled=True
     )
-    out_sum = roll_out(out_sum.reshape(row_total, D).astype(F32))
-    output = (residual + out_sum).astype(BF).reshape(trees, tok_loc, D)
 
     came = []
     for k in range(1, nf):
         perm = [(i, (i + k) % nf) for i in range(nf)]
-        grads = weight_grads(k, e_gg, e_ug, e_hidden, s_act)
+        grads = sent if nf == 2 else weight_grads(k, e_gg, e_ug, e_hidden, s_act)
         came.append([lax.ppermute(g.astype(BF), "fsdp", perm) for g in grads])
+    if nf == 2:
+        came[0] = list(there) + came[0]
 
     logit_grad = (
         expert_probs * (prob_delta - jnp.sum(expert_probs * prob_delta, axis=-1, keepdims=True))
@@ -797,54 +1086,45 @@
     mid_input, grad_gain_ffn = normalize_back(mid_grad, normed_mid, inverse_mid, gain_ffn)
     residual_grad = upstream + mid_input
     residual_low = residual_grad.astype(BF)
-    grad_output = transposed_multiply(heads, residual_low).astype(BF)
-    out_total = lax.psum_scatter(grad_output, both, scatter_dimension=0, tiled=True).astype(F32)
-    heads_grad = (
-        multiply_transposed(residual_low, w_output).astype(BF).reshape(trees, tok_loc, H, DV)
-    )
-    mixed_grad = jnp.einsum(
-        "bthv,chv->bthc", heads_grad, expand_value, preferred_element_type=F32
-    ).astype(BF)
-    mixed_grad_flat = mixed_grad.reshape(trees, tok_loc * H, LAT)
-    scores = attention_scores()
-    weights_full = jnp.exp(scores - log_total)
-    prob_grad = jnp.einsum(
-        "bqc,bjc->bqj", mixed_grad_flat, keys_latent, preferred_element_type=F32
-    )
-    score_grad = (
-        weights_full * (prob_grad - jnp.sum(weights_full * prob_grad, axis=-1, keepdims=True))
-    ).astype(BF)
-    keys_grad = (
-        jnp.einsum("bqj,bqc->bjc", score_grad, query_cat, preferred_element_type=F32) * score_scale
-    )
-    latent_part = jnp.einsum(
-        "bqj,bqc->bjc", weights_full.astype(BF), mixed_grad_flat, preferred_element_type=F32
-    )
-    keys_grad = jnp.concatenate(
-        [keys_grad[..., :LAT] + latent_part, keys_grad[..., LAT:]], axis=-1
-    ).astype(BF)
-    (own_keys_grad,) = ring_reduce(
-        ring, 4, [keys_grad.reshape(trees, nc, tok_loc, LAT + DR)], [False]
-    )
-    query_cat_grad = (
-        jnp.einsum("bqj,bjc->bqc", score_grad, keys, preferred_element_type=F32) * score_scale
-    ).reshape(trees, tok_loc, H, LAT + DR)
-    qlat_grad = query_cat_grad[..., :LAT].astype(BF)
-    qrope_grad = query_cat_grad[..., LAT:]
-    qnope_grad = jnp.einsum("bthc,chn->bthn", qlat_grad, expand_key, preferred_element_type=F32)
-    grad_key = jnp.einsum("bthc,bthn->chn", qlat_grad, query_nope, preferred_element_type=F32)
-    grad_value = jnp.einsum("bthc,bthv->chv", mixed, heads_grad, preferred_element_type=F32)
-    grad_expand = jnp.concatenate([grad_key, grad_value], axis=-1).reshape(LAT, H * (DN + DV))
+    keys_grad, qnope_grad, qrope_grad, grad_expand = attend_back(
+        residual_low,
+        w_output,
+        w_expand,
+        query_cat,
+        keys,
+        log_total,
+        allowed,
+        mixed,
+        query_nope,
+        score_scale,
+    )
+    qrope_grad = qrope_grad[..., :DR].transpose(0, 2, 1, 3)
     query_grad = jnp.concatenate(
-        [qnope_grad, rotate(qrope_grad, cosine[:, :, None, :], -sine[:, :, None, :])], axis=-1
+        [
+            qnope_grad.reshape(trees, tok_loc, H, DN),
+            rotate(qrope_grad, cosine[:, :, None, :], -sine[:, :, None, :]),
+        ],
+        axis=-1,
     )
     query_grad = query_grad.astype(BF).reshape(row_total, H * (DN + DR))
-    grad_query = transposed_multiply(hidden_in, query_grad)
+    own_keys_grad, grad_query, grad_output = ring_reduce(
+        ring,
+        4,
+        [keys_grad.reshape(trees, nc, tok_loc, LAT + 128)],
+        [False],
+        [hidden_in, heads],
+        [query_grad, residual_low],
+        [(0, D), (0, H * DV)],
+        [(0, 0, 0, query_grad.shape[1]), (1, 1, 0, D)],
+    )
+    own_keys_grad, out_sum = lax.optimization_barrier((own_keys_grad, out_sum))
+    out_sum = roll_out(out_sum.reshape(row_total, D).astype(F32))
+    output = (residual + out_sum).astype(BF).reshape(trees, tok_loc, D)
     hidden_grad = multiply_transposed(query_grad, w_query)
     latent_in_grad, grad_gain_latent = normalize_back(
         own_keys_grad[..., :LAT].reshape(row_total, LAT), latent_normed, latent_inverse, gain_latent
     )
-    rope_back = rotate(own_keys_grad[..., LAT:], cosine, -sine).reshape(row_total, DR)
+    rope_back = rotate(own_keys_grad[..., LAT : LAT + DR], cosine, -sine).reshape(row_total, DR)
     latent_grad = jnp.concatenate([latent_in_grad, rope_back], axis=-1).astype(BF)
     grad_latent = transposed_multiply(hidden_in, latent_grad)
     hidden_grad = hidden_grad + multiply_transposed(latent_grad, w_latent)
@@ -862,29 +1142,30 @@
     ).astype(BF)
     grad_small = jnp.pad(grad_small, ((0, 0), (0, PACK - grad_small.shape[1])))
     parts = [
-        grad_query.astype(BF).reshape(nf, nc, -1, w_query.shape[1]),
-        grad_expand.astype(BF).reshape(nf, nc, -1, w_expand.shape[1]),
+        grad_query.reshape(nf, nc, -1, w_query.shape[1]),
+        grad_expand.reshape(nf, nc, -1, w_expand.shape[1]),
         grad_latent.astype(BF).reshape(nf, nc, -1, w_latent.shape[1]),
         grad_small.reshape(nf, nc, 16, PACK // 16),
+        grad_output.reshape(nf, nc, -1, D),
     ]
     if nf == 2:
-        t_query, t_expand, t_latent, t_small = ring_reduce(ring, 5, parts, [True] * 4)
+        t_query, t_expand, t_latent, t_small, out_total, *ffn_sums = ring_reduce(
+            ring, 5, parts, [True] * 5, *job_arrays, job_cuts(0), job_pairs
+        )
+        came, ffn_sums = lax.optimization_barrier((came, ffn_sums))
     else:
-        t_query, t_expand, t_latent, t_small = (
+        t_query, t_expand, t_latent, t_small, out_total = (
             lax.psum_scatter(
                 x.reshape((nf * nc,) + x.shape[2:]), both, scatter_dimension=0, tiled=True
             )[0].astype(F32)
             for x in parts
         )
+        ffn_sums = weight_grads(0, e_gg, e_ug, e_hidden, s_act)
     t_small = t_small.reshape(PACK)
-    t_small, came, e_gg, e_ug, e_hidden, s_act = lax.optimization_barrier(
-        (t_small, came, e_gg, e_ug, e_hidden, s_act)
-    )
-    ffn_sums = list(weight_grads(0, e_gg, e_ug, e_hidden, s_act))
     for one in came:
-        ffn_sums = [a + b.astype(F32) for a, b in zip(ffn_sums, one)]
-    e_sums = ffn_sums[:3]
-    s_sums = [ffn_sums[3][:, :fs], ffn_sums[3][:, fp : fp + fs], ffn_sums[4][:, :fs]]
+        ffn_sums = [a.astype(F32) + b.astype(F32) for a, b in zip(ffn_sums, one)]
+    e_sums = ffn_sums[2:]
+    s_sums = [ffn_sums[0][:, :fs], ffn_sums[0][:, fp : fp + fs], ffn_sums[1][:, :fs]]
     return (
         output,
         input_grad,

time: 904 us -> 783 us (0.87)
  matrix products: 152 us -> 30.7 us
  Pallas kernels: 522 us -> 628 us
  waiting for transfers between devices: 65.4 us -> 0.18 us
  local copies, waits for them, and re-layouts: 102 us -> 53.5 us
  other arithmetic: 32.9 us -> 42.4 us
    dot_general x14 -> x2, matrix products: 72.3 us -> 3.1 us  [transposed_multiply(): lax.dot_general(left, right, (((0,), (0,)), ((), ())), preferred_element_...]
    reduce_scatter x1, waiting for transfers between devices: 65.4 us -> 0.11 us  [body(): lax.psum_scatter(out_part.reshape(trees, tree_len, D), 'ctx', scatter_dim...]
    pallas_call x0 -> x2, Pallas kernels: none -> 54.4 us  [the longest x1 36.3 us: attend_back(): pl.pallas_call(functools.partial(attend_back_kernel, scale), out_shape=[j...]
    pallas_call x3, Pallas kernels: 193 us -> 245 us  [ring_reduce(): pl.pallas_call(functools.partial(reduce_kernel, ring, tuple(wide), tuple(...]
    dot_general x8 -> x0, matrix products: 37.6 us -> none  [the longest x1 7.12 us: body(): jnp.einsum('bqj,bjc->bqc', score_grad, keys, preferred_element_type=F32)]
    add x3 -> x5, other arithmetic: 4.3 us -> 20 us  [body(): ffn_sums = [a.astype(F32) + b.astype(F32) for a, b in zip(ffn_sums, one)]]
    unnamed x158 -> x103, local copies, waits for them, and re-layouts: 31.3 us -> 18.2 us
    concatenate x3 -> x1, local copies, waits for them, and re-layouts: 11.1 us -> 0.08 us  [body(): jnp.concatenate([key_latent, key_rope, key_pad], axis=-1)]
  transfers between devices with their start and end apart: 10 -> 7, of which waited for: 1 -> 1; matrix products, arithmetic and copies ran while one was open for 29% -> 10% of each run, Pallas kernels for 28% -> 45%
where the time goes in v4:
time: 783 us; the launch traced here: 775 us
  Pallas kernels  628 us (80%)
  local copies, waits for them, and re-layouts  53.5 us (7%)
  other arithmetic  42.4 us (5%)
  matrix products  30.7 us (4%)
  between operations  15.3 us (2%)
    pallas_call x3, Pallas kernels, ring_gather(): pl.pallas_call(functools.partial(gather_kernel, ring, tuple(wide), tuple(...  250 us
    pallas_call x3, Pallas kernels, ring_reduce(): pl.pallas_call(functools.partial(reduce_kernel, ring, tuple(wide), tuple(...  245 us
    pallas_call x1, Pallas kernels, run_experts(): pl.pallas_call(functools.partial(expert_kernel, nf, experts, fp, bundle_s...  79.2 us
    pallas_call x1, Pallas kernels, attend_back(): pl.pallas_call(functools.partial(attend_back_kernel, scale), out_shape=[j...  36.3 us
    add x5, other arithmetic, body(): ffn_sums = [a.astype(F32) + b.astype(F32) for a, b in zip(ffn_sums, one)]  20 us
    unnamed x103, local copies, waits for them, and re-layouts  18.2 us
    pallas_call x1, Pallas kernels, attend(): pl.pallas_call(functools.partial(attend_kernel, scale), out_shape=[jax.Sh...  18.1 us
    dot_general x4, matrix products, multiply_transposed(): lax.dot_general(left, right, (((1,), (1,)), ((), ())), preferred_element_...  16.6 us
  transfers between devices with their start and end apart: 7, of which 1 were waited for; matrix products, arithmetic and copies ran while one was open for 10% of the time, Pallas kernels for 45%

profile of v4, /device:TPU:0, one launch (start us, length us, event | category | flops | bytes accessed | tf_op | source)
XLA Modules:
  0.0 775.3 jit_solution(15169312671286658790)
XLA Ops:
  9.1 2.1 concatenate.49
  11.8 1.2 copy.81
  13.0 1.2 copy.80
  14.2 1.2 copy.79
  15.3 1.4 fusion.5.refs_6_.refs_8_
  16.7 146.7 %ring_gather_0.1 = (bf16[2,16,64,576]{3,2,1,0:T(8,128)(2,1)}, bf16[2,16,64,3072]{3,2,1,0:T(8,128)(2,1)}, bf16[2,16,16,4096]{3,2,1,0:T(8,128)(2,1)}, bf16[2,16,16...) custom-call(bf16[64,576]{1,0:T(8,128)(2,1)} %refs_0_.1, ...), custom_call_target="tpu_custom_call" | custom-call | bytes 55312384 | tf_op jit(solution)/shard_map/ring_gather_0/pallas_call | solution.py:217
  165.2 1.5 collective-permute-start.1
  169.3 2.0 reshape_reshape.8.refs_4_
  172.3 7.7 fusion.47
  180.0 2.4 reshape.346
  182.4 2.9 fusion.48
  189.9 53.7 %ring_gather_1.1 = bf16[2,16,64,640]{3,2,1,0:T(8,128)(2,1)} custom-call(bf16[2,64,640]{2,1,0:T(8,128)(2,1)} %maximum_maximum_fusion.refs_0_), custom_call_target="tpu_custom_call" | custom-call | bytes 5242880 | tf_op jit(solution)/shard_map/ring_gather_1/pallas_call | solution.py:217
  244.9 1.3 copy_bitcast_fusion
  246.2 18.1 %attend.1 = (bf16[2,16,64,640]{3,2,1,0:T(8,128)(2,1)}, f32[2,16,64,1]{3,2,1,0:T(8,128)}, bf16[2,16,64,512]{3,2,1,0:T(8,128)(2,1)}, bf16[128,2048]{1,0:T(8,128)(2,1)}, f32[128,2048]{1,0:T(8,128)}) custom-call(bf16[128,2048]{1,0:T(8,128)(2,1)} %get-tuple-element.244.nope, bf16[128,2048]{1,0:T(8,128)(2,1)} %get-tuple-element.243.rope, ...), custom_call_target="tpu_custom_call" | custom-call | flops 4831838208 | bytes 31457280 | tf_op jit(solution)/shard_map/attend/pallas_call | solution.py:746
  264.2 1.4 multiply_reduce_fusion.4
  265.6 1.4 multiply_convert_fusion.1
  269.2 49.3 %ring_gather_2.1 = (bf16[2,16,64,2048]{3,2,1,0:T(8,128)(2,1)}, bf16[2,16,64,128]{3,2,1,0:T(8,128)(2,1)}) custom-call(bf16[2,64,2048]{2,1,0:T(8,128)(2,1)} %bitcast.124, bf16[2,64,128]{2,1,0:T(8,128)(2,1)} %bitcast.142), custom_call_target="tpu_custom_call" | custom-call | bytes 17825792 | tf_op jit(solution)/shard_map/ring_gather_2/pallas_call | solution.py:217
  318.5 79.2 %experts.1 = (bf16[2048,2048]{1,0:T(8,128)(2,1)}, bf16[2048,2048]{1,0:T(8,128)(2,1)}, bf16[2048,128]{1,0:T(8,128)(2,1)}, bf16[1024,2048]{1,0:T(8,128)(2,1)}, bf1...) custom-call(bf16[2048,2048]{1,0:T(8,128)(2,1)} %bitcast.102, ...), custom_call_target="tpu_custom_call" | custom-call | flops 52613349376 | bytes 41943040 | tf_op jit(solution)/shard_map/experts/pallas_call | solution.py:660
  397.7 55.8 %ring_reduce_3.1 = (f32[2,64,2048]{2,1,0:T(8,128)}, f32[2,64,128]{2,1,0:T(8,128)}, bf16[1024,512]{1,0:T(8,128)(2,1)}, bf16[1024,256]{1,0:T(8,128)(2,1)}, bf16[10...) custom-call(bf16[2,16,64,2048]{3,2,1,0:T(8,128)(2,1)} %bitcast.115, ...), custom_call_target="tpu_custom_call" | custom-call | bytes 1048576 | tf_op jit(solution)/shard_map/ring_reduce_3/pallas_call | solution.py:489
  455.7 2.0 multiply_reduce_fusion
  457.8 2.3 fusion.40.grad.refs_4_
  460.1 36.3 %attend_back.1 = (bf16[2,1024,640]{2,1,0:T(8,128)(2,1)}, f32[128,2048]{1,0:T(8,128)}, f32[2,16,64,128]{3,2,1,0:T(8,128)}, bf16[512,4096]{1,0:T(8,128)(2,1)}) custom-call(bf16[128,2048]{1,0:T(8,128)(2,1)} %fusion.40.grad.refs_4_, bf16[2048,2048]{1,0:T(8,128)(2,1)} %bitcast.114, bf16[512,4096]{1,0:T(8,128)(2,1)} %bitcast.121, ...), custom_call_target="tpu_custom_call" | custom-call | bytes 1048576 | tf_op jit(solution)/shard_map/attend_back/pallas_call | solution.py:825
  496.4 1.3 slice_bitcast_fusion
  499.2 1.3 maximum_convert_fusion
  500.5 2.9 convert_element_type.202.refs_3_
  505.2 2.5 reshape.381
  507.7 1.1 collective-permute-start.2
  510.9 40.9 %ring_reduce_4.1 = (f32[2,64,640]{2,1,0:T(8,128)}, bf16[2048,3072]{1,0:T(8,128)(2,1)}, bf16[2048,2048]{1,0:T(8,128)(2,1)}) custom-call(bf16[2,16,64,640]{3,2,1,0:T(8,128)(2,1)} %bitcast.122, bf16[128,2048]{1,0:T(8,128)(2,1)} %multiply_convert_fusion.refs_1_, bf16[128,2048]{1,0:T(8,128)(2,1)} %get-tuple-element.111.refs_2_, ...), custom_call_target="tpu_custom_call" | custom-call | bytes 1048576 | tf_op jit(solution)/shard_map/ring_reduce_4/pallas_call | solution.py:489
  551.8 9.9 %fusion.49 = f32[128,2048]{1,0:T(8,128)} fusion(bf16[128,3072]{1,0:T(8,128)(2,1)S(1)} %copy-done.3, bf16[2048,3072]{1,0:T(8,128)(2,1)} %bitcast.98), kind=kOutput, calls=%fused_computation.135 | convolution fusion | flops 1610612736 | bytes 14417920 | tf_op jit(solution)/shard_map/dot_general | solution.py:34
  561.9 1.7 slice.104
  563.6 1.2 fusion.26
  566.7 1.7 multiply_reduce_fusion.6
  569.6 2.9 convolution_convert_fusion
  572.5 4.5 copy.97
  577.1 4.1 multiply_reduce_fusion.1
  582.2 147.9 %ring_reduce_5.1 = (f32[64,3072]{1,0:T(8,128)}, f32[16,4096]{1,0:T(8,128)}, f32[64,576]{1,0:T(8,128)}, f32[16,128]{1,0:T(8,128)}, f32[64,2048]{1,0:T(8,128)}, /*...) custom-call(bf16[2,16,64,3072]{3,2,1,0:T(8,128)(2,1)} %bitcast.106, ...), custom_call_target="tpu_custom_call" | custom-call | bytes 1048576 | tf_op jit(solution)/shard_map/ring_reduce_5/pallas_call | solution.py:489
  730.9 1.2 slice.139
  732.8 1.3 fusion.43
  734.1 1.8 convert_add_fusion.3
  736.0 1.5 fusion.41
  737.4 2.4 copy.101
  739.8 2.4 copy.102
  742.2 2.1 convert_add_fusion.5
  744.3 2.4 copy.103
  746.7 5.9 convert_add_fusion.2
  752.6 5.1 convert_add_fusion.1
  757.7 5.1 convert_add_fusion
  762.9 2.1 multiply_add_fusion
  (190 shorter events, 31.8 us)
Async XLA Ops:
  7.2 311.4 %all-gather.2.cloned.1.call-start = ((), (), s32[]{:S(2)}) async-start(), calls=%async_computation.1 | async-start | bytes 8912896 | tf_op jit(solution)/shard_map/all_gather | solution.py:948
  16.7 146.7 %copy-start.5 = (bf16[2,64,2048]{2,1,0:T(8,128)(2,1)S(1)}, bf16[2,64,2048]{2,1,0:T(8,128)(2,1)}, u32[]{:S(2)}) copy-start(bf16[2,64,2048]{2,1,0:T(8,128)(2,1)} %param.20) | copy-start | bytes 1572868
  163.4 7.8 %copy-start.16 = (bf16[2,16,16,128]{3,2,1,0:T(8,128)(2,1)S(1)}, bf16[2,16,16,128]{3,2,1,0:T(8,128)(2,1)}, u32[]{:S(2)}) copy-start(bf16[2,16,16,128]{3,2,1,0:T(8,128)(2,1)} %get-tuple-element.82) | copy-start | bytes 393220
  163.5 8.1 %copy-start.1 = (bf16[2,64,2048]{2,1,0:T(8,128)(2,1)S(1)}, bf16[2,64,2048]{2,1,0:T(8,128)(2,1)}, u32[]{:S(2)}) copy-start(bf16[2,64,2048]{2,1,0:T(8,128)(2,1)} %param.19) | copy-start | bytes 1572868
  164.6 397.3 %reduce-scatter.2.cloned.1.call-start = ((), (), s32[]{:S(2)}) async-start(), calls=%async_computation.2 | async-start | bytes 8912896 | tf_op jit(solution)/shard_map/reduce_scatter | solution.py:1069
  164.6 153.9 %collective-permute-start = (bf16[1024,1408]{1,0:T(8,128)(2,1)}, bf16[1024,1408]{1,0:T(8,128)(2,1)}, u32[]{:S(2)}, u32[]{:S(2)}) collective-permute-start(bf16[1024,1408]{1,0:T(8,128)(2,1)} %refs_6_), channel_id=1, source_target_pairs={{0,16},{16,0},{1,17},{17,1},{2,18},{18,2},{3,19},{19,3},{4,20},{20... | collective-permute-start | bytes 8650760 | tf_op jit(solution)/shard_map/ppermute | solution.py:899
  165.2 153.3 %collective-permute-start.1 = (bf16[1024,1408]{1,0:T(8,128)(2,1)}, bf16[1024,1408]{1,0:T(8,128)(2,1)}, u32[]{:S(2)}, u32[]{:S(2)}) collective-permute-start(bf16[1024,1408]{1,0:T(8,128)(2,1)} %refs_7_), channel_id=1, source_target_pairs={{0,16},{16,0},{1,17},{17,1},{2,18},{18,2},{3,19},{19,3},{4,20},{20... | collective-permute-start | bytes 8650760 | tf_op jit(solution)/shard_map/ppermute | solution.py:899
  180.0 2.4 copy-start.26
  182.4 3.2 copy-start.41
  185.3 3.3 copy-start.4
  185.5 1.5 copy-start.37
  186.4 1.4 copy-start.27
  188.5 55.9 %copy-start.23 = (f32[512]{0:T(512)}, f32[512]{0:T(512)S(1)}, u32[]{:S(2)}) copy-start(f32[512]{0:T(512)S(1)} %reshape.407) | copy-start | bytes 6148
  188.6 378.1 %copy-start.33 = (f32[128]{0:T(128)}, f32[128]{0:T(128)S(1)}, u32[]{:S(2)}) copy-start(f32[128]{0:T(128)S(1)} %add_rsqrt_fusion.2) | copy-start | bytes 1540
  244.9 22.1 %copy-start.7 = (bf16[2048,16]{1,0:T(8,128)(2,1)}, bf16[2048,16]{1,0:T(8,128)(2,1)S(1)}, u32[]{:S(2)}) copy-start(bf16[2048,16]{1,0:T(8,128)(2,1)S(1)} %reshape.357) | copy-start | bytes 196612
  265.6 192.1 %copy-start.29 = (f32[128]{0:T(128)}, f32[128]{0:T(128)S(1)}, u32[]{:S(2)}) copy-start(f32[128]{0:T(128)S(1)} %add_rsqrt_fusion.1) | copy-start | bytes 1540
  453.5 0.7 copy-start.36
  453.5 1.0 copy-start.2
  453.6 2.0 copy-start.22
  453.6 2.1 copy-start
  454.3 1.3 copy-start.31
  457.7 38.7 %copy-start.39 = (f32[128]{0:T(128)}, f32[128]{0:T(128)S(1)}, u32[]{:S(2)}) copy-start(f32[128]{0:T(128)S(1)} %broadcast_multiply_fusion.1) | copy-start | bytes 1540
  497.7 1.3 copy-start.12
  505.2 46.6 %copy-start.3 = (bf16[128,3072]{1,0:T(8,128)(2,1)S(1)}, bf16[128,3072]{1,0:T(8,128)(2,1)}, u32[]{:S(2)}) copy-start(bf16[128,3072]{1,0:T(8,128)(2,1)} %convert_element_type.202.refs_3_) | copy-start | bytes 2359300
  507.7 226.4 %collective-permute-start.2 = (bf16[1024,1408]{1,0:T(8,128)(2,1)}, bf16[1024,1408]{1,0:T(8,128)(2,1)}, u32[]{:S(2)}, u32[]{:S(2)}) collective-permute-start(bf16[1024,1408]{1,0:T(8,128)(2,1)} %get-tuple-element.128), channel_id=1, source_target_pairs={{0,16},{16,0},{1,17},{17,1},{2,18},{18,2},{3,19},{19,3},{4,20},{20... | collective-permute-start | bytes 8650760 | tf_op jit(solution)/shard_map/ppermute | solution.py:1077
  508.9 225.2 %collective-permute-start.3 = (bf16[1024,1408]{1,0:T(8,128)(2,1)}, bf16[1024,1408]{1,0:T(8,128)(2,1)}, u32[]{:S(2)}, u32[]{:S(2)}) collective-permute-start(bf16[1024,1408]{1,0:T(8,128)(2,1)} %get-tuple-element.129), channel_id=1, source_target_pairs={{0,16},{16,0},{1,17},{17,1},{2,18},{18,2},{3,19},{19,3},{4,20},{20... | collective-permute-start | bytes 8650760 | tf_op jit(solution)/shard_map/ppermute | solution.py:1077
  509.8 224.3 %collective-permute-start.4 = (bf16[1024,1408]{1,0:T(8,128)(2,1)}, bf16[1024,1408]{1,0:T(8,128)(2,1)}, u32[]{:S(2)}, u32[]{:S(2)}) collective-permute-start(bf16[1024,1408]{1,0:T(8,128)(2,1)} %get-tuple-element.130), channel_id=1, source_target_pairs={{0,16},{16,0},{1,17},{17,1},{2,18},{18,2},{3,19},{19,3},{4,20},{20... | collective-permute-start | bytes 8650760 | tf_op jit(solution)/shard_map/ppermute | solution.py:1077
  551.8 11.8 %copy-start.28 = (f32[2,64]{1,0:T(2,128)S(1)}, f32[2,64]{1,0:T(2,128)}, u32[]{:S(2)}) copy-start(f32[2,64]{1,0:T(2,128)} %copy-done.27) | copy-start | bytes 1540
  551.8 11.8 %copy-start.38 = (f32[32]{0:T(128)S(1)}, f32[32]{0:T(128)}, u32[]{:S(2)}) copy-start(f32[32]{0:T(128)} %copy-done.37) | copy-start | bytes 388
  551.8 14.9 %copy-start.24 = (f32[512]{0:T(512)S(1)}, f32[512]{0:T(512)}, u32[]{:S(2)}) copy-start(f32[512]{0:T(512)} %copy-done.23) | copy-start | bytes 6148
  561.8 7.8 %copy-start.8 = (bf16[128,2048]{1,0:T(8,128)(2,1)S(1)}, bf16[128,2048]{1,0:T(8,128)(2,1)}, u32[]{:S(2)}) copy-start(bf16[128,2048]{1,0:T(8,128)(2,1)} %multiply_convert_fusion.refs_1_) | copy-start | bytes 1572868
  572.5 4.6 copy-start.21
  572.5 4.6 copy-start.32
  577.1 4.2 copy-start.34
  577.1 4.3 copy-start.18
  577.1 4.3 copy-start.25
  735.9 6.3 copy-start.17
  746.7 5.9 copy-start.11
  752.6 5.1 copy-start.10
  757.7 5.1 copy-start.6
  757.7 5.1 copy-start.9
  757.7 5.1 copy-start.14
  757.7 5.1 copy-start.30
  757.7 5.1 copy-start.40
  762.8 2.1 copy-start.13
  762.8 3.0 copy-start.20
  762.8 3.7 copy-start.19
  762.8 4.4 copy-start.15
  (1 other events, 0.6 us)
Sparse Core Ops, SparseCore 0:
  164.7 79.2 all-gather.1
  453.7 108.1 reduce-scatter.1

commit v5 on v4

--- a/solution.py
+++ b/solution.py
@@ -236,6 +236,194 @@
         cost_estimate=pl.CostEstimate(flops=0, bytes_accessed=2 * size, transcendentals=0),
         name="ring_gather_%d" % number,
     )(*arrays, *swaps)
+
+
+def front_kernel(ring, latent_part, *refs):
+    ins, swap_ins, (normed, cosine, sine) = refs[:5], refs[5:7], refs[7:10]
+    outs, swap_outs, (keys, hidden, latent) = refs[10:15], refs[15:17], refs[17:20]
+    small_held, kva_held, own_keys = refs[20:23]
+    own_sem, yss, yrs, rss, rrs, sss, srs, wss, wrs, load_sem = refs[23:]
+    f, c, core, p, way = ring.here()
+    n, nf = ring.chips, ring.nf
+    nc = 2 * n
+    greet(ring, f, c, core, p, way, True)
+    to_next, to_twin = (f, ring.device(p + way, core)), (f, c + 1 - 2 * core)
+    to_other, other = ((f + 1) % nf, c), (f + 1) % nf
+    started, own = [], {}
+
+    def remote(src, dst, ss, rs, dev):
+        return pltpu.make_async_remote_copy(
+            src_ref=src, dst_ref=dst, send_sem=ss, recv_sem=rs, device_id=dev, device_id_type=MESH
+        )
+
+    def place(number, owner):
+        if number < 10:
+            return outs[number // 2].at[(f + number % 2) % nf, owner]
+        return keys.at[number - 10, owner]
+
+    def send(s, number, owner, src, ring_too=True):
+        dst = place(number, owner)
+        if ring_too:
+            cp = remote(src, dst, rss.at[s, number], rrs.at[s, number], to_next)
+            cp.start()
+            started.append(cp)
+        cp = remote(src, dst, sss.at[s, number], srs.at[s, number], to_twin)
+        cp.start()
+        started.append(cp)
+
+    def keep(number, src):
+        own[number] = pltpu.make_async_copy(src, place(number, c), own_sem.at[number])
+        own[number].start()
+
+    def pass_on(s, number):
+        owner = ring.device(p - way * s, core)
+        here = place(number, owner)
+        remote(here, here, rss.at[s - 1, number], rrs.at[s - 1, number], to_next).wait_recv()
+        send(s, number, owner, here, s < n - 1)
+
+    def late(i):
+        here = outs[i].at[other, c]
+        remote(here, here, yss.at[i], yrs.at[i], to_next).wait_recv()
+        send(0, 2 * i + 1, c, here)
+
+    def from_twin(s, number):
+        here = place(number, ring.device(p + way * s, 1 - core))
+        remote(here, here, sss.at[s, number], srs.at[s, number], to_twin).wait_recv()
+
+    for i in range(5):
+        cp = remote(ins[i], outs[i].at[f, c], yss.at[i], yrs.at[i], to_other)
+        cp.start()
+        started.append(cp)
+        send(0, 2 * i, c, ins[i])
+        keep(2 * i, ins[i])
+    swapped = []
+
+    def swap():
+        for i in range(2):
+            cp = remote(swap_ins[i], swap_outs[i], wss.at[i], wrs.at[i], to_other)
+            cp.start()
+            swapped.append(cp)
+
+    bulk = [functools.partial(late, i) for i in (2, 3, 4)] + [swap]
+    bulk += [functools.partial(pass_on, s, number) for s in range(1, n) for number in range(4, 10)]
+
+    def some(count):
+        for work in bulk[:count]:
+            work()
+        del bulk[:count]
+
+    late(0)
+    late(1)
+    for s in range(1, n):
+        for number in range(4):
+            pass_on(s, number)
+        some(3)
+    for number in range(4):
+        for s in range(n):
+            from_twin(s, number)
+    for number in (0, 2):
+        own[number].wait()
+    loads = [
+        pltpu.make_async_copy(outs[i], held, load_sem.at[i])
+        for i, held in enumerate((small_held, kva_held))
+    ]
+    for cp in loads:
+        cp.start()
+    for cp in loads:
+        cp.wait()
+    lane = lax.broadcasted_iota(jnp.int32, (1, 128), 1)
+
+    def gain(row, first, each):
+        total = jnp.zeros((1, 128), F32)
+        for k in range(128 // each):
+            d = first // each + k
+            own_row = small_held[d // nc, d % nc, row : row + 1, :].astype(F32)
+            total = jnp.where(lane // each == k, own_row, total)
+        return total
+
+    for start in range(0, D, 128):
+        cut = slice(start, start + 128)
+        hidden[:, cut] = (normed[:, cut] * gain(0, start, D // (nf * nc))).astype(BF)
+    latent[:, LAT:] = jnp.zeros((latent.shape[0], 128), F32)
+    latent[:, : LAT + DR] = multiply(hidden[...], kva_held[...].reshape(D, LAT + DR))
+    trees, tok = own_keys.shape[:2]
+    low = latent[:, :LAT]
+    inverse = lax.rsqrt(jnp.mean(low * low, axis=-1, keepdims=True) + epsilon)
+    for start in range(0, LAT, 128):
+        cut = slice(start, start + 128)
+        key = (latent[:, cut] * inverse * gain(1, start, latent_part)).astype(BF)
+        for a in range(trees):
+            own_keys[a, :, cut] = key[a * tok : (a + 1) * tok]
+    half = DR // 2
+    former, latter = latent[:, LAT : LAT + half], latent[:, LAT + half : LAT + DR]
+    turned = (
+        (former * cosine[...] - latter * sine[...]).astype(BF),
+        (latter * cosine[...] + former * sine[...]).astype(BF),
+    )
+    own_keys[:, :, LAT:] = jnp.zeros((trees, tok, 128), BF)
+    for a in range(trees):
+        for k in range(2):
+            own_keys[a, :, LAT + k * half : LAT + (k + 1) * half] = turned[k][a * tok : (a + 1) * tok]
+    for a in range(trees):
+        send(0, 10 + a, c, own_keys.at[a])
+        keep(10 + a, own_keys.at[a])
+    for s in range(1, n):
+        some(3)
+        for a in range(trees):
+            pass_on(s, 10 + a)
+    some(len(bulk))
+    for number in range(4, 10 + trees):
+        for s in range(n):
+            from_twin(s, number)
+    for number in own:
+        if number not in (0, 2):
+            own[number].wait()
+    for cp in started:
+        cp.wait_send()
+    for cp in swapped:
+        cp.wait()
+
+
+def front(ring, number, arrays, swaps, normed, cosine, sine, latent_part, trees, tok):
+    n, nf = ring.chips, ring.nf
+    rows = normed.shape[0]
+    shapes = [jax.ShapeDtypeStruct((nf, 2 * n) + a.shape, a.dtype) for a in arrays]
+    size = sum(a.size * 2 for a in shapes)
+    shapes += [jax.ShapeDtypeStruct(a.shape, a.dtype) for a in swaps]
+    shapes += [
+        jax.ShapeDtypeStruct((trees, 2 * n, tok, LAT + 128), BF),
+        jax.ShapeDtypeStruct((rows, D), BF),
+        jax.ShapeDtypeStruct((rows, LAT + 128), F32),
+    ]
+    dma = pltpu.SemaphoreType.DMA
+    streams = 10 + trees
+    vmem, far = pl.BlockSpec(memory_space=pltpu.VMEM), pl.BlockSpec(memory_space=pl.ANY)
+    return pl.pallas_call(
+        functools.partial(front_kernel, ring, latent_part),
+        out_shape=shapes,
+        in_specs=[far] * 7 + [vmem] * 3,
+        out_specs=[far] * 8 + [vmem] * 2,
+        scratch_shapes=[
+            pltpu.VMEM(shapes[0].shape, BF),
+            pltpu.VMEM(shapes[1].shape, BF),
+            pltpu.VMEM((trees, tok, LAT + 128), BF),
+            dma((streams,)),
+            dma((5,)),
+            dma((5,)),
+            dma((n - 1, streams)),
+            dma((n - 1, streams)),
+            dma((n, streams)),
+            dma((n, streams)),
+            dma((2,)),
+            dma((2,)),
+            dma((2,)),
+        ],
+        compiler_params=pltpu.CompilerParams(
+            collective_id=number, has_side_effects=True, vmem_limit_bytes=32 << 20
+        ),
+        cost_estimate=pl.CostEstimate(flops=0, bytes_accessed=2 * size, transcendentals=0),
+        name="front",
+    )(*arrays, *swaps, normed, cosine, sine)
 
 
 def add_rows(shape, work):
@@ -700,17 +888,45 @@
 HEADS = 4
 
 
-def attend_kernel(scale, nope, rope, keys, allowed, expand, tokens, w_hbm, cat, lse, mixed, heads, residual, w_out, sem):
+def attend_kernel(
+    scale, hidden, cosine, sine, keys, allowed, expand, tokens, wq_hbm, wo_hbm,
+    cat, lse, mixed, heads, residual, nope, w_out, w_part, query, sem, part_sem,
+):
     trees, tok = cat.shape[0], cat.shape[2]
-    copy = pltpu.make_async_copy(w_hbm, w_out, sem)
-    copy.start()
-    for h in range(H):
-        low = nt(nope[:, h * DN : (h + 1) * DN], expand[:, h * (DN + DV) : h * (DN + DV) + DN])
-        low = low.astype(BF)
-        for b in range(trees):
-            rows = slice(b * tok, (b + 1) * tok)
-            cat[b, h, :, :LAT] = low[rows]
-            cat[b, h, :, LAT:] = rope[rows, h * 128 : (h + 1) * 128]
+    copy = pltpu.make_async_copy(wo_hbm, w_out, sem)
+    pair = 2 * (DN + DR)
+
+    def part(i):
+        return pltpu.make_async_copy(
+            wq_hbm.at[:, pl.ds(i * pair, pair)], w_part.at[i % 2], part_sem.at[i % 2]
+        )
+
+    part(0).start()
+    cat[:, :, :, LAT + DR :] = jnp.zeros((trees, H, tok, 128 - DR), BF)
+    half = DR // 2
+    for i in range(H // 2):
+        part(i).wait()
+        if i + 1 < H // 2:
+            part(i + 1).start()
+        else:
+            copy.start()
+        query[...] = multiply(hidden[...], w_part[i % 2])
+        for h in (2 * i, 2 * i + 1):
+            first = h % 2 * (DN + DR)
+            nope[:, h * DN : (h + 1) * DN] = query[:, first : first + DN].astype(BF)
+            former = query[:, first + DN : first + DN + half]
+            latter = query[:, first + DN + half : first + DN + DR]
+            turned = (
+                (former * cosine[...] - latter * sine[...]).astype(BF),
+                (latter * cosine[...] + former * sine[...]).astype(BF),
+            )
+            low = nt(nope[:, h * DN : (h + 1) * DN], expand[:, h * (DN + DV) : h * (DN + DV) + DN])
+            low = low.astype(BF)
+            for b in range(trees):
+                rows = slice(b * tok, (b + 1) * tok)
+                cat[b, h, :, :LAT] = low[rows]
+                cat[b, h, :, LAT : LAT + half] = turned[0][rows]
+                cat[b, h, :, LAT + half : LAT + DR] = turned[1][rows]
 
     def group(i, carry):
         b, g = i // (H // HEADS), i % (H // HEADS) * HEADS
@@ -738,10 +954,10 @@
         residual[:, cut] = tokens[:, cut].astype(F32) + multiply(heads[...], w_out[:, cut])
 
 
-def attend(nope, rope, keys, allowed, expand, tokens, w_output, tok, scale):
+def attend(hidden, cosine, sine, keys, allowed, expand, tokens, w_query, w_output, tok, scale):
     rows = tokens.shape[0]
     trees = rows // tok
-    vmem = pl.BlockSpec(memory_space=pltpu.VMEM)
+    vmem, far = pl.BlockSpec(memory_space=pltpu.VMEM), pl.BlockSpec(memory_space=pl.ANY)
     length, width = keys.shape[1:]
     return pl.pallas_call(
         functools.partial(attend_kernel, scale),
@@ -751,16 +967,23 @@
             jax.ShapeDtypeStruct((trees, H, tok, LAT), BF),
             jax.ShapeDtypeStruct((rows, H * DV), BF),
             jax.ShapeDtypeStruct((rows, D), F32),
+            jax.ShapeDtypeStruct((rows, H * DN), BF),
         ],
-        in_specs=[vmem] * 6 + [pl.BlockSpec(memory_space=pl.ANY)],
-        out_specs=[vmem] * 5,
-        scratch_shapes=[pltpu.VMEM(w_output.shape, BF), pltpu.SemaphoreType.DMA],
+        in_specs=[vmem] * 7 + [far] * 2,
+        out_specs=[vmem] * 6,
+        scratch_shapes=[
+            pltpu.VMEM(w_output.shape, BF),
+            pltpu.VMEM((2, D, 2 * (DN + DR)), BF),
+            pltpu.VMEM((rows, 2 * (DN + DR)), F32),
+            pltpu.SemaphoreType.DMA,
+            pltpu.SemaphoreType.DMA((2,)),
+        ],
         compiler_params=pltpu.CompilerParams(vmem_limit_bytes=56 << 20),
         cost_estimate=pl.CostEstimate(
             flops=2 * rows * H * length * 1152, bytes_accessed=30 << 20, transcendentals=rows * H * length
         ),
         name="attend",
-    )(nope, rope, keys, allowed, expand, tokens, w_output)
+    )(hidden, cosine, sine, keys, allowed, expand, tokens, w_query, w_output)
 
 
 def attend_back_kernel(
@@ -904,8 +1127,21 @@
     shared_w = jnp.concatenate(
         [jnp.pad(w, ((0, 0), (0, fp - fs))) for w in (shared_gate, shared_up, shared_down)], axis=1
     )
+    def one_mask(segment_ids, path_table):
+        return tree_mask(segment_ids, path_table, first_row, tok_loc)
+
+    allowed, positions = jax.vmap(one_mask)(segments, path_mask)
+    rotation = positions.astype(F32)[:, :, None] * frequency[None, None, :]
+    cosine, sine = jnp.cos(rotation), jnp.sin(rotation)
+    inputs = tokens.astype(F32).reshape(row_total, D)
+    inverse_in = lax.rsqrt(jnp.mean(inputs * inputs, axis=-1, keepdims=True) + epsilon)
+    normed_in = inputs * inverse_in
+
+    r_one, r_lat, r_router = norm_attn.shape[0], norm_latent.shape[0], router.size
     small = jnp.concatenate(
         [
+            jnp.tile(norm_attn, 128 // r_one),
+            jnp.tile(norm_latent, 128 // r_lat),
             norm_attn,
             norm_ffn,
             norm_latent,
@@ -913,33 +1149,41 @@
             expert_ids.astype(BF).reshape(-1),
         ]
     )
-    small = jnp.pad(small, (0, PACK - small.shape[0])).reshape(16, PACK // 16)
+    small = jnp.pad(small, (0, 2 * PACK - small.shape[0])).reshape(2 * PACK // 128, 128)
     if nf == 2:
-        w_latent, w_query, w_expand, small_all, w_output, other_gate, other_shared = ring_gather(
-            ring, 0, [attn_kva, attn_q, attn_kvb, small, attn_out], [True] * 5, [expert_gate, shared_w]
-        )
-        e_gate, s_all = [expert_gate, other_gate], [shared_w, other_shared]
-        later_up, later_down, later_grads, small_all = lax.optimization_barrier(
-            (expert_up, expert_down, out_grad, small_all)
+        small_all, w_latent, w_query, w_expand, w_output, other_gate, other_up, keys, hidden_in, latent_all = front(
+            ring,
+            0,
+            [small, attn_kva, attn_q, attn_kvb, attn_out],
+            [expert_gate, expert_up],
+            normed_in,
+            cosine.reshape(row_total, -1),
+            sine.reshape(row_total, -1),
+            r_lat,
+            trees,
+            tok_loc,
+        )
+        e_gate, e_up = [expert_gate, other_gate], [expert_up, other_up]
+        later_shared, later_down, later_grads, small_all = lax.optimization_barrier(
+            (shared_w, expert_down, out_grad, small_all)
         )
     else:
         w_latent, w_query, w_expand, small_all, w_output = (
             lax.all_gather(w, both, axis=0) for w in (attn_kva, attn_q, attn_kvb, small, attn_out)
         )
-        e_gate, s_all = fetch(expert_gate), fetch(shared_w)
-        later_up, later_down, later_grads = expert_up, expert_down, out_grad
-    e_up, e_down = fetch(later_up), fetch(later_down)
+        e_gate, e_up = fetch(expert_gate), fetch(expert_up)
+        later_shared, later_down, later_grads = shared_w, expert_down, out_grad
+    s_all, e_down = fetch(later_shared), fetch(later_down)
     w_output = w_output.reshape(H * DV, D)
     w_latent, w_query = w_latent.reshape(D, -1), w_query.reshape(D, -1)
     w_expand = w_expand.reshape(LAT, -1)
-    small_all = small_all.reshape(nf * nc, PACK)
-    r_one, r_lat, r_router = norm_attn.shape[0], norm_latent.shape[0], router.size
+    small_all = small_all.reshape(nf * nc, 2 * PACK)[:, 256:]
     cuts = [0, r_one, 2 * r_one, 2 * r_one + r_lat, 2 * r_one + r_lat + r_router]
     gain_attn = small_all[:, cuts[0] : cuts[1]].reshape(-1).astype(F32)
     gain_ffn = small_all[:, cuts[1] : cuts[2]].reshape(-1).astype(F32)
     gain_latent = small_all[:, cuts[2] : cuts[3]].reshape(-1).astype(F32)
     w_router = small_all[:, cuts[3] : cuts[4]].reshape(D, experts)
-    ids_all = lax.dynamic_slice_in_dim(small_all.reshape(nf, nc, PACK), group, 1, 0)[0]
+    ids_all = lax.dynamic_slice_in_dim(small_all.reshape(nf, nc, -1), group, 1, 0)[0]
     ids_all = ids_all[:, cuts[4] : cuts[4] + expert_ids.size].reshape(nc, trees, tok_loc, TOP)
     ids_all = ids_all.transpose(1, 0, 2, 3).reshape(group_rows, TOP)
 
@@ -947,39 +1191,28 @@
     upstream = upstream_low.astype(F32)
     tree_grads = lax.all_gather(roll_in(later_grads), "ctx", axis=1, tiled=True).reshape(group_rows, D)
 
-    def one_mask(segment_ids, path_table):
-        return tree_mask(segment_ids, path_table, first_row, tok_loc)
-
-    allowed, positions = jax.vmap(one_mask)(segments, path_mask)
-    rotation = positions.astype(F32)[:, :, None] * frequency[None, None, :]
-    cosine, sine = jnp.cos(rotation), jnp.sin(rotation)
-    inputs = tokens.astype(F32).reshape(row_total, D)
-    normed_in, inverse_in, gained_in = normalize(inputs, gain_attn)
-    hidden_in = gained_in.astype(BF)
-    latent_all = multiply(hidden_in, w_latent)
+    if nf != 2:
+        hidden_in = (normed_in * gain_attn).astype(BF)
+        latent_all = multiply(hidden_in, w_latent)
     latent_normed, latent_inverse, latent_gained = normalize(latent_all[:, :LAT], gain_latent)
-    key_latent = latent_gained.astype(BF).reshape(trees, tok_loc, LAT)
-    key_rope = rotate(latent_all[:, LAT:].reshape(trees, tok_loc, DR), cosine, sine).astype(BF)
-    key_pad = jnp.zeros((trees, tok_loc, 128 - DR), BF)
-    (keys,) = ring_gather(
-        ring, 1, [jnp.concatenate([key_latent, key_rope, key_pad], axis=-1)], [False]
-    )
+    if nf != 2:
+        key_latent = latent_gained.astype(BF).reshape(trees, tok_loc, LAT)
+        key_rope = rotate(latent_all[:, LAT:].reshape(trees, tok_loc, DR), cosine, sine).astype(BF)
+        key_pad = jnp.zeros((trees, tok_loc, 128 - DR), BF)
+        (keys,) = ring_gather(
+            ring, 1, [jnp.concatenate([key_latent, key_rope, key_pad], axis=-1)], [False]
+        )
     keys = keys.reshape(trees, tree_len, LAT + 128)
-    query_all = lax.optimization_barrier(multiply(hidden_in, w_query))
-    query_all = query_all.reshape(trees, tok_loc, H, DN + DR)
-    query_nope = query_all[..., :DN].astype(BF).reshape(row_total, H * DN)
-    query_rope = rotate(
-        query_all[..., DN:], cosine[:, :, None, :], sine[:, :, None, :]
-    ).astype(BF)
-    query_rope = jnp.pad(query_rope, ((0, 0), (0, 0), (0, 0), (0, 128 - DR)))
     allowed = allowed.astype(F32)
-    query_cat, log_total, mixed, heads, residual = attend(
-        query_nope,
-        query_rope.reshape(row_total, H * 128),
+    query_cat, log_total, mixed, heads, residual, query_nope = attend(
+        hidden_in,
+        cosine.reshape(row_total, -1),
+        sine.reshape(row_total, -1),
         keys,
         allowed,
         w_expand,
         tokens.reshape(row_total, D),
+        w_query,
         w_output,
         tok_loc,
         score_scale,

time: 783 us -> 757 us (0.967)
  matrix products: 30.7 us -> 19.4 us
    pallas_call x3 -> x1, Pallas kernels: 250 us -> 70.5 us  [ring_gather(): pl.pallas_call(functools.partial(gather_kernel, ring, tuple(wide), tuple(...]
    pallas_call x0 -> x1, Pallas kernels: none -> 158 us  [front(): pl.pallas_call(functools.partial(front_kernel, ring, latent_part), out_sh...]
    pallas_call x1, Pallas kernels: 18.1 us -> 29.6 us  [attend(): pl.pallas_call(functools.partial(attend_kernel, scale), out_shape=[jax.Sh...]
    unnamed x103 -> x98, local copies, waits for them, and re-layouts: 18.2 us -> 28.8 us
    dot_general x4 -> x2, matrix products: 11 us -> 0.44 us  [multiply(): return jnp.dot(left, right, preferred_element_type=F32)]
    add x5 -> x4, other arithmetic: 20 us -> 15.9 us  [body(): ffn_sums = [a.astype(F32) + b.astype(F32) for a, b in zip(ffn_sums, one)]]
  transfers between devices with their start and end apart: 7 -> 7, of which waited for: 1 -> 1; matrix products, arithmetic and copies ran while one was open for 10% -> 6% of each run, Pallas kernels for 45% -> 44%
where the time goes in v5:
time: 757 us; the launch traced here: 750 us
  Pallas kernels  622 us (82%)
  local copies, waits for them, and re-layouts  50.7 us (7%)
  other arithmetic  36.5 us (5%)
  matrix products  19.4 us (3%)
  between operations  15.2 us (2%)
    pallas_call x3, Pallas kernels, ring_reduce(): pl.pallas_call(functools.partial(reduce_kernel, ring, tuple(wide), tuple(...  248 us
    pallas_call x1, Pallas kernels, front(): pl.pallas_call(functools.partial(front_kernel, ring, latent_part), out_sh...  158 us
    pallas_call x1, Pallas kernels, run_experts(): pl.pallas_call(functools.partial(expert_kernel, nf, experts, fp, bundle_s...  79.2 us
    pallas_call x1, Pallas kernels, ring_gather(): pl.pallas_call(functools.partial(gather_kernel, ring, tuple(wide), tuple(...  70.5 us
    pallas_call x1, Pallas kernels, attend_back(): pl.pallas_call(functools.partial(attend_back_kernel, scale), out_shape=[j...  36.3 us
    pallas_call x1, Pallas kernels, attend(): pl.pallas_call(functools.partial(attend_kernel, scale), out_shape=[jax.Sh...  29.6 us
    unnamed x98, local copies, waits for them, and re-layouts  28.8 us
    dot_general x4, matrix products, multiply_transposed(): lax.dot_general(left, right, (((1,), (1,)), ((), ())), preferred_element_...  17.1 us
  transfers between devices with their start and end apart: 7, of which 1 were waited for; matrix products, arithmetic and copies ran while one was open for 6% of the time, Pallas kernels for 44%

profile of v5, /device:TPU:0, one launch (start us, length us, event | category | flops | bytes accessed | tf_op | source)
XLA Modules:
  0.0 750.4 jit_solution(18412471649677434396)
XLA Ops:
  8.0 1.2 multiply_reduce_fusion.5
  12.7 2.1 concatenate.39
  15.7 1.3 convert_reduce_fusion
  17.0 2.0 copy.66
  20.0 2.1 copy.68
  22.2 1.2 bitcast_multiply_fusion.refs_7_
  23.8 2.8 fusion.5.refs_8_
  26.6 1.8 copy-done.4
  28.4 158.0 %front.1 = (bf16[2,16,32,128]{3,2,1,0:T(8,128)(2,1)S(1)}, bf16[2,16,64,576]{3,2,1,0:T(8,128)(2,1)S(1)}, bf16[2,16,64,3072]{3,2,1,0:T(8,128)(2,1)}, bf16[2,16,16,...) custom-call(bf16[32,128]{1,0:T(8,128)(2,1)S(1)} %pad_bitcast_fusion., ...), custom_call_target="tpu_custom_call" | custom-call | bytes 55574528 | tf_op jit(solution)/shard_map/front/pallas_call | solution.py:401
  186.5 1.6 copy-done
  188.9 1.5 copy-done.5
  191.8 1.6 copy-done.16
  193.4 1.6 copy-done.17
  195.0 2.0 fusion.12
  197.8 1.6 collective-permute-start
  202.3 2.1 reshape_reshape.4.refs_4_
  205.8 29.6 %attend.1 = (bf16[2,16,64,640]{3,2,1,0:T(8,128)(2,1)}, f32[2,16,64,1]{3,2,1,0:T(8,128)}, bf16[2,16,64,512]{3,2,1,0:T(8,128)(2,1)}, bf16[128,2048]{1,0:T(8,128)(2...) custom-call(bf16[128,2048]{1,0:T(8,128)(2,1)} %copy-done.1, f32[128,32]{1,0:T(8,128)} %copy-done.10, ...), custom_call_target="tpu_custom_call" | custom-call | flops 4831838208 | bytes 31457280 | tf_op jit(solution)/shard_map/attend/pallas_call | solution.py:962
  235.5 1.4 multiply_reduce_fusion.4
  236.9 1.4 multiply_convert_fusion
  239.4 1.1 fusion.13
  240.5 70.5 %ring_gather_2.1 = (bf16[2,16,64,2048]{3,2,1,0:T(8,128)(2,1)}, bf16[2,16,64,128]{3,2,1,0:T(8,128)(2,1)}) custom-call(bf16[2,64,2048]{2,1,0:T(8,128)(2,1)} %bitcast.112, bf16[2,64,128]{2,1,0:T(8,128)(2,1)} %bitcast.128), custom_call_target="tpu_custom_call" | custom-call | bytes 17825792 | tf_op jit(solution)/shard_map/ring_gather_2/pallas_call | solution.py:217
  311.1 79.2 %experts.1 = (bf16[2048,2048]{1,0:T(8,128)(2,1)}, bf16[2048,2048]{1,0:T(8,128)(2,1)}, bf16[2048,128]{1,0:T(8,128)(2,1)}, bf16[1024,2048]{1,0:T(8,128)(2,1)}, bf1...) custom-call(bf16[2048,2048]{1,0:T(8,128)(2,1)} %bitcast.98, ...), custom_call_target="tpu_custom_call" | custom-call | flops 52613349376 | bytes 41943040 | tf_op jit(solution)/shard_map/experts/pallas_call | solution.py:848
  390.3 56.7 %ring_reduce_3.1 = (f32[2,64,2048]{2,1,0:T(8,128)}, f32[2,64,128]{2,1,0:T(8,128)}, bf16[1024,512]{1,0:T(8,128)(2,1)}, bf16[1024,256]{1,0:T(8,128)(2,1)}, bf16[10...) custom-call(bf16[2,16,64,2048]{3,2,1,0:T(8,128)(2,1)} %bitcast.107, ...), custom_call_target="tpu_custom_call" | custom-call | bytes 1048576 | tf_op jit(solution)/shard_map/ring_reduce_3/pallas_call | solution.py:677
  448.6 2.0 multiply_reduce_fusion
  451.1 1.4 reshape.357
  452.5 2.2 fusion.27.grad.refs_4_
  454.7 36.3 %attend_back.1 = (bf16[2,1024,640]{2,1,0:T(8,128)(2,1)}, f32[128,2048]{1,0:T(8,128)}, f32[2,16,64,128]{3,2,1,0:T(8,128)}, bf16[512,4096]{1,0:T(8,128)(2,1)}) custom-call(bf16[128,2048]{1,0:T(8,128)(2,1)} %fusion.27.grad.refs_4_, bf16[2048,2048]{1,0:T(8,128)(2,1)} %bitcast.94, bf16[512,4096]{1,0:T(8,128)(2,1)} %bitcast.102, ...), custom_call_target="tpu_custom_call" | custom-call | bytes 1048576 | tf_op jit(solution)/shard_map/attend_back/pallas_call | solution.py:1048
  491.0 1.5 copy.85
  492.5 1.3 slice_bitcast_fusion
  495.3 2.0 convert_element_type.184.refs_3_
  498.2 1.2 collective-permute-start.3
  500.2 42.7 %ring_reduce_4.1 = (f32[2,64,640]{2,1,0:T(8,128)}, bf16[2048,3072]{1,0:T(8,128)(2,1)}, bf16[2048,2048]{1,0:T(8,128)(2,1)}) custom-call(bf16[2,16,64,640]{3,2,1,0:T(8,128)(2,1)} %bitcast.110, bf16[128,2048]{1,0:T(8,128)(2,1)} %copy-done.1, bf16[128,2048]{1,0:T(8,128)(2,1)} %get-tuple-element.117.refs_2_, bf16[128,3072]{1,0:T(8,128)(2,1)} %convert_element_type.184.refs_3_, ...), custom_call_target="tpu_custom_call" | custom-call | bytes 1048576 | tf_op jit(solution)/shard_map/ring_reduce_4/pallas_call | solution.py:677
  542.9 10.3 %fusion.33 = f32[128,2048]{1,0:T(8,128)} fusion(bf16[128,3072]{1,0:T(8,128)(2,1)} %convert_element_type.184.refs_3_, bf16[2048,3072]{1,0:T(8,128)(2,1)} %bitcast.92), kind=kOutput, calls=%fused_computation.114 | convolution fusion | flops 1610612736 | bytes 14417920 | tf_op jit(solution)/shard_map/dot_general | solution.py:34
  553.3 1.4 reduce-scatter.2.cloned.1.call-done
  555.5 3.4 multiply_reduce_fusion.1
  560.0 1.7 convolution_convert_fusion
  561.7 2.6 copy.76
  564.3 148.7 %ring_reduce_5.1 = (f32[64,3072]{1,0:T(8,128)}, f32[16,4096]{1,0:T(8,128)}, f32[64,576]{1,0:T(8,128)}, f32[16,128]{1,0:T(8,128)}, f32[64,2048]{1,0:T(8,128)}, /*...) custom-call(bf16[2,16,64,3072]{3,2,1,0:T(8,128)(2,1)} %bitcast.104, ...), custom_call_target="tpu_custom_call" | custom-call | bytes 1048576 | tf_op jit(solution)/shard_map/ring_reduce_5/pallas_call | solution.py:677
  713.9 1.2 slice.113
  715.1 1.3 fusion.29
  717.1 1.3 convert_add_fusion.5
  718.5 1.2 copy.81
  720.1 1.2 copy.80
  721.3 1.2 copy.79
  722.5 5.9 convert_add_fusion.2
  728.5 2.1 multiply_add_fusion
  730.6 1.1 copy-done.27
  731.7 8.4 %convert_add_fusion = (f32[1024,1408]{1,0:T(8,128)}, f32[1024,1408]{1,0:T(8,128)}) fusion(bf16[1024,1408]{1,0:T(8,128)(2,1)} %collective-permute-done.4, bf16[1024,1408]{1,0:T(8,128)(2,1)S(1)} %copy-done.27, bf16[1024,1408]{1,0:T(8,128)(2,1)} %collective-permute-done.3, bf16[1024,1408]{1,0:T(8,128)(2,1)S(1)} %copy-done.26), kind=kLoop, calls=%fused_computation | loop fusion | flops 8650752 | bytes 23068672 | tf_op jit(solution)/shard_map/add | solution.py:1399
  (170 shorter events, 27.1 us)
Async XLA Ops:
  7.2 11.9 %copy-start.35 = (bf16[1024,176]{0,1:T(8,128)(2,1)S(1)}, bf16[1024,176]{0,1:T(8,128)(2,1)}, u32[]{:S(2)}) copy-start(bf16[1024,176]{0,1:T(8,128)(2,1)} %param.36) | copy-start | bytes 1081348
  7.2 303.9 %all-gather.2.cloned.1.call-start = ((), (), s32[]{:S(2)}) async-start(), calls=%async_computation.1 | async-start | bytes 8912896 | tf_op jit(solution)/shard_map/all_gather | solution.py:1192
  20.0 6.5 copy-start.3
  20.0 6.5 copy-start.12
  20.0 6.5 copy-start.14
  20.0 6.5 copy-start.15
  22.2 4.4 copy-start.11
  23.7 162.7 %copy-start.9 = (f32[128,32]{1,0:T(8,128)}, f32[128,32]{1,0:T(8,128)S(1)}, u32[]{:S(2)}) copy-start(f32[128,32]{1,0:T(8,128)S(1)} %get-tuple-element.236.refs_9_.sine) | copy-start | bytes 49156
  23.7 162.7 %copy-start.10 = (f32[128,32]{1,0:T(8,128)}, f32[128,32]{1,0:T(8,128)S(1)}, u32[]{:S(2)}) copy-start(f32[128,32]{1,0:T(8,128)S(1)} %get-tuple-element.237.refs_8_.cosine) | copy-start | bytes 49156
  26.6 1.8 copy-start.4
  186.5 1.6 copy-start
  188.1 0.8 copy-start.1
  188.8 1.5 copy-start.5
  190.4 0.7 copy-start.7
  191.1 0.7 copy-start.13
  191.8 1.6 copy-start.16
  193.4 1.6 copy-start.17
  197.0 357.7 %reduce-scatter.2.cloned.1.call-start = ((), (), s32[]{:S(2)}) async-start(), calls=%async_computation.2 | async-start | bytes 8912896 | tf_op jit(solution)/shard_map/reduce_scatter | solution.py:1302
  197.3 113.7 %collective-permute-start.1 = (bf16[1024,768]{1,0:T(8,128)(2,1)}, bf16[1024,768]{1,0:T(8,128)(2,1)}, u32[]{:S(2)}, u32[]{:S(2)}) collective-permute-start(bf16[1024,768]{1,0:T(8,128)(2,1)} %fusion.5.refs_8_), channel_id=1, source_target_pairs={{0,16},{16,0},{1,17},{17,1},{2,18},{18,2},{3,19},{19,3},{4,20},{20... | collective-permute-start | bytes 4718600 | tf_op jit(solution)/shard_map/ppermute | solution.py:1122
  197.8 113.2 %collective-permute-start = (bf16[1024,1408]{1,0:T(8,128)(2,1)}, bf16[1024,1408]{1,0:T(8,128)(2,1)}, u32[]{:S(2)}, u32[]{:S(2)}) collective-permute-start(bf16[1024,1408]{1,0:T(8,128)(2,1)} %refs_7_), channel_id=1, source_target_pairs={{0,16},{16,0},{1,17},{17,1},{2,18},{18,2},{3,19},{19,3},{4,20},{20... | collective-permute-start | bytes 8650760 | tf_op jit(solution)/shard_map/ppermute | solution.py:1122
  205.8 32.5 %copy-start.24 = (bf16[2048,16]{1,0:T(8,128)(2,1)}, bf16[2048,16]{1,0:T(8,128)(2,1)S(1)}, u32[]{:S(2)}) copy-start(bf16[2048,16]{1,0:T(8,128)(2,1)S(1)} %reshape.332) | copy-start | bytes 196612
  447.0 1.0 copy-start.8
  447.0 1.4 copy-start.39
  447.0 1.5 copy-start.18
  450.6 40.5 %copy-start.21 = (f32[128,2048]{1,0:T(8,128)}, f32[128,2048]{1,0:T(8,128)S(1)}, u32[]{:S(2)}) copy-start(f32[128,2048]{1,0:T(8,128)S(1)} %get-tuple-element.242) | copy-start | bytes 3145732
  497.3 219.1 %collective-permute-start.2 = (bf16[1024,1408]{1,0:T(8,128)(2,1)}, bf16[1024,1408]{1,0:T(8,128)(2,1)}, u32[]{:S(2)}, u32[]{:S(2)}) collective-permute-start(bf16[1024,1408]{1,0:T(8,128)(2,1)} %get-tuple-element.136), channel_id=1, source_target_pairs={{0,16},{16,0},{1,17},{17,1},{2,18},{18,2},{3,19},{19,3},{4,20},{20... | collective-permute-start | bytes 8650760 | tf_op jit(solution)/shard_map/ppermute | solution.py:1310
  498.2 218.3 %collective-permute-start.3 = (bf16[1024,1408]{1,0:T(8,128)(2,1)}, bf16[1024,1408]{1,0:T(8,128)(2,1)}, u32[]{:S(2)}, u32[]{:S(2)}) collective-permute-start(bf16[1024,1408]{1,0:T(8,128)(2,1)} %get-tuple-element.137), channel_id=1, source_target_pairs={{0,16},{16,0},{1,17},{17,1},{2,18},{18,2},{3,19},{19,3},{4,20},{20... | collective-permute-start | bytes 8650760 | tf_op jit(solution)/shard_map/ppermute | solution.py:1310
  499.4 217.1 %collective-permute-start.4 = (bf16[1024,1408]{1,0:T(8,128)(2,1)}, bf16[1024,1408]{1,0:T(8,128)(2,1)}, u32[]{:S(2)}, u32[]{:S(2)}) collective-permute-start(bf16[1024,1408]{1,0:T(8,128)(2,1)} %get-tuple-element.138), channel_id=1, source_target_pairs={{0,16},{16,0},{1,17},{17,1},{2,18},{18,2},{3,19},{19,3},{4,20},{20... | collective-permute-start | bytes 8650760 | tf_op jit(solution)/shard_map/ppermute | solution.py:1310
  542.9 11.8 %copy-start.34 = (f32[2,64,640]{2,1,0:T(8,128)S(1)}, f32[2,64,640]{2,1,0:T(8,128)}, u32[]{:S(2)}) copy-start(f32[2,64,640]{2,1,0:T(8,128)} %get-tuple-element.124) | copy-start | bytes 983044
  542.9 12.6 %copy-start.6 = (bf16[2,16,64,576]{3,2,1,0:T(8,128)(2,1)S(1)}, bf16[2,16,64,576]{3,2,1,0:T(8,128)(2,1)}, u32[]{:S(2)}) copy-start(bf16[2,16,64,576]{3,2,1,0:T(8,128)(2,1)} %copy-done.5) | copy-start | bytes 7077892
  555.5 3.5 copy-start.28
  555.5 3.6 copy-start.36
  555.5 4.4 copy-start.2
  713.0 6.7 copy-start.29
  713.0 6.7 copy-start.30
  722.5 6.0 copy-start.19
  722.5 6.0 copy-start.20
  722.5 6.0 copy-start.22
  722.5 6.0 copy-start.23
  722.5 6.0 copy-start.25
  722.5 6.0 copy-start.32
  728.4 2.1 copy-start.26
  728.5 3.2 copy-start.27
  731.7 8.4 %copy-start.31 = (f32[64,3072]{1,0:T(8,128)S(1)}, f32[64,3072]{1,0:T(8,128)}, u32[]{:S(2)}) copy-start(f32[64,3072]{1,0:T(8,128)} %get-tuple-element.265) | copy-start | bytes 2359300
  731.7 9.3 %copy-start.38 = (f32[64,576]{1,0:T(8,128)S(1)}, f32[64,576]{1,0:T(8,128)}, u32[]{:S(2)}) copy-start(f32[64,576]{1,0:T(8,128)} %get-tuple-element.266) | copy-start | bytes 442372
  731.7 9.9 %copy-start.37 = (f32[16,4096]{1,0:T(8,128)S(1)}, f32[16,4096]{1,0:T(8,128)}, u32[]{:S(2)}) copy-start(f32[16,4096]{1,0:T(8,128)} %get-tuple-element.268) | copy-start | bytes 786436
  731.7 10.6 %copy-start.33 = (f32[64,2048]{1,0:T(8,128)S(1)}, f32[64,2048]{1,0:T(8,128)}, u32[]{:S(2)}) copy-start(f32[64,2048]{1,0:T(8,128)} %get-tuple-element.269) | copy-start | bytes 1572868
Sparse Core Ops, SparseCore 0:
  197.1 81.1 all-gather.1
  447.2 107.4 reduce-scatter.1

commit v6 on v5

--- a/solution.py
+++ b/solution.py
@@ -419,7 +419,7 @@
             dma((2,)),
         ],
         compiler_params=pltpu.CompilerParams(
-            collective_id=number, has_side_effects=True, vmem_limit_bytes=32 << 20
+            collective_id=number, has_side_effects=True, vmem_limit_bytes=60 << 20
         ),
         cost_estimate=pl.CostEstimate(flops=0, bytes_accessed=2 * size, transcendentals=0),
         name="front",
@@ -987,10 +987,20 @@
 
 
 def attend_back_kernel(
-    scale, grad, w_out, expand, cat, keys, lse, allowed, mixed, nope, keys_grad, nope_grad, rope_grad,
-    expand_grad, heads_grad, mix_grad, low_probs, score_grad, cat_grad,
+    scale, grad, w_out, expand, cat, keys, lse, allowed, mixed, nope, cosine, sine, wq_hbm, keys_grad,
+    query_grad, hidden_grad, expand_grad, heads_grad, mix_grad, low_probs, score_grad, cat_grad,
+    rope_grad, w_part, part_sem,
 ):
     trees, tok = cat.shape[0], cat.shape[2]
+    size = w_part.shape[1]
+    parts = D // size
+
+    def part(i):
+        return pltpu.make_async_copy(
+            wq_hbm.at[pl.ds(i * size, size), :], w_part.at[i % 2], part_sem.at[i % 2]
+        )
+
+    part(0).start()
     for start in range(0, H * DV, 512):
         heads_grad[:, start : start + 512] = nt(grad[...], w_out[start : start + 512, :]).astype(BF)
     for h in range(H):
@@ -1032,16 +1042,32 @@
             total = tn(score_grad[:, cut], query) * scale
             keys_grad[b, cut, :LAT] = (total[:, :LAT] + tn(low_probs[:, cut], mix)).astype(BF)
             keys_grad[b, cut, LAT:] = total[:, LAT:].astype(BF)
+    half = DR // 2
     for h in range(H):
         low = jnp.concatenate([cat_grad[b, h] for b in range(trees)], axis=0)
         key = expand[:, h * (DN + DV) : h * (DN + DV) + DN]
-        nope_grad[:, h * DN : (h + 1) * DN] = multiply(low, key)
+        first = h * (DN + DR)
+        query_grad[:, first : first + DN] = multiply(low, key).astype(BF)
+        for b in range(trees):
+            rows = slice(b * tok, (b + 1) * tok)
+            former, latter = rope_grad[b, h, :, :half], rope_grad[b, h, :, half:DR]
+            query_grad[rows, first + DN : first + DN + half] = (
+                former * cosine[rows, :] + latter * sine[rows, :]
+            ).astype(BF)
+            query_grad[rows, first + DN + half : first + DN + DR] = (
+                latter * cosine[rows, :] - former * sine[rows, :]
+            ).astype(BF)
         expand_grad[:, h * (DN + DV) : h * (DN + DV) + DN] = tn(
             low, nope[:, h * DN : (h + 1) * DN]
         ).astype(BF)
-
-
-def attend_back(grad, w_output, expand, cat, keys, lse, allowed, mixed, nope, scale):
+    for i in range(parts):
+        part(i).wait()
+        if i + 1 < parts:
+            part(i + 1).start()
+        hidden_grad[:, i * size : (i + 1) * size] = nt(query_grad[...], w_part[i % 2])
+
+
+def attend_back(grad, w_output, expand, cat, keys, lse, allowed, mixed, nope, cosine, sine, w_query, scale):
     trees, _, tok, width = cat.shape
     length, rows = keys.shape[1], grad.shape[0]
     vmem = pl.BlockSpec(memory_space=pltpu.VMEM)
@@ -1049,11 +1075,11 @@
         functools.partial(attend_back_kernel, scale),
         out_shape=[
             jax.ShapeDtypeStruct(keys.shape, BF),
-            jax.ShapeDtypeStruct((rows, H * DN), F32),
-            jax.ShapeDtypeStruct((trees, H, tok, width - LAT), F32),
+            jax.ShapeDtypeStruct((rows, H * (DN + DR)), BF),
+            jax.ShapeDtypeStruct((rows, D), F32),
             jax.ShapeDtypeStruct(expand.shape, BF),
         ],
-        in_specs=[vmem] * 9,
+        in_specs=[vmem] * 11 + [pl.BlockSpec(memory_space=pl.ANY)],
         out_specs=[vmem] * 4,
         scratch_shapes=[
             pltpu.VMEM((rows, H * DV), BF),
@@ -1061,13 +1087,14 @@
             pltpu.VMEM((H * tok, length), BF),
             pltpu.VMEM((H * tok, length), BF),
             pltpu.VMEM((trees, H, tok, LAT), BF),
+            pltpu.VMEM((trees, H, tok, width - LAT), F32),
+            pltpu.VMEM((2, 256, H * (DN + DR)), BF),
+            pltpu.SemaphoreType.DMA((2,)),
         ],
         compiler_params=pltpu.CompilerParams(vmem_limit_bytes=60 << 20),
-        cost_estimate=pl.CostEstimate(
-            flops=0, bytes_accessed=1 << 20, transcendentals=0
-        ),
+        cost_estimate=pl.CostEstimate(flops=0, bytes_accessed=1 << 20, transcendentals=0),
         name="attend_back",
-    )(grad, w_output, expand, cat, keys, lse, allowed, mixed, nope)
+    )(grad, w_output, expand, cat, keys, lse, allowed, mixed, nope, cosine, sine, w_query)
 
 
 def body(
@@ -1319,7 +1346,7 @@
     mid_input, grad_gain_ffn = normalize_back(mid_grad, normed_mid, inverse_mid, gain_ffn)
     residual_grad = upstream + mid_input
     residual_low = residual_grad.astype(BF)
-    keys_grad, qnope_grad, qrope_grad, grad_expand = attend_back(
+    keys_grad, query_grad, hidden_grad, grad_expand = attend_back(
         residual_low,
         w_output,
         w_expand,
@@ -1329,17 +1356,11 @@
         allowed,
         mixed,
         query_nope,
+        cosine.reshape(row_total, -1),
+        sine.reshape(row_total, -1),
+        w_query,
         score_scale,
     )
-    qrope_grad = qrope_grad[..., :DR].transpose(0, 2, 1, 3)
-    query_grad = jnp.concatenate(
-        [
-            qnope_grad.reshape(trees, tok_loc, H, DN),
-            rotate(qrope_grad, cosine[:, :, None, :], -sine[:, :, None, :]),
-        ],
-        axis=-1,
-    )
-    query_grad = query_grad.astype(BF).reshape(row_total, H * (DN + DR))
     own_keys_grad, grad_query, grad_output = ring_reduce(
         ring,
         4,
@@ -1350,10 +1371,6 @@
         [(0, D), (0, H * DV)],
         [(0, 0, 0, query_grad.shape[1]), (1, 1, 0, D)],
     )
-    own_keys_grad, out_sum = lax.optimization_barrier((own_keys_grad, out_sum))
-    out_sum = roll_out(out_sum.reshape(row_total, D).astype(F32))
-    output = (residual + out_sum).astype(BF).reshape(trees, tok_loc, D)
-    hidden_grad = multiply_transposed(query_grad, w_query)
     latent_in_grad, grad_gain_latent = normalize_back(
         own_keys_grad[..., :LAT].reshape(row_total, LAT), latent_normed, latent_inverse, gain_latent
     )
@@ -1394,6 +1411,9 @@
             for x in parts
         )
         ffn_sums = weight_grads(0, e_gg, e_ug, e_hidden, s_act)
+    t_small, out_sum = lax.optimization_barrier((t_small, out_sum))
+    out_sum = roll_out(out_sum.reshape(row_total, D).astype(F32))
+    output = (residual + out_sum).astype(BF).reshape(trees, tok_loc, D)
     t_small = t_small.reshape(PACK)
     for one in came:
         ffn_sums = [a.astype(F32) + b.astype(F32) for a, b in zip(ffn_sums, one)]

time: 757 us -> 750 us (level)
  local copies, waits for them, and re-layouts: 50.7 us -> 38.2 us
  Pallas kernels: 622 us -> 633 us
    pallas_call x1, Pallas kernels: 36.3 us -> 50.5 us  [attend_back(): pl.pallas_call(functools.partial(attend_back_kernel, scale), out_shape=[j...]
    unnamed x98 -> x91, local copies, waits for them, and re-layouts: 28.8 us -> 16.2 us
    dot_general x4 -> x3, matrix products: 17.1 us -> 7.9 us  [multiply_transposed(): lax.dot_general(left, right, (((1,), (1,)), ((), ())), preferred_element_...]
  transfers between devices with their start and end apart: 7 -> 7, of which waited for: 1 -> 0; matrix products, arithmetic and copies ran while one was open for 6% -> 9% of each run, Pallas kernels for 44% -> 45%
where the time goes in v6:
time: 750 us; the launch traced here: 743 us
  Pallas kernels  633 us (84%)
  other arithmetic  38.7 us (5%)
  local copies, waits for them, and re-layouts  38.2 us (5%)
  between operations  15 us (2%)
  matrix products  12.3 us (2%)
    pallas_call x3, Pallas kernels, ring_reduce(): pl.pallas_call(functools.partial(reduce_kernel, ring, tuple(wide), tuple(...  243 us
    pallas_call x1, Pallas kernels, front(): pl.pallas_call(functools.partial(front_kernel, ring, latent_part), out_sh...  160 us
    pallas_call x1, Pallas kernels, run_experts(): pl.pallas_call(functools.partial(expert_kernel, nf, experts, fp, bundle_s...  79.2 us
    pallas_call x1, Pallas kernels, ring_gather(): pl.pallas_call(functools.partial(gather_kernel, ring, tuple(wide), tuple(...  70.5 us
    pallas_call x1, Pallas kernels, attend_back(): pl.pallas_call(functools.partial(attend_back_kernel, scale), out_shape=[j...  50.5 us
    pallas_call x1, Pallas kernels, attend(): pl.pallas_call(functools.partial(attend_kernel, scale), out_shape=[jax.Sh...  29.7 us
    add x4, other arithmetic, body(): ffn_sums = [a.astype(F32) + b.astype(F32) for a, b in zip(ffn_sums, one)]  18.2 us
    unnamed x91, local copies, waits for them, and re-layouts  16.2 us
  transfers between devices with their start and end apart: 7, of which 0 were waited for; matrix products, arithmetic and copies ran while one was open for 9% of the time, Pallas kernels for 45%

profile of v6, /device:TPU:0, one launch (start us, length us, event | category | flops | bytes accessed | tf_op | source)
XLA Modules:
  0.0 742.9 jit_solution(16361200775467397500)
XLA Ops:
  8.1 1.2 multiply_reduce_fusion.5
  11.6 0.8 copy.59
  12.8 2.1 concatenate.36
  15.6 0.8 constant_dynamic-slice_fusion
  16.3 1.3 convert_reduce_fusion
  17.7 1.2 copy.62
  19.4 1.1 bitcast_multiply_fusion.refs_7_
  20.5 1.0 multiply_sine_fusion.1
  21.5 1.4 fusion.5.refs_8_
  22.9 160.5 %front.1 = (bf16[2,16,32,128]{3,2,1,0:T(8,128)(2,1)}, bf16[2,16,64,576]{3,2,1,0:T(8,128)(2,1)}, bf16[2,16,64,3072]{3,2,1,0:T(8,128)(2,1)}, bf16[2,16,16,4096]{3,...) custom-call(bf16[32,128]{1,0:T(8,128)(2,1)} %pad_bitcast_fusion.1.re, ...), custom_call_target="tpu_custom_call" | custom-call | bytes 55574528 | tf_op jit(solution)/shard_map/front/pallas_call | solution.py:401
  183.3 1.1 fusion.12
  185.3 1.6 collective-permute-start
  186.8 1.1 copy.86
  189.8 2.0 reshape_reshape.4.refs_4_
  191.8 0.8 convert_element_type.155.allowed
  193.2 29.7 %attend.1 = (bf16[2,16,64,640]{3,2,1,0:T(8,128)(2,1)}, f32[2,16,64,1]{3,2,1,0:T(8,128)}, bf16[2,16,64,512]{3,2,1,0:T(8,128)(2,1)}, bf16[128,2048]{1,0:T(8,128)(2...) custom-call(bf16[128,2048]{1,0:T(8,128)(2,1)} %get-tuple-element.85.hidden.refs_1_, ...), custom_call_target="tpu_custom_call" | custom-call | flops 4831838208 | bytes 31457280 | tf_op jit(solution)/shard_map/attend/pallas_call | solution.py:962
  222.9 1.4 multiply_reduce_fusion.4
  224.3 1.4 multiply_convert_fusion
  226.9 1.1 fusion.13
  227.9 70.5 %ring_gather_2.1 = (bf16[2,16,64,2048]{3,2,1,0:T(8,128)(2,1)}, bf16[2,16,64,128]{3,2,1,0:T(8,128)(2,1)}) custom-call(bf16[2,64,2048]{2,1,0:T(8,128)(2,1)} %bitcast.101, bf16[2,64,128]{2,1,0:T(8,128)(2,1)} %bitcast.117), custom_call_target="tpu_custom_call" | custom-call | bytes 17825792 | tf_op jit(solution)/shard_map/ring_gather_2/pallas_call | solution.py:217
  298.5 79.2 %experts.1 = (bf16[2048,2048]{1,0:T(8,128)(2,1)}, bf16[2048,2048]{1,0:T(8,128)(2,1)}, bf16[2048,128]{1,0:T(8,128)(2,1)}, bf16[1024,2048]{1,0:T(8,128)(2,1)}, bf1...) custom-call(bf16[2048,2048]{1,0:T(8,128)(2,1)} %bitcast.85, ...), custom_call_target="tpu_custom_call" | custom-call | flops 52613349376 | bytes 41943040 | tf_op jit(solution)/shard_map/experts/pallas_call | solution.py:848
  377.7 56.8 %ring_reduce_3.1 = (f32[2,64,2048]{2,1,0:T(8,128)}, f32[2,64,128]{2,1,0:T(8,128)}, bf16[1024,512]{1,0:T(8,128)(2,1)}, bf16[1024,256]{1,0:T(8,128)(2,1)}, bf16[10...) custom-call(bf16[2,16,64,2048]{3,2,1,0:T(8,128)(2,1)} %bitcast.96, ...), custom_call_target="tpu_custom_call" | custom-call | bytes 1048576 | tf_op jit(solution)/shard_map/ring_reduce_3/pallas_call | solution.py:677
  436.2 2.5 multiply_reduce_fusion.1
  439.4 0.9 collective-permute-start.2
  440.3 1.2 collective-permute-start.3
  441.5 0.9 collective-permute-start.4
  442.3 0.9 convolution_convert_fusion.1
  443.5 1.4 reshape.337
  445.5 1.7 fusion.35.grad.refs_4_
  447.3 50.5 %attend_back.1 = (bf16[2,1024,640]{2,1,0:T(8,128)(2,1)}, bf16[128,3072]{1,0:T(8,128)(2,1)}, f32[128,2048]{1,0:T(8,128)}, bf16[512,4096]{1,0:T(8,128)(2,1)}) custom-call(bf16[128,2048]{1,0:T(8,128)(2,1)} %fusion.35.grad.refs_4_, bf16[2048,2048]{1,0:T(8,128)(2,1)} %bitcast.81, bf16[512,4096]{1,0:T(8,128)(2,1)} %bitcast.89, ...), custom_call_target="tpu_custom_call" | custom-call | bytes 1048576 | tf_op jit(solution)/shard_map/attend_back/pallas_call | solution.py:1074
  497.9 37.8 %ring_reduce_4.1 = (f32[2,64,640]{2,1,0:T(8,128)}, bf16[2048,3072]{1,0:T(8,128)(2,1)}, bf16[2048,2048]{1,0:T(8,128)(2,1)}) custom-call(bf16[2,16,64,640]{3,2,1,0:T(8,128)(2,1)} %bitcast.100, bf16[128,2048]{1,0:T(8,128)(2,1)} %get-tuple-element.85.hidden.refs_1_, bf16[128,2048]{1,0:T(8,128)(2,1)} %get-tuple-element.117.refs_2_, ...), custom_call_target="tpu_custom_call" | custom-call | bytes 1048576 | tf_op jit(solution)/shard_map/ring_reduce_4/pallas_call | solution.py:677
  535.6 1.0 slice.70
  537.5 1.2 fusion.18
  539.7 4.1 multiply_reduce_fusion
  544.7 3.1 convolution_convert_fusion
  547.8 4.4 copy.70
  552.2 148.5 %ring_reduce_5.1 = (f32[64,3072]{1,0:T(8,128)}, f32[16,4096]{1,0:T(8,128)}, f32[64,576]{1,0:T(8,128)}, f32[16,128]{1,0:T(8,128)}, f32[64,2048]{1,0:T(8,128)}, /*...) custom-call(bf16[2,16,64,3072]{3,2,1,0:T(8,128)(2,1)} %bitcast.91, ...), custom_call_target="tpu_custom_call" | custom-call | bytes 1048576 | tf_op jit(solution)/shard_map/ring_reduce_5/pallas_call | solution.py:677
  700.7 2.1 convert_add_fusion.5
  702.8 2.4 copy.75
  705.2 1.8 convert_add_fusion.3
  707.1 1.5 fusion.36
  708.5 2.4 copy.74
  710.9 2.4 copy.73
  713.3 5.9 convert_add_fusion.2
  719.3 8.3 %convert_add_fusion = (f32[1024,1408]{1,0:T(8,128)}, f32[1024,1408]{1,0:T(8,128)}) fusion(bf16[1024,1408]{1,0:T(8,128)(2,1)} %collective-permute-done.4, bf16[1024,1408]{1,0:T(8,128)(2,1)S(1)} %copy-done.8, bf16[1024,1408]{1,0:T(8,128)(2,1)} %collective-permute-done.3, bf16[1024,1408]{1,0:T(8,128)(2,1)S(1)} %copy-done.7), kind=kLoop, calls=%fused_computation | loop fusion | flops 8650752 | bytes 23068672 | tf_op jit(solution)/shard_map/add | solution.py:1419
  729.5 3.3 multiply_add_fusion
  732.8 0.9 copy.91
  735.1 0.8 copy.94
  (155 shorter events, 18.3 us)
Async XLA Ops:
  7.2 12.2 %copy-start.1 = (bf16[2,64,2048]{2,1,0:T(8,128)(2,1)S(1)}, bf16[2,64,2048]{2,1,0:T(8,128)(2,1)}, u32[]{:S(2)}) copy-start(bf16[2,64,2048]{2,1,0:T(8,128)(2,1)} %param.19) | copy-start | bytes 1572868
  7.2 11.7 %copy-start.14 = (bf16[1024,176]{0,1:T(8,128)(2,1)S(1)}, bf16[1024,176]{0,1:T(8,128)(2,1)}, u32[]{:S(2)}) copy-start(bf16[1024,176]{0,1:T(8,128)(2,1)} %param.36) | copy-start | bytes 1081348
  7.2 12.0 %copy-start.15 = (bf16[1024,176]{0,1:T(8,128)(2,1)S(1)}, bf16[1024,176]{0,1:T(8,128)(2,1)}, u32[]{:S(2)}) copy-start(bf16[1024,176]{0,1:T(8,128)(2,1)} %param.37) | copy-start | bytes 1081348
  7.2 291.3 %all-gather.2.cloned.1.call-start = ((), (), s32[]{:S(2)}) async-start(), calls=%async_computation.1 | async-start | bytes 8912896 | tf_op jit(solution)/shard_map/all_gather | solution.py:1219
  7.3 13.2 %copy-start.32 = (f32[32]{0:T(128)}, f32[32]{0:T(128)S(1)}, u32[]{:S(2)}) copy-start(f32[32]{0:T(128)S(1)} %negate_power_fusion) | copy-start | bytes 388
  9.5 12.0 %copy-start.28 = (f32[128]{0:T(128)}, f32[128]{0:T(128)S(1)}, u32[]{:S(2)}) copy-start(f32[128]{0:T(128)S(1)} %rsqrt.28) | copy-start | bytes 1540
  17.6 1.3 copy-start.30
  22.8 160.5 %copy-start.4 = (bf16[2,64,2048]{2,1,0:T(8,128)(2,1)S(1)}, bf16[2,64,2048]{2,1,0:T(8,128)(2,1)}, u32[]{:S(2)}) copy-start(bf16[2,64,2048]{2,1,0:T(8,128)(2,1)} %param.20) | copy-start | bytes 1572868
  184.5 543.1 %reduce-scatter.2.cloned.1.call-start = ((), (), s32[]{:S(2)}) async-start(), calls=%async_computation.2 | async-start | bytes 8912896 | tf_op jit(solution)/shard_map/reduce_scatter | solution.py:1329
  184.7 113.7 %collective-permute-start.1 = (bf16[1024,768]{1,0:T(8,128)(2,1)}, bf16[1024,768]{1,0:T(8,128)(2,1)}, u32[]{:S(2)}, u32[]{:S(2)}) collective-permute-start(bf16[1024,768]{1,0:T(8,128)(2,1)} %fusion.5.refs_8_), channel_id=1, source_target_pairs={{0,16},{16,0},{1,17},{17,1},{2,18},{18,2},{3,19},{19,3},{4,20},{20... | collective-permute-start | bytes 4718600 | tf_op jit(solution)/shard_map/ppermute | solution.py:1149
  185.3 113.2 %collective-permute-start = (bf16[1024,1408]{1,0:T(8,128)(2,1)}, bf16[1024,1408]{1,0:T(8,128)(2,1)}, u32[]{:S(2)}, u32[]{:S(2)}) collective-permute-start(bf16[1024,1408]{1,0:T(8,128)(2,1)} %refs_7_), channel_id=1, source_target_pairs={{0,16},{16,0},{1,17},{17,1},{2,18},{18,2},{3,19},{19,3},{4,20},{20... | collective-permute-start | bytes 8650760 | tf_op jit(solution)/shard_map/ppermute | solution.py:1149
  193.2 32.5 %copy-start.6 = (bf16[2048,16]{1,0:T(8,128)(2,1)}, bf16[2048,16]{1,0:T(8,128)(2,1)S(1)}, u32[]{:S(2)}) copy-start(bf16[2048,16]{1,0:T(8,128)(2,1)S(1)} %reshape.316) | copy-start | bytes 196612
  224.3 1.7 copy-start.25
  434.5 1.0 copy-start.9
  434.5 1.6 copy-start.19
  434.5 1.7 copy-start
  434.5 1.7 copy-start.26
  436.2 5.3 copy-start.20
  439.4 261.2 %collective-permute-start.2 = (bf16[1024,1408]{1,0:T(8,128)(2,1)}, bf16[1024,1408]{1,0:T(8,128)(2,1)}, u32[]{:S(2)}, u32[]{:S(2)}) collective-permute-start(bf16[1024,1408]{1,0:T(8,128)(2,1)} %get-tuple-element.136), channel_id=1, source_target_pairs={{0,16},{16,0},{1,17},{17,1},{2,18},{18,2},{3,19},{19,3},{4,20},{20... | collective-permute-start | bytes 8650760 | tf_op jit(solution)/shard_map/ppermute | solution.py:1337
  440.3 260.4 %collective-permute-start.3 = (bf16[1024,1408]{1,0:T(8,128)(2,1)}, bf16[1024,1408]{1,0:T(8,128)(2,1)}, u32[]{:S(2)}, u32[]{:S(2)}) collective-permute-start(bf16[1024,1408]{1,0:T(8,128)(2,1)} %get-tuple-element.137), channel_id=1, source_target_pairs={{0,16},{16,0},{1,17},{17,1},{2,18},{18,2},{3,19},{19,3},{4,20},{20... | collective-permute-start | bytes 8650760 | tf_op jit(solution)/shard_map/ppermute | solution.py:1337
  441.5 259.2 %collective-permute-start.4 = (bf16[1024,1408]{1,0:T(8,128)(2,1)}, bf16[1024,1408]{1,0:T(8,128)(2,1)}, u32[]{:S(2)}, u32[]{:S(2)}) collective-permute-start(bf16[1024,1408]{1,0:T(8,128)(2,1)} %get-tuple-element.138), channel_id=1, source_target_pairs={{0,16},{16,0},{1,17},{17,1},{2,18},{18,2},{3,19},{19,3},{4,20},{20... | collective-permute-start | bytes 8650760 | tf_op jit(solution)/shard_map/ppermute | solution.py:1337
  445.5 52.3 %copy-start.34 = (f32[128]{0:T(128)}, f32[128]{0:T(128)S(1)}, u32[]{:S(2)}) copy-start(f32[128]{0:T(128)S(1)} %broadcast_multiply_fusion.2) | copy-start | bytes 1540
  497.8 38.8 %copy-start.23 = (f32[512]{0:T(512)S(1)}, f32[512]{0:T(512)}, u32[]{:S(2)}) copy-start(f32[512]{0:T(512)} %reshape.367) | copy-start | bytes 6148
  497.8 38.8 %copy-start.36 = (f32[128]{0:T(128)S(1)}, f32[128]{0:T(128)}, u32[]{:S(2)}) copy-start(f32[128]{0:T(128)} %add_rsqrt_fusion.1) | copy-start | bytes 1540
  497.8 39.7 %copy-start.31 = (f32[2,64]{1,0:T(2,128)S(1)}, f32[2,64]{1,0:T(2,128)}, u32[]{:S(2)}) copy-start(f32[2,64]{1,0:T(2,128)} %copy-done.30) | copy-start | bytes 1540
  497.8 39.7 %copy-start.33 = (f32[32]{0:T(128)S(1)}, f32[32]{0:T(128)}, u32[]{:S(2)}) copy-start(f32[32]{0:T(128)} %copy-done.32) | copy-start | bytes 388
  497.9 41.8 %copy-start.2 = (bf16[2,64,2048]{2,1,0:T(8,128)(2,1)S(1)}, bf16[2,64,2048]{2,1,0:T(8,128)(2,1)}, u32[]{:S(2)}) copy-start(bf16[2,64,2048]{2,1,0:T(8,128)(2,1)} %param.19) | copy-start | bytes 1572868
  539.0 0.7 copy-start.10
  539.0 4.8 copy-start.16
  539.0 4.8 copy-start.21
  539.0 4.8 copy-start.22
  539.7 5.0 copy-start.3
  552.2 148.5 %copy-start.13 = (bf16[1024,256]{1,0:T(8,128)(2,1)S(1)}, bf16[1024,256]{1,0:T(8,128)(2,1)}, u32[]{:S(2)}) copy-start(bf16[1024,256]{1,0:T(8,128)(2,1)} %get-tuple-element.153) | copy-start | bytes 1572868
  713.3 5.9 copy-start.7
  713.3 5.9 copy-start.8
  719.2 8.3 %copy-start.24 = (f32[16,128]{1,0:T(8,128)S(1)}, f32[16,128]{1,0:T(8,128)}, u32[]{:S(2)}) copy-start(f32[16,128]{1,0:T(8,128)} %get-tuple-element.129) | copy-start | bytes 24580
  719.2 10.2 %copy-start.5 = (bf16[2,64,2048]{2,1,0:T(8,128)(2,1)S(1)}, bf16[2,64,2048]{2,1,0:T(8,128)(2,1)}, u32[]{:S(2)}) copy-start(bf16[2,64,2048]{2,1,0:T(8,128)(2,1)} %param.20) | copy-start | bytes 1572868
  719.2 10.2 %copy-start.27 = (f32[128]{0:T(128)S(1)}, f32[128]{0:T(128)}, u32[]{:S(2)}) copy-start(f32[128]{0:T(128)} %copy-done.25) | copy-start | bytes 1540
  719.3 10.2 %copy-start.29 = (f32[128]{0:T(128)S(1)}, f32[128]{0:T(128)}, u32[]{:S(2)}) copy-start(f32[128]{0:T(128)} %copy-done.28) | copy-start | bytes 1540
  719.3 10.2 %copy-start.35 = (f32[128]{0:T(128)S(1)}, f32[128]{0:T(128)}, u32[]{:S(2)}) copy-start(f32[128]{0:T(128)} %copy-done.34) | copy-start | bytes 1540
  729.4 3.4 copy-start.11
  729.5 4.2 copy-start.18
  729.5 4.9 copy-start.17
  729.5 5.6 copy-start.12
Sparse Core Ops, SparseCore 0:
  184.6 81.1 all-gather.1
  434.6 109.2 reduce-scatter.1

commit v7 on v6

--- a/solution.py
+++ b/solution.py
@@ -1314,9 +1314,7 @@
             *job_arrays,
             job_cuts(1),
             job_pairs,
-            (0, 1),
-        )
-        there, sent = sent[5:], sent[2:5]
+        )
     else:
         back_sum, delta_sum = ring_reduce(
             ring, 3, [by_owner(back), by_owner(delta_out)], [False] * 2
@@ -1335,8 +1333,6 @@
         perm = [(i, (i + k) % nf) for i in range(nf)]
         grads = sent if nf == 2 else weight_grads(k, e_gg, e_ug, e_hidden, s_act)
         came.append([lax.ppermute(g.astype(BF), "fsdp", perm) for g in grads])
-    if nf == 2:
-        came[0] = list(there) + came[0]
 
     logit_grad = (
         expert_probs * (prob_delta - jnp.sum(expert_probs * prob_delta, axis=-1, keepdims=True))

time: 750 us -> 747 us (level)
    unnamed x91 -> x85, local copies, waits for them, and re-layouts: 16.2 us -> 15.5 us
  transfers between devices with their start and end apart: 7 -> 9, of which waited for: 0 -> 0; matrix products, arithmetic and copies ran while one was open for 9% -> 8% of each run, Pallas kernels for 45% -> 46%
where the time goes in v7:
time: 747 us; the launch traced here: 740 us
  Pallas kernels  630 us (84%)
  other arithmetic  39.4 us (5%)
  local copies, waits for them, and re-layouts  36.3 us (5%)
  between operations  15 us (2%)
  matrix products  11.5 us (2%)
  starting transfers between devices  7.97 us (1%)
    pallas_call x3, Pallas kernels, ring_reduce(): pl.pallas_call(functools.partial(reduce_kernel, ring, tuple(wide), tuple(...  240 us
    pallas_call x1, Pallas kernels, front(): pl.pallas_call(functools.partial(front_kernel, ring, latent_part), out_sh...  160 us
    pallas_call x1, Pallas kernels, run_experts(): pl.pallas_call(functools.partial(expert_kernel, nf, experts, fp, bundle_s...  79.2 us
    pallas_call x1, Pallas kernels, ring_gather(): pl.pallas_call(functools.partial(gather_kernel, ring, tuple(wide), tuple(...  70.5 us
    pallas_call x1, Pallas kernels, attend_back(): pl.pallas_call(functools.partial(attend_back_kernel, scale), out_shape=[j...  49.9 us
    pallas_call x1, Pallas kernels, attend(): pl.pallas_call(functools.partial(attend_kernel, scale), out_shape=[jax.Sh...  29.7 us
    add x4, other arithmetic, body(): ffn_sums = [a.astype(F32) + b.astype(F32) for a, b in zip(ffn_sums, one)]  18.3 us
    unnamed x85, local copies, waits for them, and re-layouts  15.5 us
  transfers between devices with their start and end apart: 9, of which 0 were waited for; matrix products, arithmetic and copies ran while one was open for 8% of the time, Pallas kernels for 46%

profile of v7, /device:TPU:0, one launch (start us, length us, event | category | flops | bytes accessed | tf_op | source)
XLA Modules:
  0.0 740.3 jit_solution(7844365836010144006)
XLA Ops:
  8.1 1.2 multiply_reduce_fusion.5
  11.6 0.8 copy.59
  12.8 2.1 concatenate.36
  16.3 1.3 convert_reduce_fusion
  17.7 1.2 copy.62
  19.4 1.1 bitcast_multiply_fusion.refs_7_
  20.5 1.0 multiply_sine_fusion.1
  21.5 1.4 fusion.5.refs_8_
  22.9 160.5 %front.1 = (bf16[2,16,32,128]{3,2,1,0:T(8,128)(2,1)}, bf16[2,16,64,576]{3,2,1,0:T(8,128)(2,1)}, bf16[2,16,64,3072]{3,2,1,0:T(8,128)(2,1)}, bf16[2,16,16,4096]{3,...) custom-call(bf16[32,128]{1,0:T(8,128)(2,1)} %pad_bitcast_fusion.1.re, ...), custom_call_target="tpu_custom_call" | custom-call | bytes 55574528 | tf_op jit(solution)/shard_map/front/pallas_call | solution.py:401
  183.4 1.1 fusion.12
  185.3 1.6 collective-permute-start
  186.8 1.1 copy.86
  189.8 2.0 reshape_reshape.4.refs_4_
  191.8 0.8 convert_element_type.155.allowed
  193.2 29.7 %attend.1 = (bf16[2,16,64,640]{3,2,1,0:T(8,128)(2,1)}, f32[2,16,64,1]{3,2,1,0:T(8,128)}, bf16[2,16,64,512]{3,2,1,0:T(8,128)(2,1)}, bf16[128,2048]{1,0:T(8,128)(2...) custom-call(bf16[128,2048]{1,0:T(8,128)(2,1)} %get-tuple-element.85.hidden.refs_1_, ...), custom_call_target="tpu_custom_call" | custom-call | flops 4831838208 | bytes 31457280 | tf_op jit(solution)/shard_map/attend/pallas_call | solution.py:962
  222.9 1.4 multiply_reduce_fusion.4
  224.3 1.4 multiply_convert_fusion
  226.9 1.1 fusion.13
  227.9 70.5 %ring_gather_2.1 = (bf16[2,16,64,2048]{3,2,1,0:T(8,128)(2,1)}, bf16[2,16,64,128]{3,2,1,0:T(8,128)(2,1)}) custom-call(bf16[2,64,2048]{2,1,0:T(8,128)(2,1)} %bitcast.101, bf16[2,64,128]{2,1,0:T(8,128)(2,1)} %bitcast.117), custom_call_target="tpu_custom_call" | custom-call | bytes 17825792 | tf_op jit(solution)/shard_map/ring_gather_2/pallas_call | solution.py:217
  298.5 79.2 %experts.1 = (bf16[2048,2048]{1,0:T(8,128)(2,1)}, bf16[2048,2048]{1,0:T(8,128)(2,1)}, bf16[2048,128]{1,0:T(8,128)(2,1)}, bf16[1024,2048]{1,0:T(8,128)(2,1)}, bf1...) custom-call(bf16[2048,2048]{1,0:T(8,128)(2,1)} %bitcast.85, ...), custom_call_target="tpu_custom_call" | custom-call | flops 52613349376 | bytes 41943040 | tf_op jit(solution)/shard_map/experts/pallas_call | solution.py:848
  377.7 52.2 %ring_reduce_3.1 = (f32[2,64,2048]{2,1,0:T(8,128)}, f32[2,64,128]{2,1,0:T(8,128)}, bf16[1024,512]{1,0:T(8,128)(2,1)}, bf16[1024,256]{1,0:T(8,128)(2,1)}, bf16[10...) custom-call(bf16[2,16,64,2048]{3,2,1,0:T(8,128)(2,1)} %bitcast.96, ...), custom_call_target="tpu_custom_call" | custom-call | bytes 1048576 | tf_op jit(solution)/shard_map/ring_reduce_3/pallas_call | solution.py:677
  431.7 2.5 multiply_reduce_fusion.1
  434.9 1.4 collective-permute-start.4
  436.9 1.4 collective-permute-start.6
  438.3 0.9 convolution_convert_fusion.1
  439.5 0.8 reshape.337
  440.9 1.4 collective-permute-start.2
  443.0 1.7 fusion.35.grad.refs_4_
  444.7 49.9 %attend_back.1 = (bf16[2,1024,640]{2,1,0:T(8,128)(2,1)}, bf16[128,3072]{1,0:T(8,128)(2,1)}, f32[128,2048]{1,0:T(8,128)}, bf16[512,4096]{1,0:T(8,128)(2,1)}) custom-call(bf16[128,2048]{1,0:T(8,128)(2,1)} %fusion.35.grad.refs_4_, bf16[2048,2048]{1,0:T(8,128)(2,1)} %bitcast.81, bf16[512,4096]{1,0:T(8,128)(2,1)} %bitcast.89, ...), custom_call_target="tpu_custom_call" | custom-call | bytes 1048576 | tf_op jit(solution)/shard_map/attend_back/pallas_call | solution.py:1074
  494.7 35.2 %ring_reduce_4.1 = (f32[2,64,640]{2,1,0:T(8,128)}, bf16[2048,3072]{1,0:T(8,128)(2,1)}, bf16[2048,2048]{1,0:T(8,128)(2,1)}) custom-call(bf16[2,16,64,640]{3,2,1,0:T(8,128)(2,1)} %bitcast.100, bf16[128,2048]{1,0:T(8,128)(2,1)} %get-tuple-element.85.hidden.refs_1_, bf16[128,2048]{1,0:T(8,128)(2,1)} %get-tuple-element.117.refs_2_, ...), custom_call_target="tpu_custom_call" | custom-call | bytes 1048576 | tf_op jit(solution)/shard_map/ring_reduce_4/pallas_call | solution.py:677
  529.9 1.0 slice.70
  531.1 1.2 fusion.18
  532.3 0.8 multiply_convert_fusion.1
  533.3 4.1 multiply_reduce_fusion
  538.4 2.2 convolution_convert_fusion
  540.6 4.4 copy.70
  544.9 152.9 %ring_reduce_5.1 = (f32[64,3072]{1,0:T(8,128)}, f32[16,4096]{1,0:T(8,128)}, f32[64,576]{1,0:T(8,128)}, f32[16,128]{1,0:T(8,128)}, f32[64,2048]{1,0:T(8,128)}, /*...) custom-call(bf16[2,16,64,3072]{3,2,1,0:T(8,128)(2,1)} %bitcast.91, ...), custom_call_target="tpu_custom_call" | custom-call | bytes 1048576 | tf_op jit(solution)/shard_map/ring_reduce_5/pallas_call | solution.py:677
  697.9 2.3 convert_add_fusion.5
  700.2 2.4 copy.75
  702.6 1.8 convert_add_fusion.3
  704.4 1.5 fusion.36
  705.9 2.4 copy.74
  708.3 2.4 copy.73
  710.7 5.9 convert_add_fusion.2
  716.7 8.3 %convert_add_fusion = (f32[1024,1408]{1,0:T(8,128)}, f32[1024,1408]{1,0:T(8,128)}) fusion(bf16[1024,1408]{1,0:T(8,128)(2,1)} %collective-permute-done.6, bf16[1024,1408]{1,0:T(8,128)(2,1)S(1)} %copy-done.8, bf16[1024,1408]{1,0:T(8,128)(2,1)} %collective-permute-done.5, bf16[1024,1408]{1,0:T(8,128)(2,1)S(1)} %copy-done.7), kind=kLoop, calls=%fused_computation | loop fusion | flops 8650752 | bytes 23068672 | tf_op jit(solution)/shard_map/add | solution.py:1415
  726.9 3.3 multiply_add_fusion
  730.2 0.9 copy.91
  732.5 0.8 copy.94
  (153 shorter events, 19.0 us)
Async XLA Ops:
  7.2 12.2 %copy-start.1 = (bf16[2,64,2048]{2,1,0:T(8,128)(2,1)S(1)}, bf16[2,64,2048]{2,1,0:T(8,128)(2,1)}, u32[]{:S(2)}) copy-start(bf16[2,64,2048]{2,1,0:T(8,128)(2,1)} %param.19) | copy-start | bytes 1572868
  7.2 11.7 %copy-start.13 = (bf16[1024,176]{0,1:T(8,128)(2,1)S(1)}, bf16[1024,176]{0,1:T(8,128)(2,1)}, u32[]{:S(2)}) copy-start(bf16[1024,176]{0,1:T(8,128)(2,1)} %param.36) | copy-start | bytes 1081348
  7.2 12.0 %copy-start.14 = (bf16[1024,176]{0,1:T(8,128)(2,1)S(1)}, bf16[1024,176]{0,1:T(8,128)(2,1)}, u32[]{:S(2)}) copy-start(bf16[1024,176]{0,1:T(8,128)(2,1)} %param.37) | copy-start | bytes 1081348
  7.2 291.3 %all-gather.2.cloned.1.call-start = ((), (), s32[]{:S(2)}) async-start(), calls=%async_computation.1 | async-start | bytes 8912896 | tf_op jit(solution)/shard_map/all_gather | solution.py:1219
  7.3 13.2 %copy-start.29 = (f32[32]{0:T(128)}, f32[32]{0:T(128)S(1)}, u32[]{:S(2)}) copy-start(f32[32]{0:T(128)S(1)} %negate_power_fusion) | copy-start | bytes 388
  9.5 12.0 %copy-start.25 = (f32[128]{0:T(128)}, f32[128]{0:T(128)S(1)}, u32[]{:S(2)}) copy-start(f32[128]{0:T(128)S(1)} %rsqrt.28) | copy-start | bytes 1540
  17.6 1.3 copy-start.27
  22.8 160.5 %copy-start.4 = (bf16[2,64,2048]{2,1,0:T(8,128)(2,1)S(1)}, bf16[2,64,2048]{2,1,0:T(8,128)(2,1)}, u32[]{:S(2)}) copy-start(bf16[2,64,2048]{2,1,0:T(8,128)(2,1)} %param.20) | copy-start | bytes 1572868
  184.5 540.5 %reduce-scatter.2.cloned.1.call-start = ((), (), s32[]{:S(2)}) async-start(), calls=%async_computation.2 | async-start | bytes 8912896 | tf_op jit(solution)/shard_map/reduce_scatter | solution.py:1327
  184.7 113.7 %collective-permute-start.1 = (bf16[1024,768]{1,0:T(8,128)(2,1)}, bf16[1024,768]{1,0:T(8,128)(2,1)}, u32[]{:S(2)}, u32[]{:S(2)}) collective-permute-start(bf16[1024,768]{1,0:T(8,128)(2,1)} %fusion.5.refs_8_), channel_id=1, source_target_pairs={{0,16},{16,0},{1,17},{17,1},{2,18},{18,2},{3,19},{19,3},{4,20},{20... | collective-permute-start | bytes 4718600 | tf_op jit(solution)/shard_map/ppermute | solution.py:1149
  185.3 113.2 %collective-permute-start = (bf16[1024,1408]{1,0:T(8,128)(2,1)}, bf16[1024,1408]{1,0:T(8,128)(2,1)}, u32[]{:S(2)}, u32[]{:S(2)}) collective-permute-start(bf16[1024,1408]{1,0:T(8,128)(2,1)} %refs_7_), channel_id=1, source_target_pairs={{0,16},{16,0},{1,17},{17,1},{2,18},{18,2},{3,19},{19,3},{4,20},{20... | collective-permute-start | bytes 8650760 | tf_op jit(solution)/shard_map/ppermute | solution.py:1149
  193.2 32.5 %copy-start.6 = (bf16[2048,16]{1,0:T(8,128)(2,1)}, bf16[2048,16]{1,0:T(8,128)(2,1)S(1)}, u32[]{:S(2)}) copy-start(bf16[2048,16]{1,0:T(8,128)(2,1)S(1)} %reshape.316) | copy-start | bytes 196612
  224.3 1.7 copy-start.22
  429.9 1.0 copy-start.9
  429.9 1.6 copy-start.17
  429.9 1.7 copy-start
  429.9 1.7 copy-start.23
  431.6 5.3 copy-start.18
  434.9 263.0 %collective-permute-start.4 = (bf16[1024,1408]{1,0:T(8,128)(2,1)}, bf16[1024,1408]{1,0:T(8,128)(2,1)}, u32[]{:S(2)}, u32[]{:S(2)}) collective-permute-start(bf16[1024,1408]{1,0:T(8,128)(2,1)} %get-tuple-element.136), channel_id=1, source_target_pairs={{0,16},{16,0},{1,17},{17,1},{2,18},{18,2},{3,19},{19,3},{4,20},{20... | collective-permute-start | bytes 8650760 | tf_op jit(solution)/shard_map/ppermute | solution.py:1335
  436.3 261.6 %collective-permute-start.5 = (bf16[1024,1408]{1,0:T(8,128)(2,1)}, bf16[1024,1408]{1,0:T(8,128)(2,1)}, u32[]{:S(2)}, u32[]{:S(2)}) collective-permute-start(bf16[1024,1408]{1,0:T(8,128)(2,1)} %get-tuple-element.137), channel_id=1, source_target_pairs={{0,16},{16,0},{1,17},{17,1},{2,18},{18,2},{3,19},{19,3},{4,20},{20... | collective-permute-start | bytes 8650760 | tf_op jit(solution)/shard_map/ppermute | solution.py:1335
  436.9 261.0 %collective-permute-start.6 = (bf16[1024,1408]{1,0:T(8,128)(2,1)}, bf16[1024,1408]{1,0:T(8,128)(2,1)}, u32[]{:S(2)}, u32[]{:S(2)}) collective-permute-start(bf16[1024,1408]{1,0:T(8,128)(2,1)} %get-tuple-element.138), channel_id=1, source_target_pairs={{0,16},{16,0},{1,17},{17,1},{2,18},{18,2},{3,19},{19,3},{4,20},{20... | collective-permute-start | bytes 8650760 | tf_op jit(solution)/shard_map/ppermute | solution.py:1335
  440.3 257.6 %collective-permute-start.3 = (bf16[1024,256]{1,0:T(8,128)(2,1)}, bf16[1024,256]{1,0:T(8,128)(2,1)}, u32[]{:S(2)}, u32[]{:S(2)}) collective-permute-start(bf16[1024,256]{1,0:T(8,128)(2,1)} %get-tuple-element.135), channel_id=1, source_target_pairs={{0,16},{16,0},{1,17},{17,1},{2,18},{18,2},{3,19},{19,3},{4,20},{20... | collective-permute-start | bytes 1572872 | tf_op jit(solution)/shard_map/ppermute | solution.py:1335
  440.9 257.0 %collective-permute-start.2 = (bf16[1024,512]{1,0:T(8,128)(2,1)}, bf16[1024,512]{1,0:T(8,128)(2,1)}, u32[]{:S(2)}, u32[]{:S(2)}) collective-permute-start(bf16[1024,512]{1,0:T(8,128)(2,1)} %get-tuple-element.134), channel_id=1, source_target_pairs={{0,16},{16,0},{1,17},{17,1},{2,18},{18,2},{3,19},{19,3},{4,20},{20... | collective-permute-start | bytes 3145736 | tf_op jit(solution)/shard_map/ppermute | solution.py:1335
  443.0 51.6 %copy-start.31 = (f32[128]{0:T(128)}, f32[128]{0:T(128)S(1)}, u32[]{:S(2)}) copy-start(f32[128]{0:T(128)S(1)} %broadcast_multiply_fusion.2) | copy-start | bytes 1540
  494.7 36.2 %copy-start.20 = (f32[512]{0:T(512)S(1)}, f32[512]{0:T(512)}, u32[]{:S(2)}) copy-start(f32[512]{0:T(512)} %reshape.367) | copy-start | bytes 6148
  494.7 36.2 %copy-start.33 = (f32[128]{0:T(128)S(1)}, f32[128]{0:T(128)}, u32[]{:S(2)}) copy-start(f32[128]{0:T(128)} %add_rsqrt_fusion.1) | copy-start | bytes 1540
  494.7 36.4 %copy-start.28 = (f32[2,64]{1,0:T(2,128)S(1)}, f32[2,64]{1,0:T(2,128)}, u32[]{:S(2)}) copy-start(f32[2,64]{1,0:T(2,128)} %copy-done.27) | copy-start | bytes 1540
  494.7 36.4 %copy-start.30 = (f32[32]{0:T(128)S(1)}, f32[32]{0:T(128)}, u32[]{:S(2)}) copy-start(f32[32]{0:T(128)} %copy-done.29) | copy-start | bytes 388
  494.7 38.6 %copy-start.2 = (bf16[2,64,2048]{2,1,0:T(8,128)(2,1)S(1)}, bf16[2,64,2048]{2,1,0:T(8,128)(2,1)}, u32[]{:S(2)}) copy-start(bf16[2,64,2048]{2,1,0:T(8,128)(2,1)} %param.19) | copy-start | bytes 1572868
  533.1 4.4 copy-start.19
  533.3 5.0 copy-start.3
  533.3 5.0 copy-start.10
  710.7 5.9 copy-start.7
  710.7 5.9 copy-start.8
  716.6 8.3 %copy-start.21 = (f32[16,128]{1,0:T(8,128)S(1)}, f32[16,128]{1,0:T(8,128)}, u32[]{:S(2)}) copy-start(f32[16,128]{1,0:T(8,128)} %get-tuple-element.129) | copy-start | bytes 24580
  716.6 10.2 %copy-start.5 = (bf16[2,64,2048]{2,1,0:T(8,128)(2,1)S(1)}, bf16[2,64,2048]{2,1,0:T(8,128)(2,1)}, u32[]{:S(2)}) copy-start(bf16[2,64,2048]{2,1,0:T(8,128)(2,1)} %param.20) | copy-start | bytes 1572868
  716.6 10.2 %copy-start.24 = (f32[128]{0:T(128)S(1)}, f32[128]{0:T(128)}, u32[]{:S(2)}) copy-start(f32[128]{0:T(128)} %copy-done.22) | copy-start | bytes 1540
  716.6 10.2 %copy-start.26 = (f32[128]{0:T(128)S(1)}, f32[128]{0:T(128)}, u32[]{:S(2)}) copy-start(f32[128]{0:T(128)} %copy-done.25) | copy-start | bytes 1540
  716.7 10.2 %copy-start.32 = (f32[128]{0:T(128)S(1)}, f32[128]{0:T(128)}, u32[]{:S(2)}) copy-start(f32[128]{0:T(128)} %copy-done.31) | copy-start | bytes 1540
  726.8 3.4 copy-start.11
  726.8 4.2 copy-start.16
  726.9 4.9 copy-start.15
  726.9 5.6 copy-start.12
Sparse Core Ops, SparseCore 0:
  184.6 81.1 all-gather.1
  430.1 108.4 reduce-scatter.1
